TPU v7x, 128 devices: a whole 4x4x4 slice. The times are simulated.
128 devices in a mesh: slab: 32 (over y, x, core), mp: 4 (over z).
Axes of the slice: x: 4, y: 4, z: 4, core: 2. Of those that a mesh axis runs over, the one named last changes fastest.
Arguments:
- velocity: float32 [3, 256, 512, 256], P(None, 'slab', 'mp'), may hold values from -6 to 6
- anchors: int32 [3, 32, 4, 256], P(None, 'slab', 'mp'), may hold values from 0 to 504, as said below
- dest: int32 [32, 4, 256, 1], P('slab', 'mp'), may hold values from 0 to 31; in each aligned block of 256 rows (0 to 255, 256 to 511, ..., all dimensions but the last counted through in order) at most 16 rows name the same one
- w_lift: bfloat16 [1536, 512], replicated, may hold values from -0.15625 to 0.15625
- w_query: bfloat16 [512, 512], P(None, 'mp'), may hold values from -0.25 to 0.25
- w_key: bfloat16 [512, 512], P(None, 'mp'), may hold values from -0.25 to 0.25
- w_value: bfloat16 [512, 512], P(None, 'mp'), may hold values from -0.25 to 0.25
- w_out: bfloat16 [512, 512], P('mp'), may hold values from -0.25 to 0.25
- w_proj: bfloat16 [512, 1536], replicated, may hold values from -0.25 to 0.25
Outputs:
- new_velocity: float32 [3, 256, 512, 256], P(None, 'slab', 'mp')
- loss: float32 [], replicated
- g_lift: float32 [1536, 512], P('slab')
- g_query: float32 [512, 512], P(None, 'mp')
- g_key: float32 [512, 512], P(None, 'mp')
- g_value: float32 [512, 512], P(None, 'mp')
- g_out: float32 [512, 512], P('mp')
- g_proj: float32 [512, 1536], P('slab')
Inputs may be any that keep to these rules, and one draw needn't show every extreme that they name: Each device's 256 anchors are distinct, multiples of 8 in each coordinate (z, y, x along the first dimension), and name patches inside that device's own block of the grid. `dest`: among the 256 rows of one device no trainer shard is named more than 16 times, and in some device's rows some shard is named exactly 16 times; every shard is named by some row.
All inputs are finite; a program needn't handle non-finite values.
Results may differ from a plain program's by a relative error of at most 0.0035.
Values may be sent and summed in bfloat16 or wider, within the bound.
No kernel may reach another device: no remote copies, remote signals or barrier semaphores. Data moves between devices by JAX's collectives and lax.ppermute only.
A program may use at most 192 MiB of HBM per device.

v0:
```python
import jax
import jax.numpy as jnp
from jax import lax
from jax.experimental import pallas as pl
from jax.experimental.pallas import tpu as pltpu
from jax.sharding import PartitionSpec as P


TIME_STEP = 0.1
VISCOSITY = 0.2
EPSILON = 1e-05
F32 = jnp.float32
BF16 = jnp.bfloat16
CHUNK = 256


def iota(shape, dim):
    return lax.broadcasted_iota(jnp.int32, shape, dim)


def dot(a, b, contract=(1, 0)):
    dims = (((contract[0],), (contract[1],)), ((), ()))
    return lax.dot_general(a, b, dims, preferred_element_type=F32)


def split(a):
    high = a.astype(BF16)
    return high, (a - high.astype(F32)).astype(BF16)


def head_mean(a, mix):
    high, low = split(a)
    halves = [
        dot(high[:, at : at + 256], mix) + dot(low[:, at : at + 256], mix) for at in (0, 256)
    ]
    return jnp.concatenate(halves, axis=1)


def mean_matrix():
    same = iota((256, 256), 0) // 64 == iota((256, 256), 1) // 64
    return jnp.where(same, 1.0 / 64, 0.0).astype(BF16)


def selections(once_ref, pair_ref, turn_ref):
    row, col = iota((256, 256), 0), iota((256, 256), 1)
    turn_ref[...] = jnp.where(col == (row & 31) * 8 + (row >> 5), 1.0, 0.0).astype(BF16)

    def spread(i, carry):
        at = pl.ds(pl.multiple_of(i * 128, 128), 128)
        row, col = iota((128, 1024), 0), iota((128, 1024), 1)
        once_ref[at, :] = jnp.where(col == 8 * row + i, 1.0, 0.0).astype(BF16)
        return carry

    lax.fori_loop(0, 8, spread, 0)
    row, col = iota((512, 512), 0), iota((512, 512), 1)
    pair_ref[...] = jnp.where(col == 8 * (row & 63) + (row >> 6), 1.0, 0.0).astype(BF16)


def cut_patches(load, pick_ref, out_ref, once_ref, pair_ref, turn_ref, whole_ref, rest_ref):
    row, col = iota((128, 256), 0), iota((128, 256), 1)
    turn_pair = jnp.where(col == (row & 31) * 8 + 2 * (row >> 5), 1.0, 0.0).astype(BF16)

    def strips(i, carry):
        cells = [load(2 * i), load(2 * i + 1)]
        first = jnp.concatenate([c[:128] for c in cells], axis=0).astype(BF16)
        last = [c[128:] for c in cells]
        last = [jnp.concatenate([c, pltpu.roll(c, 255, 1)], axis=0) for c in last]
        last = jnp.concatenate(last, axis=0).astype(BF16)
        whole = dot(turn_ref[...], first, (1, 1)).astype(BF16)
        rest = dot(turn_pair, last, (1, 1)).astype(BF16)
        for k in range(2):
            at = pl.ds(pl.multiple_of(i * 64 + k * 32, 32), 32)
            lanes = slice(k * 128, (k + 1) * 128)
            for x in range(8):
                whole_ref[at, x * 128 : (x + 1) * 128] = whole[x * 32 : (x + 1) * 32, lanes]
            for x in range(4):
                rest_ref[at, x * 128 : (x + 1) * 128] = rest[x * 32 : (x + 1) * 32, lanes]
        return carry

    lax.fori_loop(0, 8, strips, 0)

    def place(i, carry):
        at = pl.ds(pl.multiple_of(i * CHUNK, CHUNK), CHUNK)
        pick = pick_ref[at, :]
        picked = dot(pick, whole_ref[...]).astype(BF16)
        out_ref[at, 0:1024] = dot(picked, once_ref[...]).astype(BF16)
        picked = dot(pick, rest_ref[...]).astype(BF16)
        out_ref[at, 1024:1536] = dot(picked, pair_ref[...]).astype(BF16)
        return carry

    lax.fori_loop(0, 512 // CHUNK, place, 0)


CUT_SCRATCH = [
    pltpu.VMEM((1024, 1024), BF16),
    pltpu.VMEM((512, 512), BF16),
    pltpu.VMEM((256, 256), BF16),
    pltpu.VMEM((512, 1024), BF16),
    pltpu.VMEM((512, 512), BF16),
]


def old_kernel(field_hbm, anchor_ref, dest_ref, out_ref, pick_ref, field_ref, sem, *scratch):
    fetch = pltpu.make_async_copy(field_hbm, field_ref, sem)
    fetch.start()
    selections(*scratch[:3])
    target = dest_ref[...].astype(F32)
    wide = jnp.broadcast_to(target, (256, 256))
    row, col = iota((256, 256), 0), iota((256, 256), 1)
    tall = jnp.sum(jnp.where(row == col, wide, 0.0), axis=1, keepdims=True)
    ahead = jnp.where((tall == wide) & (row < col), 1.0, 0.0)
    slot = target * 16.0 + jnp.sum(ahead, axis=0, keepdims=True)
    patch = ((anchor_ref[1] >> 3) & 15) * 32 + ((anchor_ref[2] >> 3) & 31)
    row = iota((512, 256), 0)
    sent = jnp.where(row == slot.astype(jnp.int32), 1.0, 0.0)
    taken = jnp.where(row == patch, 1.0, 0.0).astype(BF16)
    pick_ref[...] = dot(sent.astype(BF16), taken, (1, 1)).astype(BF16)
    tag = jnp.sum(sent, axis=1, keepdims=True)
    out_ref[:, 1536:1664] = jnp.broadcast_to(tag, (512, 128)).astype(BF16)
    fetch.wait()

    def load(by):
        at = pl.ds(pl.multiple_of(by * 8, 8), 8)
        return field_ref[:, :, at, :].reshape(192, 256)

    cut_patches(load, pick_ref, out_ref, *scratch)


def new_kernel(
    field_hbm, z_prev_ref, z_next_ref, y_prev_ref, y_next_ref, pick_ref,
    new_hbm, out_ref, pad_ref, new_ref, sem, *scratch,
):
    fetch = pltpu.make_async_copy(field_hbm, pad_ref.at[:, 1:9, 8:136, :], sem.at[0])
    fetch.start()
    selections(*scratch[:3])
    pad_ref[:, 0:1, 8:136, :] = z_prev_ref[...]
    pad_ref[:, 9:10, 8:136, :] = z_next_ref[...]
    pad_ref[:, 1:9, 7:8, :] = y_prev_ref[...]
    pad_ref[:, 1:9, 136:137, :] = y_next_ref[...]
    fetch.wait()
    near = VISCOSITY * TIME_STEP

    def layer(z, carry):
        for y in range(0, 128, 32):
            along = [pad_ref[c, z + 1, 8 + y : 40 + y, :] for c in range(3)]
            drift = [(0.5 * TIME_STEP) * v for v in along]
            ahead = [near - v for v in drift]
            behind = [near + v for v in drift]
            for c in range(3):
                centre = along[c]
                z_next = pad_ref[c, z + 2, 8 + y : 40 + y, :]
                z_prev = pad_ref[c, z, 8 + y : 40 + y, :]
                y_next = pad_ref[c, z + 1, 9 + y : 41 + y, :]
                y_prev = pad_ref[c, z + 1, 7 + y : 39 + y, :]
                x_next = pltpu.roll(centre, 255, 1)
                x_prev = pltpu.roll(centre, 1, 1)
                new_ref[c, z, y : y + 32, :] = (
                    (1.0 - 6.0 * near) * centre
                    + (ahead[0] * x_next + behind[0] * x_prev)
                    + (ahead[1] * y_next + behind[1] * y_prev)
                    + (ahead[2] * z_next + behind[2] * z_prev)
                )
        return carry

    lax.fori_loop(0, 8, layer, 0)
    store = pltpu.make_async_copy(new_ref, new_hbm, sem.at[1])
    store.start()

    def load(by):
        at = pl.ds(pl.multiple_of(by * 8, 8), 8)
        return new_ref[:, :, at, :].reshape(192, 256)

    cut_patches(load, pick_ref, out_ref, *scratch)
    store.wait()


def pack(blocks):
    row, col = iota((128, 128), 0), iota((128, 128), 1)
    return jnp.where(row // 64 == col // 64, blocks[0], pltpu.roll(blocks[1], 64, 1))


def unpack(packed):
    row, col = iota((128, 128), 0), iota((128, 128), 1)
    own = row // 64 == col // 64
    return jnp.where(own, packed, 0.0), jnp.where(own, pltpu.roll(packed, 64, 1), 0.0)


def absolute(m, j):
    return pl.multiple_of(((m - j) & 3) * 128, 128)


def forward_kernel(
    m_ref, old_ref, lift_w_ref, w0_ref, w1_ref, w2_ref, w3_ref,
    lifted_ref, query_ref, key_ref, key_spread_ref, value_ref, value_spread_ref,
    query_w_ref, key_w_ref, value_w_ref, out_w_ref, sums_ref, acc_ref,
):
    m = m_ref[0]
    for j, block in enumerate((w0_ref, w1_ref, w2_ref, w3_ref)):
        at = pl.ds(absolute(m, j), 128)
        query_w_ref[:, at] = block[0]
        key_w_ref[:, at] = block[1]
        value_w_ref[:, at] = block[2]
        for k in range(4):
            out_w_ref[at, k * 128 : (k + 1) * 128] = block[3, k * 128 : (k + 1) * 128, :]
    acc_ref[...] = jnp.zeros_like(acc_ref)
    mix = mean_matrix()

    def rows(i, carry):
        at = pl.ds(pl.multiple_of(i * CHUNK, CHUNK), CHUNK)
        lifted = dot(old_ref[at, 0:1536], lift_w_ref[...]).astype(BF16)
        lifted_ref[at, :] = lifted
        query_ref[at, :] = dot(lifted, query_w_ref[...]).astype(BF16)
        normed = []
        for w_ref, hat_ref, spread_ref in (
            (key_w_ref, key_ref, key_spread_ref),
            (value_w_ref, value_ref, value_spread_ref),
        ):
            heads = dot(lifted, w_ref[...])
            shifted = heads - head_mean(heads, mix)
            spread = jnp.sqrt(head_mean(shifted * shifted, mix) + EPSILON)
            hat = shifted / spread
            normed.append(hat.astype(BF16))
            hat_ref[at, :] = normed[-1]
            spread_ref[at, :] = spread
        for p in range(4):
            part = slice(p * 128, (p + 1) * 128)
            acc_ref[p] += dot(normed[0][:, part], normed[1][:, part], (0, 0))
        return carry

    lax.fori_loop(0, 512 // CHUNK, rows, 0)
    sums_ref[0:128, :] = pack((acc_ref[0], acc_ref[1]))
    sums_ref[128:256, :] = pack((acc_ref[2], acc_ref[3]))
    count = jnp.sum(old_ref[:, 1536:1664].astype(F32), axis=0, keepdims=True)
    sums_ref[256:264, :] = jnp.broadcast_to(count, (8, 128))


def middle_kernel(
    s0_ref, s1_ref, s2_ref, s3_ref, lifted_ref, query_ref, new_ref,
    out_w_ref, proj_w_ref,
    send_ref, d_query_ref, d_hidden_ref, sums_ref, count_ref,
    hidden_ref, d_guess_ref, attended_ref, d_tokens_ref, acc_ref, high_ref, low_ref, loss_ref,
):
    total = (s0_ref[...] + s1_ref[...]) + (s2_ref[...] + s3_ref[...])
    count = total[256:264, :]
    count_ref[...] = count
    for p in range(2):
        blocks = unpack(total[p * 128 : (p + 1) * 128] / count[0:1, :])
        for q in range(2):
            high_ref[2 * p + q], low_ref[2 * p + q] = split(blocks[q])
    acc_ref[...] = jnp.zeros_like(acc_ref)
    loss_ref[...] = jnp.zeros_like(loss_ref)

    def rows(i, carry):
        at = pl.ds(pl.multiple_of(i * CHUNK, CHUNK), CHUNK)
        query = query_ref[at, :]
        parts = []
        for p in range(4):
            part = query[:, p * 128 : (p + 1) * 128]
            parts.append(dot(part, high_ref[p]) + dot(part, low_ref[p]))
        attended = jnp.concatenate(parts, axis=1).astype(BF16)
        attended_ref[at, :] = attended
        mixed = dot(attended, out_w_ref[...])
        hidden = (lifted_ref[at, :].astype(F32) + mixed).astype(BF16)
        hidden_ref[at, :] = hidden
        error = dot(hidden, proj_w_ref[...]) - new_ref[at, :].astype(F32)
        loss_ref[...] += jnp.sum((error * error).reshape(CHUNK // 8, 8, 1536), axis=0)
        d_guess = (error * (1.0 / 32768)).astype(BF16)
        d_guess_ref[at, :] = d_guess
        d_hidden = dot(d_guess, proj_w_ref[...], (1, 1))
        d_hidden_ref[at, :] = d_hidden
        d_tokens = d_hidden.astype(BF16)
        d_tokens_ref[at, :] = d_tokens
        high, low = split(dot(d_tokens, out_w_ref[...], (1, 1)))
        for p in range(4):
            part = slice(p * 128, (p + 1) * 128)
            back = (
                dot(high[:, part], high_ref[p], (1, 1))
                + dot(high[:, part], low_ref[p], (1, 1))
                + dot(low[:, part], high_ref[p], (1, 1))
            )
            d_query_ref[at, part] = back.astype(BF16)
            acc_ref[p] += dot(query[:, part], high[:, part], (0, 0)) + dot(
                query[:, part], low[:, part], (0, 0)
            )
        return carry

    lax.fori_loop(0, 512 // CHUNK, rows, 0)
    sums_ref[0:128, :] = pack((acc_ref[0], acc_ref[1]))
    sums_ref[128:256, :] = pack((acc_ref[2], acc_ref[3]))
    loss = jnp.sum(loss_ref[...], axis=(0, 1), keepdims=True) * (1.0 / 50331648)
    sums_ref[256:264, :] = jnp.broadcast_to(loss, (8, 128))
    grad = dot(hidden_ref[...], d_guess_ref[...], (0, 0)).astype(BF16)
    for n in range(4):
        for j in range(3):
            at = n * 384 + j * 128
            send_ref[:, n, 16 * j : 16 * j + 16, :] = grad[:, at : at + 128].reshape(32, 16, 128)
    grad = dot(d_tokens_ref[...], attended_ref[...], (0, 0)).astype(BF16)
    for n in range(4):
        send_ref[:, n, 48:64, :] = grad[:, n * 128 : (n + 1) * 128].reshape(32, 16, 128)


def backward_kernel(
    s0_ref, s1_ref, s2_ref, s3_ref, count_ref, old_hbm, lifted_ref, key_ref, key_spread_ref,
    value_ref, value_spread_ref, d_query_ref, d_hidden_ref, query_w_ref, key_w_ref, value_w_ref,
    send_ref, loss_ref, high_ref, low_ref, d_heads_ref, d_lifted_ref, old_ref, sem,
):
    fetch = pltpu.make_async_copy(old_hbm.at[:, 0:1536], old_ref, sem)
    fetch.start()
    total = (s0_ref[...] + s1_ref[...]) + (s2_ref[...] + s3_ref[...])
    loss_ref[...] = total[256:264, :]
    for p in range(2):
        blocks = unpack(total[p * 128 : (p + 1) * 128] / count_ref[0:1, :])
        for q in range(2):
            high_ref[2 * p + q], low_ref[2 * p + q] = split(blocks[q])
    mix = mean_matrix()

    def rows(i, carry):
        at = pl.ds(pl.multiple_of(i * CHUNK, CHUNK), CHUNK)
        d_query = d_query_ref[at, :]
        d_heads_ref[at, 0:512] = d_query
        d_lifted = d_hidden_ref[at, :] + dot(d_query, query_w_ref[...], (1, 1))
        for hat_ref, spread_ref, other_ref, across, lanes, w_ref in (
            (key_ref, key_spread_ref, value_ref, (1, 1), 512, key_w_ref),
            (value_ref, value_spread_ref, key_ref, (1, 0), 1024, value_w_ref),
        ):
            other = other_ref[at, :]
            parts = []
            for p in range(4):
                part = other[:, p * 128 : (p + 1) * 128]
                parts.append(dot(part, high_ref[p], across) + dot(part, low_ref[p], across))
            grad = jnp.concatenate(parts, axis=1)
            hat = hat_ref[at, :].astype(F32)
            inner = head_mean(grad, mix)
            cross = head_mean(grad * hat, mix)
            grad = ((grad - inner - hat * cross) / spread_ref[at, :]).astype(BF16)
            d_heads_ref[at, lanes : lanes + 512] = grad
            d_lifted = d_lifted + dot(grad, w_ref[...], (1, 1))
        d_lifted_ref[at, :] = d_lifted.astype(BF16)
        return carry

    lax.fori_loop(0, 512 // CHUNK, rows, 0)
    grad = dot(lifted_ref[...], d_heads_ref[...], (0, 0)).astype(BF16)
    for n in range(4):
        for j in range(3):
            at = 512 * j + 128 * n
            send_ref[:, n, 48 + 16 * j : 64 + 16 * j, :] = grad[:, at : at + 128].reshape(32, 16, 128)
    fetch.wait()
    grad = dot(old_ref[...], d_lifted_ref[...], (0, 0)).astype(BF16)
    for n in range(4):
        send_ref[:, n, 0:48, :] = grad[:, n * 128 : (n + 1) * 128].reshape(32, 48, 128)


def last_kernel(
    m_ref, r0_ref, r1_ref, r2_ref, r3_ref, heads_ref,
    lift_ref, query_ref, key_ref, value_ref, out_ref, proj_ref, loss_ref,
):
    m = m_ref[0]
    for j, block in enumerate((r0_ref, r1_ref, r2_ref, r3_ref)):
        lift_ref[:, pl.ds(absolute(m, j), 128)] = block[0:48, :]
        for k in range(3):
            at = pl.multiple_of(((m - j) & 3) * 384 + k * 128, 128)
            proj_ref[:, pl.ds(at, 128)] = block[48 + 16 * k : 64 + 16 * k, :]
    query_ref[...] = heads_ref[:, 0:16, :].astype(F32).reshape(512, 128)
    key_ref[...] = heads_ref[:, 16:32, :].astype(F32).reshape(512, 128)
    value_ref[...] = heads_ref[:, 32:48, :].astype(F32).reshape(512, 128)
    out_ref[...] = heads_ref[:, 48:64, :].astype(F32).reshape(512, 128).T
    loss = jnp.sum(heads_ref[:, 64:80, :].astype(F32), axis=0)
    loss_ref[...] = jnp.broadcast_to(loss[0:1] + loss[1:2], (8, 128))


def call(body, outs, scratch=(), ins="", results=None):
    spaces = {"s": pltpu.SMEM, "h": pl.ANY, "v": pltpu.VMEM}
    return pl.pallas_call(
        body,
        out_shape=[jax.ShapeDtypeStruct(shape, kind) for shape, kind in outs],
        in_specs=[pl.BlockSpec(memory_space=spaces[k]) for k in ins],
        out_specs=[pl.BlockSpec(memory_space=spaces[k]) for k in results or "v" * len(outs)],
        scratch_shapes=list(scratch),
        compiler_params=pltpu.CompilerParams(vmem_limit_bytes=60 << 20),
    )


def around(value):
    got = [value]
    for d in (1, 2, 3):
        got.append(lax.ppermute(value, "mp", [(i, (i + d) % 4) for i in range(4)]))
    return got


def exchange(value, axes):
    return lax.all_to_all(value, axes, split_axis=0, concat_axis=0, tiled=True)


def step(velocity, anchors, dest, w_lift, w_query, w_key, w_value, w_out, w_proj):
    slabs = lax.axis_size("slab")
    m = lax.axis_index("mp").reshape(1)
    up = [(i, (i + 1) % slabs) for i in range(slabs)]
    z_prev = lax.ppermute(velocity[:, 7:8], "slab", up)
    z_next = lax.ppermute(velocity[:, 0:1], "slab", [(j, i) for i, j in up])
    up = [(i, (i + 1) % 4) for i in range(4)]
    y_prev = lax.ppermute(velocity[:, :, 127:128], "mp", up)
    y_next = lax.ppermute(velocity[:, :, 0:1], "mp", [(j, i) for i, j in up])
    tall = jnp.concatenate([w_out[:, k * 128 : (k + 1) * 128] for k in range(4)], axis=0)
    heads_w = around(jnp.stack([w_query, w_key, w_value, tall]))

    send_old, pick = call(
        old_kernel,
        [((512, 1664), BF16), ((512, 512), BF16)],
        [pltpu.VMEM((3, 8, 128, 256), F32), pltpu.SemaphoreType.DMA] + CUT_SCRATCH,
        "hvv",
    )(velocity, anchors.reshape(3, 1, 256), dest.reshape(1, 256))
    old = exchange(send_old, "slab")
    new_velocity, send_new = call(
        new_kernel,
        [((3, 8, 128, 256), F32), ((512, 1536), BF16)],
        [
            pltpu.VMEM((3, 10, 144, 256), F32),
            pltpu.VMEM((3, 8, 128, 256), F32),
            pltpu.SemaphoreType.DMA((2,)),
        ]
        + CUT_SCRATCH,
        "hvvvvv",
        "hv",
    )(velocity, z_prev, z_next, y_prev, y_next, pick)
    new = exchange(send_new, "slab")

    wide, wide_f = ((512, 512), BF16), ((512, 512), F32)
    lifted, query, key, key_spread, value, value_spread, wq, wk, wv, wo, sums = call(
        forward_kernel,
        [wide, wide, wide, wide_f, wide, wide_f, wide, wide, wide, wide, ((264, 128), F32)],
        [pltpu.VMEM((4, 128, 128), F32)],
        "svvvvvv",
    )(m, old, w_lift, *heads_w)
    sums = around(sums)
    send_out, d_query, d_hidden, d_sums, count = call(
        middle_kernel,
        [((32, 4, 64, 128), BF16), wide, wide_f, ((264, 128), F32), ((8, 128), F32)],
        [
            pltpu.VMEM((512, 512), BF16),
            pltpu.VMEM((512, 1536), BF16),
            pltpu.VMEM((512, 512), BF16),
            pltpu.VMEM((512, 512), BF16),
            pltpu.VMEM((4, 128, 128), F32),
            pltpu.VMEM((4, 128, 128), BF16),
            pltpu.VMEM((4, 128, 128), BF16),
            pltpu.VMEM((8, 1536), F32),
        ],
        "vvvvvvvvv",
    )(*sums, lifted, query, new, wo, w_proj)
    d_sums = around(d_sums)
    everyone = ("slab", "mp")
    got_out = exchange(send_out.reshape(128, 64, 128), everyone)
    send_in, loss_part = call(
        backward_kernel,
        [((32, 4, 96, 128), BF16), ((8, 128), F32)],
        [
            pltpu.VMEM((4, 128, 128), BF16),
            pltpu.VMEM((4, 128, 128), BF16),
            pltpu.VMEM((512, 1536), BF16),
            pltpu.VMEM((512, 512), BF16),
            pltpu.VMEM((512, 1536), BF16),
            pltpu.SemaphoreType.DMA,
        ],
        "vvvvvhvvvvvvvvvv",
    )(*d_sums, count, old, lifted, key, key_spread, value, value_spread, d_query, d_hidden, wq, wk, wv)
    got_in = exchange(send_in.reshape(128, 96, 128), everyone)

    total_out = jnp.sum(got_out.astype(F32), axis=0)
    total_in = jnp.sum(got_in.astype(F32), axis=0)
    blocks = jnp.concatenate([total_in[0:48], total_out[0:48]], axis=0)
    loss_high = loss_part.astype(BF16)
    loss_low = (loss_part - loss_high.astype(F32)).astype(BF16)
    heads = jnp.concatenate([total_in[48:96], total_out[48:64]], axis=0).astype(BF16)
    heads = jnp.concatenate([heads, loss_high[0:1], loss_low[0:1], jnp.zeros((14, 128), BF16)], axis=0)
    heads = exchange(jnp.broadcast_to(heads[None], (32, 80, 128)), "slab")
    lift, g_query, g_key, g_value, g_out, proj, loss = call(
        last_kernel,
        [
            ((48, 512), F32),
            ((512, 128), F32),
            ((512, 128), F32),
            ((512, 128), F32),
            ((128, 512), F32),
            ((16, 1536), F32),
            ((8, 128), F32),
        ],
        (),
        "svvvvv",
    )(m, *around(blocks), heads)
    return (new_velocity, loss[0, 0], lift, g_query, g_key, g_value, g_out, proj)


def solution(mesh):
    return jax.shard_map(
        step,
        mesh=mesh,
        in_specs=(
            P(None, "slab", "mp", None),
            P(None, "slab", "mp", None),
            P("slab", "mp", None, None),
            P(),
            P(None, "mp"),
            P(None, "mp"),
            P(None, "mp"),
            P("mp", None),
            P(),
        ),
        out_specs=(
            P(None, "slab", "mp", None),
            P(),
            P("slab", None),
            P(None, "mp"),
            P(None, "mp"),
            P(None, "mp"),
            P("mp", None),
            P("slab", None),
        ),
        check_vma=False,
    )
```

profile of v0, /device:TPU:6, one launch (start us, length us, event | category | flops | bytes accessed | tf_op | source)
XLA Modules:
  0.0 245.4 jit_solution(12591634541963109399)
XLA Ops:
  0.6 8.7 %shard_map.152 = (bf16[512,1664]{1,0:T(8,128)(2,1)}, bf16[512,512]{1,0:T(8,128)(2,1)}) custom-call(f32[3,8,128,256]{3,2,1,0:T(8,128)} %field_hbm.3, s32[3,1,256]{2,1,0:T(1,128)} %bitcast.25, s32[1,256]{1,0:T(1,128)} %bitcast.26), custom_call_target="tpu_custom_call" | custom-call | tf_op jit(solution)/shard_map/pallas_call | solution.py:406
  9.4 7.6 %all-to-all-start = ((bf16[32,16,1664]{2,1,0:T(8,128)(2,1)}), bf16[32,16,1664]{2,1,0:T(8,128)(2,1)S(1)}, u32[]{:S(2)}, u32[]{:S(2)}) async-start(bf16[32,16,1664]{2,1,0:T(8,128)(2,1)} %bitcast.20), calls=%async_computation | async-start | bytes 3407872 | tf_op jit(solution)/shard_map/all_to_all | solution.py:391
  17.0 1.2 fusion.1
  18.2 0.2 collective-permute-start
  18.4 1.6 collective-permute-start.1
  20.0 1.1 fusion
  21.1 2.0 collective-permute-start.2
  23.0 2.2 collective-permute-start.3
  25.2 1.7 collective-permute-done.2.y_prev_ref
  27.0 0.0 collective-permute-done.3.y_next_ref
  27.0 15.6 %collective-permute-done.z_prev_ref = f32[3,1,128,256]{3,2,1,0:T(8,128)S(1)} collective-permute-done((f32[3,1,128,256]{3,2,1,0:T(8,128)S(1)}, f32[3,1,128,256]{3,2,1,0:T(8,128)S(1)}, u32[]{:S(2)}, u32[]{:S(2)}) %collective-permute-start) | collective-permute-done | bytes 393248 | tf_op jit(solution)/shard_map/ppermute | solution.py:398
  42.6 0.0 collective-permute-done.1.z_next_ref
  42.6 0.7 copy-done.3
  43.3 0.1 copy-done.4
  43.5 12.1 %shard_map.153 = (f32[3,8,128,256]{3,2,1,0:T(8,128)}, bf16[512,1536]{1,0:T(8,128)(2,1)}) custom-call(f32[3,8,128,256]{3,2,1,0:T(8,128)} %field_hbm.3, f32[3,1,128,256]{3,2,1,0:T(8,128)} %copy-done.3, f32[3,1,128,256]{3,2,1,0:T(8,128)} %copy-done.4, f32[3,8,1,256]{3,2,1,0:T(1,128)} %copy-done.18, f32[3,8,1,256]{3,2,1,0:T(1,128)} %copy-done.19, ...), custom_call_target="tpu_custom_call" | custom-call | tf_op jit(solution)/shard_map/pallas_call | solution.py:413
  55.6 0.0 all-to-all-done
  55.6 7.1 %all-to-all-start.1 = ((bf16[32,16,1536]{2,1,0:T(8,128)(2,1)}), bf16[32,16,1536]{2,1,0:T(8,128)(2,1)S(1)}, u32[]{:S(2)}, u32[]{:S(2)}) async-start(bf16[32,16,1536]{2,1,0:T(8,128)(2,1)} %bitcast.21), calls=%async_computation.1 | async-start | bytes 3145728 | tf_op jit(solution)/shard_map/all_to_all | solution.py:391
  62.8 1.8 pad_maximum_fusion.w0_ref
  64.7 1.9 collective-permute-start.4
  66.6 3.6 %collective-permute-start.5 = (bf16[4,512,128]{2,1,0:T(8,128)(2,1)}, bf16[4,512,128]{2,1,0:T(8,128)(2,1)}, u32[]{:S(2)}, u32[]{:S(2)}) collective-permute-start(bf16[4,512,128]{2,1,0:T(8,128)(2,1)} %pad_maximum_fusion.w0_ref), channel_id=1, source_target_pairs={{0,2},{1,3},{2,0},{3,1},{4,6},{5,7},{6,4},{7,5},{8,10},{9,11},{10,... | collective-permute-start | bytes 1572872 | tf_op jit(solution)/shard_map/ppermute | solution.py:386
  70.2 1.0 collective-permute-start.6
  71.2 10.0 %collective-permute-done.4.w1_ref = bf16[4,512,128]{2,1,0:T(8,128)(2,1)} collective-permute-done((bf16[4,512,128]{2,1,0:T(8,128)(2,1)}, bf16[4,512,128]{2,1,0:T(8,128)(2,1)}, u32[]{:S(2)}, u32[]{:S(2)}) %collective-permute-start.4) | collective-permute-done | bytes 524320 | tf_op jit(solution)/shard_map/ppermute | solution.py:386
  81.2 12.4 %collective-permute-done.5.w2_ref = bf16[4,512,128]{2,1,0:T(8,128)(2,1)} collective-permute-done((bf16[4,512,128]{2,1,0:T(8,128)(2,1)}, bf16[4,512,128]{2,1,0:T(8,128)(2,1)}, u32[]{:S(2)}, u32[]{:S(2)}) %collective-permute-start.5) | collective-permute-done | bytes 524320 | tf_op jit(solution)/shard_map/ppermute | solution.py:386
  93.6 9.4 %shard_map.154 = (bf16[512,512]{1,0:T(8,128)(2,1)}, bf16[512,512]{1,0:T(8,128)(2,1)}, bf16[512,512]{1,0:T(8,128)(2,1)}, f32[512,512]{1,0:T(8,128)}, bf16[512,512...) custom-call(s32[1]{0:T(128)} %bitcast.2.m_ref, ...), custom_call_target="tpu_custom_call" | custom-call | tf_op jit(solution)/shard_map/pallas_call | solution.py:428
  103.1 1.1 collective-permute-start.7
  104.2 2.4 collective-permute-start.8
  106.6 1.3 collective-permute-start.9
  107.9 1.7 collective-permute-done.7.s1_ref
  109.7 3.5 %collective-permute-done.8.s2_ref = f32[264,128]{1,0:T(8,128)S(1)} collective-permute-done((f32[264,128]{1,0:T(8,128)}, f32[264,128]{1,0:T(8,128)S(1)}, u32[]{:S(2)}, u32[]{:S(2)}) %collective-permute-start.8) | collective-permute-done | bytes 135200 | tf_op jit(solution)/shard_map/ppermute | solution.py:386
  113.2 0.0 collective-permute-done.9.s3_ref
  113.2 0.0 all-to-all-done.1
  113.2 0.6 copy-done.7
  113.8 0.0 copy-done.8
  113.9 0.6 copy-done.1
  114.5 9.6 %shard_map.155 = (bf16[32,4,64,128]{3,2,1,0:T(8,128)(2,1)}, bf16[512,512]{1,0:T(8,128)(2,1)}, f32[512,512]{1,0:T(8,128)}, f32[264,128]{1,0:T(8,128)}, f32[8,128]{1,0:T(8,128)}) custom-call(f32[264,128]{1,0:T(8,128)} %get-tuple-element.40.s0_ref, f32[264,128]{1,0:T(8,128)} %copy-done.6, f32[264,128]{1,0:T(8,128)} %copy-done.7, f32[264,128]{1,0:T(8,128)} %copy-done.8, ...), custom_call_target="tpu_custom_call" | custom-call | tf_op jit(solution)/shard_map/pallas_call | solution.py:435
  124.0 8.9 %all-to-all-start.3 = ((bf16[128,64,128]{2,1,0:T(8,128)(2,1)}), bf16[128,64,128]{2,1,0:T(8,128)(2,1)}, u32[]{:S(2)}, u32[]{:S(2)}) async-start(bf16[128,64,128]{2,1,0:T(8,128)(2,1)} %bitcast.19), calls=%async_computation.3 | async-start | bytes 4194304 | tf_op jit(solution)/shard_map/all_to_all | solution.py:391
  132.9 1.7 collective-permute-start.10
  134.6 3.2 %collective-permute-start.11 = (f32[264,128]{1,0:T(8,128)S(1)}, f32[264,128]{1,0:T(8,128)S(1)}, u32[]{:S(2)}, u32[]{:S(2)}) collective-permute-start(f32[264,128]{1,0:T(8,128)S(1)} %copy-done.9), channel_id=1, source_target_pairs={{0,2},{1,3},{2,0},{3,1},{4,6},{5,7},{6,4},{7,5},{8,10},{9,11},{10,... | collective-permute-start | bytes 405512 | tf_op jit(solution)/shard_map/ppermute | solution.py:386
  137.8 1.2 collective-permute-start.12
  139.0 22.6 %collective-permute-done.10.s1_ref = f32[264,128]{1,0:T(8,128)S(1)} collective-permute-done((f32[264,128]{1,0:T(8,128)S(1)}, f32[264,128]{1,0:T(8,128)S(1)}, u32[]{:S(2)}, u32[]{:S(2)}) %collective-permute-start.10) | collective-permute-done | bytes 135200 | tf_op jit(solution)/shard_map/ppermute | solution.py:386
  161.6 3.1 %collective-permute-done.11.s2_ref = f32[264,128]{1,0:T(8,128)S(1)} collective-permute-done((f32[264,128]{1,0:T(8,128)S(1)}, f32[264,128]{1,0:T(8,128)S(1)}, u32[]{:S(2)}, u32[]{:S(2)}) %collective-permute-start.11) | collective-permute-done | bytes 135200 | tf_op jit(solution)/shard_map/ppermute | solution.py:386
  164.8 0.0 collective-permute-done.12.s3_ref
  164.8 0.6 copy-done.11
  165.4 0.0 copy-done.12
  165.5 10.4 %shard_map.156 = (bf16[32,4,96,128]{3,2,1,0:T(8,128)(2,1)}, f32[8,128]{1,0:T(8,128)}) custom-call(f32[264,128]{1,0:T(8,128)} %get-tuple-element.45.s0_ref, f32[264,128]{1,0:T(8,128)} %copy-done.10, f32[264,128]{1,0:T(8,128)} %copy-done.11, f32[264,128]{1,0:T(8,128)} %copy-done.12, f32[8,128]{1,0:T(8,128)} %get-tuple-element.46.count_ref, ...), custom_call_target="tpu_custom_call" | custom-call | tf_op jit(solution)/shard_map/pallas_call | solution.py:453
  175.8 0.0 all-to-all-done.3
  175.8 0.0 copy-start.20
  175.9 7.5 %all-to-all-start.2 = ((bf16[128,96,128]{2,1,0:T(8,128)(2,1)}), bf16[128,96,128]{2,1,0:T(8,128)(2,1)S(1)}, u32[]{:S(2)}, u32[]{:S(2)}) async-start(bf16[128,96,128]{2,1,0:T(8,128)(2,1)} %bitcast.18), calls=%async_computation.2 | async-start | bytes 6291456 | tf_op jit(solution)/shard_map/all_to_all | solution.py:391
  183.4 2.0 convert_reduce_fusion.1
  185.3 38.2 %all-to-all-done.2 = bf16[128,96,128]{2,1,0:T(8,128)(2,1)S(1)} async-done(((bf16[128,96,128]{2,1,0:T(8,128)(2,1)}), bf16[128,96,128]{2,1,0:T(8,128)(2,1)S(1)}, u32[]{:S(2)}, u32[]{:S(2)}) %all-to-all-start.2) | async-done | bytes 3145760 | tf_op jit(solution)/shard_map/all_to_all | solution.py:391
  223.5 0.5 convert_reduce_fusion
  224.0 0.2 concatenate.14
  224.2 0.9 broadcast_in_dim.10
  225.1 5.3 %all-to-all-start.4 = ((bf16[32,80,128]{2,1,0:T(8,128)(2,1)}), bf16[32,80,128]{2,1,0:T(8,128)(2,1)S(1)}, u32[]{:S(2)}, u32[]{:S(2)}) async-start(bf16[32,80,128]{2,1,0:T(8,128)(2,1)} %broadcast_in_dim.10), calls=%async_computation.4 | async-start | bytes 1310720 | tf_op jit(solution)/shard_map/all_to_all | solution.py:391
  230.5 0.9 collective-permute-start.13
  231.3 2.0 collective-permute-start.14
  233.3 1.0 collective-permute-start.15
  234.3 2.0 collective-permute-done.13.r1_ref
  236.3 0.6 collective-permute-done.14.r2_ref
  236.9 0.5 collective-permute-done.15.r3_ref
  237.4 3.7 %all-to-all-done.4.heads_ref = bf16[32,80,128]{2,1,0:T(8,128)(2,1)S(1)} async-done(((bf16[32,80,128]{2,1,0:T(8,128)(2,1)}), bf16[32,80,128]{2,1,0:T(8,128)(2,1)S(1)}, u32[]{:S(2)}, u32[]{:S(2)}) %all-to-all-start.4) | async-done | bytes 655392 | tf_op jit(solution)/shard_map/all_to_all | solution.py:391
  241.1 0.8 copy-done.2
  242.0 2.3 shard_map.157
  244.2 1.2 slice.61
  (45 shorter events, 0.1 us)
Async XLA Ops:
  9.4 46.2 %all-to-all-start = ((bf16[32,16,1664]{2,1,0:T(8,128)(2,1)}), bf16[32,16,1664]{2,1,0:T(8,128)(2,1)S(1)}, u32[]{:S(2)}, u32[]{:S(2)}) async-start(bf16[32,16,1664]{2,1,0:T(8,128)(2,1)} %bitcast.20), calls=%async_computation | async-start | bytes 3407872 | tf_op jit(solution)/shard_map/all_to_all | solution.py:391
  18.2 24.4 %collective-permute-start = (f32[3,1,128,256]{3,2,1,0:T(8,128)S(1)}, f32[3,1,128,256]{3,2,1,0:T(8,128)S(1)}, u32[]{:S(2)}, u32[]{:S(2)}) collective-permute-start(f32[3,1,128,256]{3,2,1,0:T(8,128)S(1)} %get-tuple-element.71), channel_id=1, source_target_pairs={{0,4},{4,8},{8,12},{12,16},{16,20},{20,24},{24,28},{28,32},{32,36}... | collective-permute-start | bytes 1179656 | tf_op jit(solution)/shard_map/ppermute | solution.py:398
  18.4 24.2 %collective-permute-start.1 = (f32[3,1,128,256]{3,2,1,0:T(8,128)S(1)}, f32[3,1,128,256]{3,2,1,0:T(8,128)S(1)}, u32[]{:S(2)}, u32[]{:S(2)}) collective-permute-start(f32[3,1,128,256]{3,2,1,0:T(8,128)S(1)} %get-tuple-element.70), channel_id=1, source_target_pairs={{4,0},{8,4},{12,8},{16,12},{20,16},{24,20},{28,24},{32,28},{36,32}... | collective-permute-start | bytes 1179656 | tf_op jit(solution)/shard_map/ppermute | solution.py:399
  21.1 5.9 %collective-permute-start.2 = (f32[3,8,1,256]{3,2,1,0:T(1,128)S(1)}, f32[3,8,1,256]{3,2,1,0:T(1,128)S(1)}, u32[]{:S(2)}, u32[]{:S(2)}) collective-permute-start(f32[3,8,1,256]{3,2,1,0:T(1,128)S(1)} %get-tuple-element.69), channel_id=1, source_target_pairs={{0,1},{1,2},{2,3},{3,0},{4,5},{5,6},{6,7},{7,4},{8,9},{9,10},{10,1... | collective-permute-start | bytes 73736 | tf_op jit(solution)/shard_map/ppermute | solution.py:401
  23.0 3.9 %collective-permute-start.3 = (f32[3,8,1,256]{3,2,1,0:T(1,128)S(1)}, f32[3,8,1,256]{3,2,1,0:T(1,128)S(1)}, u32[]{:S(2)}, u32[]{:S(2)}) collective-permute-start(f32[3,8,1,256]{3,2,1,0:T(1,128)S(1)} %get-tuple-element.68), channel_id=1, source_target_pairs={{1,0},{2,1},{3,2},{0,3},{5,4},{6,5},{7,6},{4,7},{9,8},{10,9},{11,1... | collective-permute-start | bytes 73736 | tf_op jit(solution)/shard_map/ppermute | solution.py:402
  27.0 15.6 %copy-start.18 = (f32[3,8,1,256]{3,2,1,0:T(1,128)}, f32[3,8,1,256]{3,2,1,0:T(1,128)S(1)}, u32[]{:S(2)}) copy-start(f32[3,8,1,256]{3,2,1,0:T(1,128)S(1)} %collective-permute-done.2.y_prev_ref) | copy-start | bytes 73732
  27.0 15.6 %copy-start.19 = (f32[3,8,1,256]{3,2,1,0:T(1,128)}, f32[3,8,1,256]{3,2,1,0:T(1,128)S(1)}, u32[]{:S(2)}) copy-start(f32[3,8,1,256]{3,2,1,0:T(1,128)S(1)} %collective-permute-done.3.y_next_ref) | copy-start | bytes 73732
  42.6 0.7 copy-start.3
  42.6 0.9 copy-start.4
  43.5 19.3 %copy-start.13 = (bf16[128,512]{1,0:T(8,128)(2,1)S(1)}, bf16[128,512]{1,0:T(8,128)(2,1)}, u32[]{:S(2)}) copy-start(bf16[128,512]{1,0:T(8,128)(2,1)} %param.16) | copy-start | bytes 393220
  43.5 19.4 %copy-start.14 = (bf16[512,128]{1,0:T(8,128)(2,1)S(1)}, bf16[512,128]{1,0:T(8,128)(2,1)}, u32[]{:S(2)}) copy-start(bf16[512,128]{1,0:T(8,128)(2,1)} %param.15) | copy-start | bytes 393220
  55.6 38.0 %copy-start = (bf16[32,16,1664]{2,1,0:T(8,128)(2,1)}, bf16[32,16,1664]{2,1,0:T(8,128)(2,1)S(1)}, u32[]{:S(2)}) copy-start(bf16[32,16,1664]{2,1,0:T(8,128)(2,1)S(1)} %all-to-all-done) | copy-start | bytes 5111812
  55.6 57.6 %all-to-all-start.1 = ((bf16[32,16,1536]{2,1,0:T(8,128)(2,1)}), bf16[32,16,1536]{2,1,0:T(8,128)(2,1)S(1)}, u32[]{:S(2)}, u32[]{:S(2)}) async-start(bf16[32,16,1536]{2,1,0:T(8,128)(2,1)} %bitcast.21), calls=%async_computation.1 | async-start | bytes 3145728 | tf_op jit(solution)/shard_map/all_to_all | solution.py:391
  64.7 16.6 %collective-permute-start.4 = (bf16[4,512,128]{2,1,0:T(8,128)(2,1)}, bf16[4,512,128]{2,1,0:T(8,128)(2,1)}, u32[]{:S(2)}, u32[]{:S(2)}) collective-permute-start(bf16[4,512,128]{2,1,0:T(8,128)(2,1)} %pad_maximum_fusion.w0_ref), channel_id=1, source_target_pairs={{0,1},{1,2},{2,3},{3,0},{4,5},{5,6},{6,7},{7,4},{8,9},{9,10},{10,1... | collective-permute-start | bytes 1572872 | tf_op jit(solution)/shard_map/ppermute | solution.py:386
  66.6 27.1 %collective-permute-start.5 = (bf16[4,512,128]{2,1,0:T(8,128)(2,1)}, bf16[4,512,128]{2,1,0:T(8,128)(2,1)}, u32[]{:S(2)}, u32[]{:S(2)}) collective-permute-start(bf16[4,512,128]{2,1,0:T(8,128)(2,1)} %pad_maximum_fusion.w0_ref), channel_id=1, source_target_pairs={{0,2},{1,3},{2,0},{3,1},{4,6},{5,7},{6,4},{7,5},{8,10},{9,11},{10,... | collective-permute-start | bytes 1572872 | tf_op jit(solution)/shard_map/ppermute | solution.py:386
  70.2 23.5 %collective-permute-start.6 = (bf16[4,512,128]{2,1,0:T(8,128)(2,1)}, bf16[4,512,128]{2,1,0:T(8,128)(2,1)}, u32[]{:S(2)}, u32[]{:S(2)}) collective-permute-start(bf16[4,512,128]{2,1,0:T(8,128)(2,1)} %pad_maximum_fusion.w0_ref), channel_id=1, source_target_pairs={{0,3},{1,0},{2,1},{3,2},{4,7},{5,4},{6,5},{7,6},{8,11},{9,8},{10,9... | collective-permute-start | bytes 1572872 | tf_op jit(solution)/shard_map/ppermute | solution.py:386
  103.1 6.6 %collective-permute-start.7 = (f32[264,128]{1,0:T(8,128)}, f32[264,128]{1,0:T(8,128)S(1)}, u32[]{:S(2)}, u32[]{:S(2)}) collective-permute-start(f32[264,128]{1,0:T(8,128)} %get-tuple-element.40.s0_ref), channel_id=1, source_target_pairs={{0,1},{1,2},{2,3},{3,0},{4,5},{5,6},{6,7},{7,4},{8,9},{9,10},{10,1... | collective-permute-start | bytes 405512 | tf_op jit(solution)/shard_map/ppermute | solution.py:386
  104.2 9.0 %collective-permute-start.8 = (f32[264,128]{1,0:T(8,128)}, f32[264,128]{1,0:T(8,128)S(1)}, u32[]{:S(2)}, u32[]{:S(2)}) collective-permute-start(f32[264,128]{1,0:T(8,128)} %get-tuple-element.40.s0_ref), channel_id=1, source_target_pairs={{0,2},{1,3},{2,0},{3,1},{4,6},{5,7},{6,4},{7,5},{8,10},{9,11},{10,... | collective-permute-start | bytes 405512 | tf_op jit(solution)/shard_map/ppermute | solution.py:386
  106.6 6.6 %collective-permute-start.9 = (f32[264,128]{1,0:T(8,128)}, f32[264,128]{1,0:T(8,128)S(1)}, u32[]{:S(2)}, u32[]{:S(2)}) collective-permute-start(f32[264,128]{1,0:T(8,128)} %get-tuple-element.40.s0_ref), channel_id=1, source_target_pairs={{0,3},{1,0},{2,1},{3,2},{4,7},{5,4},{6,5},{7,6},{8,11},{9,8},{10,9... | collective-permute-start | bytes 405512 | tf_op jit(solution)/shard_map/ppermute | solution.py:386
  109.7 3.5 %copy-start.6 = (f32[264,128]{1,0:T(8,128)}, f32[264,128]{1,0:T(8,128)S(1)}, u32[]{:S(2)}) copy-start(f32[264,128]{1,0:T(8,128)S(1)} %collective-permute-done.7.s1_ref) | copy-start | bytes 405508
  113.2 0.7 copy-start.7
  113.2 0.7 copy-start.8
  113.2 1.3 copy-start.1
  124.0 8.9 %copy-start.9 = (f32[264,128]{1,0:T(8,128)S(1)}, f32[264,128]{1,0:T(8,128)}, u32[]{:S(2)}) copy-start(f32[264,128]{1,0:T(8,128)} %get-tuple-element.45.s0_ref) | copy-start | bytes 405508
  124.0 51.8 %all-to-all-start.3 = ((bf16[128,64,128]{2,1,0:T(8,128)(2,1)}), bf16[128,64,128]{2,1,0:T(8,128)(2,1)}, u32[]{:S(2)}, u32[]{:S(2)}) async-start(bf16[128,64,128]{2,1,0:T(8,128)(2,1)} %bitcast.19), calls=%async_computation.3 | async-start | bytes 4194304 | tf_op jit(solution)/shard_map/all_to_all | solution.py:391
  132.9 28.7 %collective-permute-start.10 = (f32[264,128]{1,0:T(8,128)S(1)}, f32[264,128]{1,0:T(8,128)S(1)}, u32[]{:S(2)}, u32[]{:S(2)}) collective-permute-start(f32[264,128]{1,0:T(8,128)S(1)} %copy-done.9), channel_id=1, source_target_pairs={{0,1},{1,2},{2,3},{3,0},{4,5},{5,6},{6,7},{7,4},{8,9},{9,10},{10,1... | collective-permute-start | bytes 405512 | tf_op jit(solution)/shard_map/ppermute | solution.py:386
  134.6 30.1 %collective-permute-start.11 = (f32[264,128]{1,0:T(8,128)S(1)}, f32[264,128]{1,0:T(8,128)S(1)}, u32[]{:S(2)}, u32[]{:S(2)}) collective-permute-start(f32[264,128]{1,0:T(8,128)S(1)} %copy-done.9), channel_id=1, source_target_pairs={{0,2},{1,3},{2,0},{3,1},{4,6},{5,7},{6,4},{7,5},{8,10},{9,11},{10,... | collective-permute-start | bytes 405512 | tf_op jit(solution)/shard_map/ppermute | solution.py:386
  137.8 26.9 %collective-permute-start.12 = (f32[264,128]{1,0:T(8,128)S(1)}, f32[264,128]{1,0:T(8,128)S(1)}, u32[]{:S(2)}, u32[]{:S(2)}) collective-permute-start(f32[264,128]{1,0:T(8,128)S(1)} %copy-done.9), channel_id=1, source_target_pairs={{0,3},{1,0},{2,1},{3,2},{4,7},{5,4},{6,5},{7,6},{8,11},{9,8},{10,9... | collective-permute-start | bytes 405512 | tf_op jit(solution)/shard_map/ppermute | solution.py:386
  161.6 3.1 %copy-start.10 = (f32[264,128]{1,0:T(8,128)}, f32[264,128]{1,0:T(8,128)S(1)}, u32[]{:S(2)}) copy-start(f32[264,128]{1,0:T(8,128)S(1)} %collective-permute-done.10.s1_ref) | copy-start | bytes 405508
  164.8 0.7 copy-start.11
  164.8 0.7 copy-start.12
  175.8 7.5 %copy-start.20 = (f32[8,128]{1,0:T(8,128)S(1)}, f32[8,128]{1,0:T(8,128)}, u32[]{:S(2)}) copy-start(f32[8,128]{1,0:T(8,128)} %get-tuple-element.58) | copy-start | bytes 12292
  175.9 47.6 %all-to-all-start.2 = ((bf16[128,96,128]{2,1,0:T(8,128)(2,1)}), bf16[128,96,128]{2,1,0:T(8,128)(2,1)S(1)}, u32[]{:S(2)}, u32[]{:S(2)}) async-start(bf16[128,96,128]{2,1,0:T(8,128)(2,1)} %bitcast.18), calls=%async_computation.2 | async-start | bytes 6291456 | tf_op jit(solution)/shard_map/all_to_all | solution.py:391
  225.1 16.0 %all-to-all-start.4 = ((bf16[32,80,128]{2,1,0:T(8,128)(2,1)}), bf16[32,80,128]{2,1,0:T(8,128)(2,1)S(1)}, u32[]{:S(2)}, u32[]{:S(2)}) async-start(bf16[32,80,128]{2,1,0:T(8,128)(2,1)} %broadcast_in_dim.10), calls=%async_computation.4 | async-start | bytes 1310720 | tf_op jit(solution)/shard_map/all_to_all | solution.py:391
  230.4 10.7 %copy-start.5 = (f32[96,128]{1,0:T(8,128)}, f32[96,128]{1,0:T(8,128)S(1)}, u32[]{:S(2)}) copy-start(f32[96,128]{1,0:T(8,128)S(1)} %pad_maximum_fusion.1.r0_ref) | copy-start | bytes 147460
  230.5 5.9 %collective-permute-start.13 = (f32[96,128]{1,0:T(8,128)S(1)}, f32[96,128]{1,0:T(8,128)S(1)}, u32[]{:S(2)}, u32[]{:S(2)}) collective-permute-start(f32[96,128]{1,0:T(8,128)S(1)} %pad_maximum_fusion.1.r0_ref), channel_id=1, source_target_pairs={{0,1},{1,2},{2,3},{3,0},{4,5},{5,6},{6,7},{7,4},{8,9},{9,10},{10,1... | collective-permute-start | bytes 147464 | tf_op jit(solution)/shard_map/ppermute | solution.py:386
  231.3 5.6 %collective-permute-start.14 = (f32[96,128]{1,0:T(8,128)S(1)}, f32[96,128]{1,0:T(8,128)S(1)}, u32[]{:S(2)}, u32[]{:S(2)}) collective-permute-start(f32[96,128]{1,0:T(8,128)S(1)} %pad_maximum_fusion.1.r0_ref), channel_id=1, source_target_pairs={{0,2},{1,3},{2,0},{3,1},{4,6},{5,7},{6,4},{7,5},{8,10},{9,11},{10,... | collective-permute-start | bytes 147464 | tf_op jit(solution)/shard_map/ppermute | solution.py:386
  233.3 4.1 %collective-permute-start.15 = (f32[96,128]{1,0:T(8,128)S(1)}, f32[96,128]{1,0:T(8,128)S(1)}, u32[]{:S(2)}, u32[]{:S(2)}) collective-permute-start(f32[96,128]{1,0:T(8,128)S(1)} %pad_maximum_fusion.1.r0_ref), channel_id=1, source_target_pairs={{0,3},{1,0},{2,1},{3,2},{4,7},{5,4},{6,5},{7,6},{8,11},{9,8},{10,9... | collective-permute-start | bytes 147464 | tf_op jit(solution)/shard_map/ppermute | solution.py:386
  236.3 4.8 %copy-start.15 = (f32[96,128]{1,0:T(8,128)}, f32[96,128]{1,0:T(8,128)S(1)}, u32[]{:S(2)}) copy-start(f32[96,128]{1,0:T(8,128)S(1)} %collective-permute-done.13.r1_ref) | copy-start | bytes 147460
  236.9 4.2 %copy-start.16 = (f32[96,128]{1,0:T(8,128)}, f32[96,128]{1,0:T(8,128)S(1)}, u32[]{:S(2)}) copy-start(f32[96,128]{1,0:T(8,128)S(1)} %collective-permute-done.14.r2_ref) | copy-start | bytes 147460
  237.4 3.7 %copy-start.17 = (f32[96,128]{1,0:T(8,128)}, f32[96,128]{1,0:T(8,128)S(1)}, u32[]{:S(2)}) copy-start(f32[96,128]{1,0:T(8,128)S(1)} %collective-permute-done.15.r3_ref) | copy-start | bytes 147460
  241.1 0.8 copy-start.2
where the time goes:
time: 249 us; the launch traced here: 245 us
  waiting for transfers between devices  116 us (47%)
  starting transfers between devices  63.7 us (26%)
  Pallas kernels  52.5 us (21%)
  local copies, waits for them, and re-layouts  8.29 us (3%)
  other arithmetic  4.3 us (2%)
    ppermute x12, waiting for transfers between devices, around(): got.append(lax.ppermute(value, 'mp', [(i, (i + d) % 4) for i in range(4)]))  56.6 us
    all_to_all x5, waiting for transfers between devices, exchange(): return lax.all_to_all(value, axes, split_axis=0, concat_axis=0, tiled=True)  41.8 us
    all_to_all x5, starting transfers between devices, exchange(): return lax.all_to_all(value, axes, split_axis=0, concat_axis=0, tiled=True)  36.4 us
    ppermute x12, starting transfers between devices, around(): got.append(lax.ppermute(value, 'mp', [(i, (i + d) % 4) for i in range(4)]))  21.3 us
    ppermute x1, waiting for transfers between devices, step(): z_prev = lax.ppermute(velocity[:, 7:8], 'slab', up)  15.6 us
    pallas_call x1, Pallas kernels, step(): call(new_kernel, [((3, 8, 128, 256), F32), ((512, 1536), BF16)], [pltpu.V...  12.1 us
    pallas_call x1, Pallas kernels, step(): call(backward_kernel, [((32, 4, 96, 128), BF16), ((8, 128), F32)], [pltpu...  10.4 us
    pallas_call x1, Pallas kernels, step(): call(middle_kernel, [((32, 4, 64, 128), BF16), wide, wide_f, ((264, 128),...  9.55 us
  transfers between devices with their start and end apart: 21, of which 13 were waited for; matrix products, arithmetic and copies ran while one was open for 2% of the time, Pallas kernels for 13%

commit v1 on v0

--- a/solution.py
+++ b/solution.py
@@ -190,11 +190,11 @@
 
 
 def forward_kernel(
-    m_ref, old_ref, lift_w_ref, w0_ref, w1_ref, w2_ref, w3_ref,
+    place_ref, old_ref, lift_w_ref, w0_ref, w1_ref, w2_ref, w3_ref,
     lifted_ref, query_ref, key_ref, key_spread_ref, value_ref, value_spread_ref,
     query_w_ref, key_w_ref, value_w_ref, out_w_ref, sums_ref, acc_ref,
 ):
-    m = m_ref[0]
+    m = place_ref[0]
     for j, block in enumerate((w0_ref, w1_ref, w2_ref, w3_ref)):
         at = pl.ds(absolute(m, j), 128)
         query_w_ref[:, at] = block[0]
@@ -234,10 +234,21 @@
     sums_ref[256:264, :] = jnp.broadcast_to(count, (8, 128))
 
 
+def dealer(place_ref, mine_ref, theirs_ref):
+    first = place_ref[1] == 0
+
+    def deal(grad, rows, n, at):
+        grad = grad.reshape(16, 2, rows, 128)
+        even, odd = grad[:, 0], grad[:, 1]
+        mine_ref[:, n, at : at + rows, :] = jnp.where(first, even, odd).astype(BF16)
+        theirs_ref[:, n, at : at + rows, :] = jnp.where(first, odd, even).astype(BF16)
+
+    return deal
+
+
 def middle_kernel(
-    s0_ref, s1_ref, s2_ref, s3_ref, lifted_ref, query_ref, new_ref,
-    out_w_ref, proj_w_ref,
-    send_ref, d_query_ref, d_hidden_ref, sums_ref, count_ref,
+    place_ref, s0_ref, s1_ref, s2_ref, s3_ref, lifted_ref, query_ref, new_ref, out_w_ref, proj_w_ref,
+    mine_ref, theirs_ref, d_query_ref, d_hidden_ref, sums_ref, count_ref,
     hidden_ref, d_guess_ref, attended_ref, d_tokens_ref, acc_ref, high_ref, low_ref, loss_ref,
 ):
     total = (s0_ref[...] + s1_ref[...]) + (s2_ref[...] + s3_ref[...])
@@ -289,20 +300,21 @@
     sums_ref[128:256, :] = pack((acc_ref[2], acc_ref[3]))
     loss = jnp.sum(loss_ref[...], axis=(0, 1), keepdims=True) * (1.0 / 50331648)
     sums_ref[256:264, :] = jnp.broadcast_to(loss, (8, 128))
-    grad = dot(hidden_ref[...], d_guess_ref[...], (0, 0)).astype(BF16)
+    deal = dealer(place_ref, mine_ref, theirs_ref)
+    grad = dot(hidden_ref[...], d_guess_ref[...], (0, 0))
     for n in range(4):
         for j in range(3):
             at = n * 384 + j * 128
-            send_ref[:, n, 16 * j : 16 * j + 16, :] = grad[:, at : at + 128].reshape(32, 16, 128)
-    grad = dot(d_tokens_ref[...], attended_ref[...], (0, 0)).astype(BF16)
+            deal(grad[:, at : at + 128], 16, n, 16 * j)
+    grad = dot(d_tokens_ref[...], attended_ref[...], (0, 0))
     for n in range(4):
-        send_ref[:, n, 48:64, :] = grad[:, n * 128 : (n + 1) * 128].reshape(32, 16, 128)
+        deal(grad[:, n * 128 : (n + 1) * 128], 16, n, 48)
 
 
 def backward_kernel(
-    s0_ref, s1_ref, s2_ref, s3_ref, count_ref, old_hbm, lifted_ref, key_ref, key_spread_ref,
+    place_ref, s0_ref, s1_ref, s2_ref, s3_ref, count_ref, old_hbm, lifted_ref, key_ref, key_spread_ref,
     value_ref, value_spread_ref, d_query_ref, d_hidden_ref, query_w_ref, key_w_ref, value_w_ref,
-    send_ref, loss_ref, high_ref, low_ref, d_heads_ref, d_lifted_ref, old_ref, sem,
+    mine_ref, theirs_ref, loss_ref, high_ref, low_ref, d_heads_ref, d_lifted_ref, old_ref, sem,
 ):
     fetch = pltpu.make_async_copy(old_hbm.at[:, 0:1536], old_ref, sem)
     fetch.start()
@@ -339,22 +351,23 @@
         return carry
 
     lax.fori_loop(0, 512 // CHUNK, rows, 0)
-    grad = dot(lifted_ref[...], d_heads_ref[...], (0, 0)).astype(BF16)
+    deal = dealer(place_ref, mine_ref, theirs_ref)
+    grad = dot(lifted_ref[...], d_heads_ref[...], (0, 0))
     for n in range(4):
         for j in range(3):
             at = 512 * j + 128 * n
-            send_ref[:, n, 48 + 16 * j : 64 + 16 * j, :] = grad[:, at : at + 128].reshape(32, 16, 128)
+            deal(grad[:, at : at + 128], 16, n, 48 + 16 * j)
     fetch.wait()
-    grad = dot(old_ref[...], d_lifted_ref[...], (0, 0)).astype(BF16)
+    grad = dot(old_ref[...], d_lifted_ref[...], (0, 0))
     for n in range(4):
-        send_ref[:, n, 0:48, :] = grad[:, n * 128 : (n + 1) * 128].reshape(32, 48, 128)
+        deal(grad[:, n * 128 : (n + 1) * 128], 48, n, 0)
 
 
 def last_kernel(
-    m_ref, r0_ref, r1_ref, r2_ref, r3_ref, heads_ref,
+    place_ref, r0_ref, r1_ref, r2_ref, r3_ref, heads_ref,
     lift_ref, query_ref, key_ref, value_ref, out_ref, proj_ref, loss_ref,
 ):
-    m = m_ref[0]
+    m = place_ref[0]
     for j, block in enumerate((r0_ref, r1_ref, r2_ref, r3_ref)):
         lift_ref[:, pl.ds(absolute(m, j), 128)] = block[0:48, :]
         for k in range(3):
@@ -365,7 +378,7 @@
     value_ref[...] = heads_ref[:, 32:48, :].astype(F32).reshape(512, 128)
     out_ref[...] = heads_ref[:, 48:64, :].astype(F32).reshape(512, 128).T
     loss = jnp.sum(heads_ref[:, 64:80, :].astype(F32), axis=0)
-    loss_ref[...] = jnp.broadcast_to(loss[0:1] + loss[1:2], (8, 128))
+    loss_ref[...] = loss[0:1, 0:1] + loss[1:2, 0:1]
 
 
 def call(body, outs, scratch=(), ins="", results=None):
@@ -391,9 +404,27 @@
     return lax.all_to_all(value, axes, split_axis=0, concat_axis=0, tiled=True)
 
 
+def pair_sum(mine, theirs):
+    got = lax.ppermute(theirs, "slab", [(i, i ^ 1) for i in range(32)])
+    return (mine.astype(F32) + got.astype(F32)).astype(BF16)
+
+
+def total(partial):
+    groups = [[(2 * q + c) * 4 + n for q in range(16) for n in range(4)] for c in range(2)]
+    got = lax.all_to_all(
+        partial.reshape(64, -1, 128),
+        ("slab", "mp"),
+        split_axis=0,
+        concat_axis=0,
+        axis_index_groups=groups,
+        tiled=True,
+    )
+    return jnp.sum(got.astype(F32), axis=0)
+
+
 def step(velocity, anchors, dest, w_lift, w_query, w_key, w_value, w_out, w_proj):
     slabs = lax.axis_size("slab")
-    m = lax.axis_index("mp").reshape(1)
+    place = jnp.stack([lax.axis_index("mp"), lax.axis_index("slab") & 1])
     up = [(i, (i + 1) % slabs) for i in range(slabs)]
     z_prev = lax.ppermute(velocity[:, 7:8], "slab", up)
     z_next = lax.ppermute(velocity[:, 0:1], "slab", [(j, i) for i, j in up])
@@ -430,11 +461,11 @@
         [wide, wide, wide, wide_f, wide, wide_f, wide, wide, wide, wide, ((264, 128), F32)],
         [pltpu.VMEM((4, 128, 128), F32)],
         "svvvvvv",
-    )(m, old, w_lift, *heads_w)
+    )(place, old, w_lift, *heads_w)
     sums = around(sums)
-    send_out, d_query, d_hidden, d_sums, count = call(
+    mine, theirs, d_query, d_hidden, d_sums, count = call(
         middle_kernel,
-        [((32, 4, 64, 128), BF16), wide, wide_f, ((264, 128), F32), ((8, 128), F32)],
+        [((16, 4, 64, 128), BF16), ((16, 4, 64, 128), BF16), wide, wide_f, ((264, 128), F32), ((8, 128), F32)],
         [
             pltpu.VMEM((512, 512), BF16),
             pltpu.VMEM((512, 1536), BF16),
@@ -445,14 +476,13 @@
             pltpu.VMEM((4, 128, 128), BF16),
             pltpu.VMEM((8, 1536), F32),
         ],
-        "vvvvvvvvv",
-    )(*sums, lifted, query, new, wo, w_proj)
+        "svvvvvvvvv",
+    )(place, *sums, lifted, query, new, wo, w_proj)
     d_sums = around(d_sums)
-    everyone = ("slab", "mp")
-    got_out = exchange(send_out.reshape(128, 64, 128), everyone)
-    send_in, loss_part = call(
+    total_out = total(pair_sum(mine, theirs))
+    mine, theirs, loss_part = call(
         backward_kernel,
-        [((32, 4, 96, 128), BF16), ((8, 128), F32)],
+        [((16, 4, 96, 128), BF16), ((16, 4, 96, 128), BF16), ((8, 128), F32)],
         [
             pltpu.VMEM((4, 128, 128), BF16),
             pltpu.VMEM((4, 128, 128), BF16),
@@ -461,12 +491,9 @@
             pltpu.VMEM((512, 1536), BF16),
             pltpu.SemaphoreType.DMA,
         ],
-        "vvvvvhvvvvvvvvvv",
-    )(*d_sums, count, old, lifted, key, key_spread, value, value_spread, d_query, d_hidden, wq, wk, wv)
-    got_in = exchange(send_in.reshape(128, 96, 128), everyone)
-
-    total_out = jnp.sum(got_out.astype(F32), axis=0)
-    total_in = jnp.sum(got_in.astype(F32), axis=0)
+        "svvvvvhvvvvvvvvvv",
+    )(place, *d_sums, count, old, lifted, key, key_spread, value, value_spread, d_query, d_hidden, wq, wk, wv)
+    total_in = total(pair_sum(mine, theirs))
     blocks = jnp.concatenate([total_in[0:48], total_out[0:48]], axis=0)
     loss_high = loss_part.astype(BF16)
     loss_low = (loss_part - loss_high.astype(F32)).astype(BF16)
@@ -482,12 +509,12 @@
             ((512, 128), F32),
             ((128, 512), F32),
             ((16, 1536), F32),
-            ((8, 128), F32),
+            ((1, 1), F32),
         ],
         (),
         "svvvvv",
-    )(m, *around(blocks), heads)
-    return (new_velocity, loss[0, 0], lift, g_query, g_key, g_value, g_out, proj)
+    )(place, *around(blocks), heads)
+    return (new_velocity, loss.reshape(()), lift, g_query, g_key, g_value, g_out, proj)
 
 
 def solution(mesh):

time: 249 us -> 229 us (0.920)
  waiting for transfers between devices: 116 us -> 93 us
    all_to_all x5 -> x3, waiting for transfers between devices: 41.8 us -> 3.93 us  [exchange(): return lax.all_to_all(value, axes, split_axis=0, concat_axis=0, tiled=True)]
    all_to_all x0 -> x2, waiting for transfers between devices: none -> 34.8 us  [total(): lax.all_to_all(partial.reshape(64, -1, 128), ('slab', 'mp'), split_axis=0...]
    ppermute x12, waiting for transfers between devices: 56.6 us -> 37 us  [around(): got.append(lax.ppermute(value, 'mp', [(i, (i + d) % 4) for i in range(4)]))]
    all_to_all x0 -> x2, starting transfers between devices: none -> 16.8 us  [total(): lax.all_to_all(partial.reshape(64, -1, 128), ('slab', 'mp'), split_axis=0...]
    all_to_all x5 -> x3, starting transfers between devices: 36.4 us -> 21.4 us  [exchange(): return lax.all_to_all(value, axes, split_axis=0, concat_axis=0, tiled=True)]
    convert_element_type x0 -> x2, other arithmetic: none -> 4.45 us  [pair_sum(): return (mine.astype(F32) + got.astype(F32)).astype(BF16)]
    ppermute x12, starting transfers between devices: 21.3 us -> 18.8 us  [around(): got.append(lax.ppermute(value, 'mp', [(i, (i + d) % 4) for i in range(4)]))]
  transfers between devices with their start and end apart: 21 -> 23, of which waited for: 13 -> 15; matrix products, arithmetic and copies ran while one was open for 2% -> 4% of each run, Pallas kernels for 13% -> 14%
where the time goes in v1:
time: 229 us; the launch traced here: 224 us
  waiting for transfers between devices  93 us (41%)
  starting transfers between devices  63.1 us (28%)
  Pallas kernels  52.9 us (23%)
  local copies, waits for them, and re-layouts  7.89 us (3%)
  other arithmetic  6.5 us (3%)
    ppermute x12, waiting for transfers between devices, around(): got.append(lax.ppermute(value, 'mp', [(i, (i + d) % 4) for i in range(4)]))  37 us
    all_to_all x2, waiting for transfers between devices, total(): lax.all_to_all(partial.reshape(64, -1, 128), ('slab', 'mp'), split_axis=0...  34.8 us
    all_to_all x3, starting transfers between devices, exchange(): return lax.all_to_all(value, axes, split_axis=0, concat_axis=0, tiled=True)  21.4 us
    ppermute x12, starting transfers between devices, around(): got.append(lax.ppermute(value, 'mp', [(i, (i + d) % 4) for i in range(4)]))  18.8 us
    all_to_all x2, starting transfers between devices, total(): lax.all_to_all(partial.reshape(64, -1, 128), ('slab', 'mp'), split_axis=0...  16.8 us
    ppermute x1, waiting for transfers between devices, step(): z_prev = lax.ppermute(velocity[:, 7:8], 'slab', up)  15.6 us
    pallas_call x1, Pallas kernels, step(): call(new_kernel, [((3, 8, 128, 256), F32), ((512, 1536), BF16)], [pltpu.V...  12.1 us
    pallas_call x1, Pallas kernels, step(): call(backward_kernel, [((16, 4, 96, 128), BF16), ((16, 4, 96, 128), BF16)...  10.5 us
  transfers between devices with their start and end apart: 23, of which 15 were waited for; matrix products, arithmetic and copies ran while one was open for 4% of the time, Pallas kernels for 14%

profile of v1, /device:TPU:6, one launch (start us, length us, event | category | flops | bytes accessed | tf_op | source)
XLA Modules:
  0.0 224.5 jit_solution(1329494139918666106)
XLA Ops:
  0.6 8.8 %shard_map.152 = (bf16[512,1664]{1,0:T(8,128)(2,1)}, bf16[512,512]{1,0:T(8,128)(2,1)}) custom-call(f32[3,8,128,256]{3,2,1,0:T(8,128)} %field_hbm.3, s32[3,1,256]{2,1,0:T(1,128)} %bitcast.24, s32[1,256]{1,0:T(1,128)} %bitcast.25), custom_call_target="tpu_custom_call" | custom-call | tf_op jit(solution)/shard_map/pallas_call | solution.py:437
  9.4 7.6 %all-to-all-start = ((bf16[32,16,1664]{2,1,0:T(8,128)(2,1)}), bf16[32,16,1664]{2,1,0:T(8,128)(2,1)S(1)}, u32[]{:S(2)}, u32[]{:S(2)}) async-start(bf16[32,16,1664]{2,1,0:T(8,128)(2,1)} %bitcast.19), calls=%async_computation | async-start | bytes 3407872 | tf_op jit(solution)/shard_map/all_to_all | solution.py:404
  17.0 1.2 fusion.1
  18.2 0.2 collective-permute-start
  18.4 1.6 collective-permute-start.1
  20.0 1.1 fusion
  21.1 2.0 collective-permute-start.2
  23.1 2.2 collective-permute-start.3
  25.3 1.7 collective-permute-done.2.y_prev_ref
  27.0 15.6 %collective-permute-done.z_prev_ref = f32[3,1,128,256]{3,2,1,0:T(8,128)S(1)} collective-permute-done((f32[3,1,128,256]{3,2,1,0:T(8,128)S(1)}, f32[3,1,128,256]{3,2,1,0:T(8,128)S(1)}, u32[]{:S(2)}, u32[]{:S(2)}) %collective-permute-start) | collective-permute-done | bytes 393248 | tf_op jit(solution)/shard_map/ppermute | solution.py:429
  42.6 0.7 copy-done.8
  43.3 0.1 copy-done.9
  43.5 12.1 %shard_map.153 = (f32[3,8,128,256]{3,2,1,0:T(8,128)}, bf16[512,1536]{1,0:T(8,128)(2,1)}) custom-call(f32[3,8,128,256]{3,2,1,0:T(8,128)} %field_hbm.3, f32[3,1,128,256]{3,2,1,0:T(8,128)} %copy-done.8, f32[3,1,128,256]{3,2,1,0:T(8,128)} %copy-done.9, f32[3,8,1,256]{3,2,1,0:T(1,128)} %copy-done.22, f32[3,8,1,256]{3,2,1,0:T(1,128)} %copy-done.23, ...), custom_call_target="tpu_custom_call" | custom-call | tf_op jit(solution)/shard_map/pallas_call | solution.py:444
  55.6 0.0 copy-start.17
  55.6 0.0 copy-start.18
  55.6 7.3 %all-to-all-start.1 = ((bf16[32,16,1536]{2,1,0:T(8,128)(2,1)}), bf16[32,16,1536]{2,1,0:T(8,128)(2,1)S(1)}, u32[]{:S(2)}, u32[]{:S(2)}) async-start(bf16[32,16,1536]{2,1,0:T(8,128)(2,1)} %bitcast.20), calls=%async_computation.1 | async-start | bytes 3145728 | tf_op jit(solution)/shard_map/all_to_all | solution.py:404
  63.0 1.0 pad_maximum_fusion.w0_ref
  64.0 2.0 collective-permute-start.4
  66.0 3.6 %collective-permute-start.5 = (bf16[4,512,128]{2,1,0:T(8,128)(2,1)S(1)}, bf16[4,512,128]{2,1,0:T(8,128)(2,1)S(1)}, u32[]{:S(2)}, u32[]{:S(2)}) collective-permute-start(bf16[4,512,128]{2,1,0:T(8,128)(2,1)S(1)} %pad_maximum_fusion.w0_ref), channel_id=1, source_target_pairs={{0,2},{1,3},{2,0},{3,1},{4,6},{5,7},{6,4},{7,5},{8,10},{9,11},{10,... | collective-permute-start | bytes 1572872 | tf_op jit(solution)/shard_map/ppermute | solution.py:399
  69.6 1.0 collective-permute-start.6
  70.6 0.6 pad_add_fusion.place_ref
  71.2 9.2 %collective-permute-done.4.w1_ref = bf16[4,512,128]{2,1,0:T(8,128)(2,1)S(1)} collective-permute-done((bf16[4,512,128]{2,1,0:T(8,128)(2,1)S(1)}, bf16[4,512,128]{2,1,0:T(8,128)(2,1)S(1)}, u32[]{:S(2)}, u32[]{:S(2)}) %collective-permute-start.4) | collective-permute-done | bytes 524320 | tf_op jit(solution)/shard_map/ppermute | solution.py:399
  80.3 12.4 %collective-permute-done.5.w2_ref = bf16[4,512,128]{2,1,0:T(8,128)(2,1)S(1)} collective-permute-done((bf16[4,512,128]{2,1,0:T(8,128)(2,1)S(1)}, bf16[4,512,128]{2,1,0:T(8,128)(2,1)S(1)}, u32[]{:S(2)}, u32[]{:S(2)}) %collective-permute-start.5) | collective-permute-done | bytes 524320 | tf_op jit(solution)/shard_map/ppermute | solution.py:399
  92.8 0.8 copy-done.7
  93.6 9.5 %shard_map.154 = (bf16[512,512]{1,0:T(8,128)(2,1)}, bf16[512,512]{1,0:T(8,128)(2,1)}, bf16[512,512]{1,0:T(8,128)(2,1)}, f32[512,512]{1,0:T(8,128)}, bf16[512,512...) custom-call(s32[2]{0:T(128)} %pad_add_fusion.place_ref, ...), custom_call_target="tpu_custom_call" | custom-call | tf_op jit(solution)/shard_map/pallas_call | solution.py:459
  103.1 0.6 collective-permute-start.7
  103.7 2.4 %collective-permute-start.8 = (f32[264,128]{1,0:T(8,128)}, f32[264,128]{1,0:T(8,128)S(1)}, u32[]{:S(2)}, u32[]{:S(2)}) collective-permute-start(f32[264,128]{1,0:T(8,128)} %get-tuple-element.42.s0_ref), channel_id=1, source_target_pairs={{0,2},{1,3},{2,0},{3,1},{4,6},{5,7},{6,4},{7,5},{8,10},{9,11},{10,... | collective-permute-start | bytes 405512 | tf_op jit(solution)/shard_map/ppermute | solution.py:399
  106.1 1.2 collective-permute-start.9
  107.3 3.1 %collective-permute-done.7.s1_ref = f32[264,128]{1,0:T(8,128)S(1)} collective-permute-done((f32[264,128]{1,0:T(8,128)}, f32[264,128]{1,0:T(8,128)S(1)}, u32[]{:S(2)}, u32[]{:S(2)}) %collective-permute-start.7) | collective-permute-done | bytes 135200 | tf_op jit(solution)/shard_map/ppermute | solution.py:399
  110.4 2.3 %collective-permute-done.8.s2_ref = f32[264,128]{1,0:T(8,128)S(1)} collective-permute-done((f32[264,128]{1,0:T(8,128)}, f32[264,128]{1,0:T(8,128)S(1)}, u32[]{:S(2)}, u32[]{:S(2)}) %collective-permute-start.8) | collective-permute-done | bytes 135200 | tf_op jit(solution)/shard_map/ppermute | solution.py:399
  112.7 0.1 collective-permute-done.9.s3_ref
  112.8 0.5 copy-done.14
  113.3 0.1 copy-done.16
  113.5 0.5 copy-done.1
  114.0 9.7 %shard_map.155 = (bf16[16,4,64,128]{3,2,1,0:T(8,128)(2,1)}, bf16[16,4,64,128]{3,2,1,0:T(8,128)(2,1)}, bf16[512,512]{1,0:T(8,128)(2,1)}, f32[512,512]{1,0:T(8,128...) custom-call(s32[2]{0:T(128)} %pad_add_fusion.place_ref, f32[264,128]{1,0:T(8,128)} %get-tuple-element.42.s0_ref, ...), custom_call_target="tpu_custom_call" | custom-call | tf_op jit(solution)/shard_map/pallas_call | solution.py:466
  123.7 0.0 collective-permute-start.14
  123.8 0.8 collective-permute-start.10
  124.6 3.4 %collective-permute-start.11 = (f32[264,128]{1,0:T(8,128)}, f32[264,128]{1,0:T(8,128)S(1)}, u32[]{:S(2)}, u32[]{:S(2)}) collective-permute-start(f32[264,128]{1,0:T(8,128)} %get-tuple-element.47.s0_ref), channel_id=1, source_target_pairs={{0,2},{1,3},{2,0},{3,1},{4,6},{5,7},{6,4},{7,5},{8,10},{9,11},{10,... | collective-permute-start | bytes 405512 | tf_op jit(solution)/shard_map/ppermute | solution.py:399
  128.0 3.2 %collective-permute-done.10.s1_ref = f32[264,128]{1,0:T(8,128)S(1)} collective-permute-done((f32[264,128]{1,0:T(8,128)}, f32[264,128]{1,0:T(8,128)S(1)}, u32[]{:S(2)}, u32[]{:S(2)}) %collective-permute-start.10) | collective-permute-done | bytes 135200 | tf_op jit(solution)/shard_map/ppermute | solution.py:399
  131.2 3.8 %collective-permute-done.11.s2_ref = f32[264,128]{1,0:T(8,128)S(1)} collective-permute-done((f32[264,128]{1,0:T(8,128)}, f32[264,128]{1,0:T(8,128)S(1)}, u32[]{:S(2)}, u32[]{:S(2)}) %collective-permute-start.11) | collective-permute-done | bytes 135200 | tf_op jit(solution)/shard_map/ppermute | solution.py:399
  135.0 0.6 copy-done.13
  135.6 0.0 copy-done.15
  135.7 10.5 %shard_map.156 = (bf16[16,4,96,128]{3,2,1,0:T(8,128)(2,1)}, bf16[16,4,96,128]{3,2,1,0:T(8,128)(2,1)}, f32[8,128]{1,0:T(8,128)}) custom-call(s32[2]{0:T(128)} %pad_add_fusion.place_ref, f32[264,128]{1,0:T(8,128)} %get-tuple-element.47.s0_ref, f32[264,128]{1,0:T(8,128)} %copy-done.11, f32[264,128]{1,0:T(8,128)} %copy-done.13, f32[264,128]{1,0:T(8,128)} %copy-done.15, ...), custom_call_target="tpu_custom_call" | custom-call | tf_op jit(solution)/shard_map/pallas_call | solution.py:483
  146.2 0.1 collective-permute-start.13
  146.3 1.4 add_convert_fusion.1
  147.8 9.7 %all-to-all-start.3 = ((bf16[64,64,128]{2,1,0:T(8,128)(2,1)}), bf16[64,64,128]{2,1,0:T(8,128)(2,1)S(1)}, u32[]{:S(2)}, u32[]{:S(2)}) async-start(bf16[64,64,128]{2,1,0:T(8,128)(2,1)} %bitcast.13), calls=%async_computation.3 | async-start | bytes 2097152 | tf_op jit(solution)/shard_map/all_to_all | solution.py:414
  157.5 3.0 %add_convert_fusion = bf16[16,4,96,128]{3,2,1,0:T(8,128)(2,1)} fusion(bf16[16,4,96,128]{3,2,1,0:T(8,128)(2,1)} %collective-permute-done.13, bf16[16,4,96,128]{3,2,1,0:T(8,128)(2,1)S(1)} %copy-done.4), kind=kLoop, calls=%fused_computation.1 | loop fusion | flops 3145728 | bytes 4718592 | tf_op jit(solution)/shard_map/convert_element_type | solution.py:409
  160.5 13.9 %all-to-all-done.3 = bf16[64,64,128]{2,1,0:T(8,128)(2,1)S(1)} async-done(((bf16[64,64,128]{2,1,0:T(8,128)(2,1)}), bf16[64,64,128]{2,1,0:T(8,128)(2,1)S(1)}, u32[]{:S(2)}, u32[]{:S(2)}) %all-to-all-start.3) | async-done | bytes 1048608 | tf_op jit(solution)/shard_map/all_to_all | solution.py:414
  174.4 7.2 %all-to-all-start.2 = ((bf16[64,96,128]{2,1,0:T(8,128)(2,1)}), bf16[64,96,128]{2,1,0:T(8,128)(2,1)S(1)}, u32[]{:S(2)}, u32[]{:S(2)}) async-start(bf16[64,96,128]{2,1,0:T(8,128)(2,1)} %bitcast.12), calls=%async_computation.2 | async-start | bytes 3145728 | tf_op jit(solution)/shard_map/all_to_all | solution.py:414
  181.6 0.2 convert_reduce_fusion.1
  181.8 20.9 %all-to-all-done.2 = bf16[64,96,128]{2,1,0:T(8,128)(2,1)S(1)} async-done(((bf16[64,96,128]{2,1,0:T(8,128)(2,1)}), bf16[64,96,128]{2,1,0:T(8,128)(2,1)S(1)}, u32[]{:S(2)}, u32[]{:S(2)}) %all-to-all-start.2) | async-done | bytes 1572896 | tf_op jit(solution)/shard_map/all_to_all | solution.py:414
  202.7 0.2 convert_reduce_fusion
  202.9 0.2 concatenate.14
  203.1 0.9 broadcast_in_dim.10
  204.0 6.5 %all-to-all-start.4 = ((bf16[32,80,128]{2,1,0:T(8,128)(2,1)}), bf16[32,80,128]{2,1,0:T(8,128)(2,1)S(1)}, u32[]{:S(2)}, u32[]{:S(2)}) async-start(bf16[32,80,128]{2,1,0:T(8,128)(2,1)} %broadcast_in_dim.10), calls=%async_computation.4 | async-start | bytes 1310720 | tf_op jit(solution)/shard_map/all_to_all | solution.py:404
  210.6 0.9 collective-permute-start.15
  211.5 1.6 collective-permute-start.16
  213.1 1.3 collective-permute-start.17
  214.4 2.1 collective-permute-done.15.r1_ref
  216.5 0.6 collective-permute-done.16.r2_ref
  217.1 0.3 collective-permute-done.17.r3_ref
  217.4 3.9 %all-to-all-done.4.heads_ref = bf16[32,80,128]{2,1,0:T(8,128)(2,1)S(1)} async-done(((bf16[32,80,128]{2,1,0:T(8,128)(2,1)}), bf16[32,80,128]{2,1,0:T(8,128)(2,1)S(1)}, u32[]{:S(2)}, u32[]{:S(2)}) %all-to-all-start.4) | async-done | bytes 655392 | tf_op jit(solution)/shard_map/all_to_all | solution.py:404
  221.3 0.8 copy-done.2
  222.2 2.3 %shard_map.157 = (f32[48,512]{1,0:T(8,128)}, f32[512,128]{1,0:T(8,128)}, f32[512,128]{1,0:T(8,128)}, f32[512,128]{1,0:T(8,128)}, f32[128,512]{1,0:T(8,128)}, /*index=5*/f32[16,1536]{1,0:T(8,128)}, f32[1,1]{1,0:T(1,128)}) custom-call(s32[2]{0:T(128)} %pad_add_fusion.place_ref, f32[96,128]{1,0:T(8,128)} %copy-done.10, f32[96,128]{1,0:T(8,128)} %copy-done.19, ...), custom_call_target="tpu_custom_call" | custom-call | tf_op jit(solution)/shard_map/pallas_call | solution.py:503
  (59 shorter events, 0.2 us)
Async XLA Ops:
  9.4 46.2 %all-to-all-start = ((bf16[32,16,1664]{2,1,0:T(8,128)(2,1)}), bf16[32,16,1664]{2,1,0:T(8,128)(2,1)S(1)}, u32[]{:S(2)}, u32[]{:S(2)}) async-start(bf16[32,16,1664]{2,1,0:T(8,128)(2,1)} %bitcast.19), calls=%async_computation | async-start | bytes 3407872 | tf_op jit(solution)/shard_map/all_to_all | solution.py:404
  18.2 24.4 %collective-permute-start = (f32[3,1,128,256]{3,2,1,0:T(8,128)S(1)}, f32[3,1,128,256]{3,2,1,0:T(8,128)S(1)}, u32[]{:S(2)}, u32[]{:S(2)}) collective-permute-start(f32[3,1,128,256]{3,2,1,0:T(8,128)S(1)} %get-tuple-element.75), channel_id=1, source_target_pairs={{0,4},{4,8},{8,12},{12,16},{16,20},{20,24},{24,28},{28,32},{32,36}... | collective-permute-start | bytes 1179656 | tf_op jit(solution)/shard_map/ppermute | solution.py:429
  18.4 24.2 %collective-permute-start.1 = (f32[3,1,128,256]{3,2,1,0:T(8,128)S(1)}, f32[3,1,128,256]{3,2,1,0:T(8,128)S(1)}, u32[]{:S(2)}, u32[]{:S(2)}) collective-permute-start(f32[3,1,128,256]{3,2,1,0:T(8,128)S(1)} %get-tuple-element.74), channel_id=1, source_target_pairs={{4,0},{8,4},{12,8},{16,12},{20,16},{24,20},{28,24},{32,28},{36,32}... | collective-permute-start | bytes 1179656 | tf_op jit(solution)/shard_map/ppermute | solution.py:430
  21.1 5.9 %collective-permute-start.2 = (f32[3,8,1,256]{3,2,1,0:T(1,128)S(1)}, f32[3,8,1,256]{3,2,1,0:T(1,128)S(1)}, u32[]{:S(2)}, u32[]{:S(2)}) collective-permute-start(f32[3,8,1,256]{3,2,1,0:T(1,128)S(1)} %get-tuple-element.73), channel_id=1, source_target_pairs={{0,1},{1,2},{2,3},{3,0},{4,5},{5,6},{6,7},{7,4},{8,9},{9,10},{10,1... | collective-permute-start | bytes 73736 | tf_op jit(solution)/shard_map/ppermute | solution.py:432
  23.1 3.9 %collective-permute-start.3 = (f32[3,8,1,256]{3,2,1,0:T(1,128)S(1)}, f32[3,8,1,256]{3,2,1,0:T(1,128)S(1)}, u32[]{:S(2)}, u32[]{:S(2)}) collective-permute-start(f32[3,8,1,256]{3,2,1,0:T(1,128)S(1)} %get-tuple-element.72), channel_id=1, source_target_pairs={{1,0},{2,1},{3,2},{0,3},{5,4},{6,5},{7,6},{4,7},{9,8},{10,9},{11,1... | collective-permute-start | bytes 73736 | tf_op jit(solution)/shard_map/ppermute | solution.py:433
  27.0 15.6 %copy-start.22 = (f32[3,8,1,256]{3,2,1,0:T(1,128)}, f32[3,8,1,256]{3,2,1,0:T(1,128)S(1)}, u32[]{:S(2)}) copy-start(f32[3,8,1,256]{3,2,1,0:T(1,128)S(1)} %collective-permute-done.2.y_prev_ref) | copy-start | bytes 73732
  27.0 15.6 %copy-start.23 = (f32[3,8,1,256]{3,2,1,0:T(1,128)}, f32[3,8,1,256]{3,2,1,0:T(1,128)S(1)}, u32[]{:S(2)}) copy-start(f32[3,8,1,256]{3,2,1,0:T(1,128)S(1)} %collective-permute-done.3.y_next_ref) | copy-start | bytes 73732
  42.6 0.8 copy-start.8
  42.6 0.9 copy-start.9
  55.6 7.3 %copy-start.17 = (bf16[128,512]{1,0:T(8,128)(2,1)S(1)}, bf16[128,512]{1,0:T(8,128)(2,1)}, u32[]{:S(2)}) copy-start(bf16[128,512]{1,0:T(8,128)(2,1)} %param.16) | copy-start | bytes 393220
  55.6 7.3 %copy-start = (bf16[32,16,1664]{2,1,0:T(8,128)(2,1)}, bf16[32,16,1664]{2,1,0:T(8,128)(2,1)S(1)}, u32[]{:S(2)}) copy-start(bf16[32,16,1664]{2,1,0:T(8,128)(2,1)S(1)} %all-to-all-done) | copy-start | bytes 5111812
  55.6 7.3 %copy-start.18 = (bf16[512,128]{1,0:T(8,128)(2,1)S(1)}, bf16[512,128]{1,0:T(8,128)(2,1)}, u32[]{:S(2)}) copy-start(bf16[512,128]{1,0:T(8,128)(2,1)} %param.15) | copy-start | bytes 393220
  55.6 57.2 %all-to-all-start.1 = ((bf16[32,16,1536]{2,1,0:T(8,128)(2,1)}), bf16[32,16,1536]{2,1,0:T(8,128)(2,1)S(1)}, u32[]{:S(2)}, u32[]{:S(2)}) async-start(bf16[32,16,1536]{2,1,0:T(8,128)(2,1)} %bitcast.20), calls=%async_computation.1 | async-start | bytes 3145728 | tf_op jit(solution)/shard_map/all_to_all | solution.py:404
  64.0 28.7 %copy-start.3 = (bf16[4,512,128]{2,1,0:T(8,128)(2,1)}, bf16[4,512,128]{2,1,0:T(8,128)(2,1)S(1)}, u32[]{:S(2)}) copy-start(bf16[4,512,128]{2,1,0:T(8,128)(2,1)S(1)} %pad_maximum_fusion.w0_ref) | copy-start | bytes 1572868
  64.0 16.3 %collective-permute-start.4 = (bf16[4,512,128]{2,1,0:T(8,128)(2,1)S(1)}, bf16[4,512,128]{2,1,0:T(8,128)(2,1)S(1)}, u32[]{:S(2)}, u32[]{:S(2)}) collective-permute-start(bf16[4,512,128]{2,1,0:T(8,128)(2,1)S(1)} %pad_maximum_fusion.w0_ref), channel_id=1, source_target_pairs={{0,1},{1,2},{2,3},{3,0},{4,5},{5,6},{6,7},{7,4},{8,9},{9,10},{10,1... | collective-permute-start | bytes 1572872 | tf_op jit(solution)/shard_map/ppermute | solution.py:399
  66.0 26.7 %collective-permute-start.5 = (bf16[4,512,128]{2,1,0:T(8,128)(2,1)S(1)}, bf16[4,512,128]{2,1,0:T(8,128)(2,1)S(1)}, u32[]{:S(2)}, u32[]{:S(2)}) collective-permute-start(bf16[4,512,128]{2,1,0:T(8,128)(2,1)S(1)} %pad_maximum_fusion.w0_ref), channel_id=1, source_target_pairs={{0,2},{1,3},{2,0},{3,1},{4,6},{5,7},{6,4},{7,5},{8,10},{9,11},{10,... | collective-permute-start | bytes 1572872 | tf_op jit(solution)/shard_map/ppermute | solution.py:399
  69.6 23.2 %collective-permute-start.6 = (bf16[4,512,128]{2,1,0:T(8,128)(2,1)S(1)}, bf16[4,512,128]{2,1,0:T(8,128)(2,1)}, u32[]{:S(2)}, u32[]{:S(2)}) collective-permute-start(bf16[4,512,128]{2,1,0:T(8,128)(2,1)S(1)} %pad_maximum_fusion.w0_ref), channel_id=1, source_target_pairs={{0,3},{1,0},{2,1},{3,2},{4,7},{5,4},{6,5},{7,6},{8,11},{9,8},{10,9... | collective-permute-start | bytes 1572872 | tf_op jit(solution)/shard_map/ppermute | solution.py:399
  80.3 12.4 %copy-start.6 = (bf16[4,512,128]{2,1,0:T(8,128)(2,1)}, bf16[4,512,128]{2,1,0:T(8,128)(2,1)S(1)}, u32[]{:S(2)}) copy-start(bf16[4,512,128]{2,1,0:T(8,128)(2,1)S(1)} %collective-permute-done.4.w1_ref) | copy-start | bytes 1572868
  92.8 0.8 copy-start.7
  103.1 7.3 %collective-permute-start.7 = (f32[264,128]{1,0:T(8,128)}, f32[264,128]{1,0:T(8,128)S(1)}, u32[]{:S(2)}, u32[]{:S(2)}) collective-permute-start(f32[264,128]{1,0:T(8,128)} %get-tuple-element.42.s0_ref), channel_id=1, source_target_pairs={{0,1},{1,2},{2,3},{3,0},{4,5},{5,6},{6,7},{7,4},{8,9},{9,10},{10,1... | collective-permute-start | bytes 405512 | tf_op jit(solution)/shard_map/ppermute | solution.py:399
  103.7 9.0 %collective-permute-start.8 = (f32[264,128]{1,0:T(8,128)}, f32[264,128]{1,0:T(8,128)S(1)}, u32[]{:S(2)}, u32[]{:S(2)}) collective-permute-start(f32[264,128]{1,0:T(8,128)} %get-tuple-element.42.s0_ref), channel_id=1, source_target_pairs={{0,2},{1,3},{2,0},{3,1},{4,6},{5,7},{6,4},{7,5},{8,10},{9,11},{10,... | collective-permute-start | bytes 405512 | tf_op jit(solution)/shard_map/ppermute | solution.py:399
  106.1 6.7 %collective-permute-start.9 = (f32[264,128]{1,0:T(8,128)}, f32[264,128]{1,0:T(8,128)S(1)}, u32[]{:S(2)}, u32[]{:S(2)}) collective-permute-start(f32[264,128]{1,0:T(8,128)} %get-tuple-element.42.s0_ref), channel_id=1, source_target_pairs={{0,3},{1,0},{2,1},{3,2},{4,7},{5,4},{6,5},{7,6},{8,11},{9,8},{10,9... | collective-permute-start | bytes 405512 | tf_op jit(solution)/shard_map/ppermute | solution.py:399
  110.4 2.4 %copy-start.12 = (f32[264,128]{1,0:T(8,128)}, f32[264,128]{1,0:T(8,128)S(1)}, u32[]{:S(2)}) copy-start(f32[264,128]{1,0:T(8,128)S(1)} %collective-permute-done.7.s1_ref) | copy-start | bytes 405508
  112.7 0.7 copy-start.14
  112.8 0.7 copy-start.16
  112.8 1.2 copy-start.1
  123.7 22.6 %collective-permute-start.14 = (bf16[16,4,64,128]{3,2,1,0:T(8,128)(2,1)}, bf16[16,4,64,128]{3,2,1,0:T(8,128)(2,1)S(1)}, u32[]{:S(2)}, u32[]{:S(2)}) collective-permute-start(bf16[16,4,64,128]{3,2,1,0:T(8,128)(2,1)} %get-tuple-element.61), channel_id=1, source_target_pairs={{0,4},{4,0},{8,12},{12,8},{16,20},{20,16},{24,28},{28,24},{32,36},... | collective-permute-start | bytes 3145736 | tf_op jit(solution)/shard_map/ppermute | solution.py:408
  123.8 7.4 %collective-permute-start.10 = (f32[264,128]{1,0:T(8,128)}, f32[264,128]{1,0:T(8,128)S(1)}, u32[]{:S(2)}, u32[]{:S(2)}) collective-permute-start(f32[264,128]{1,0:T(8,128)} %get-tuple-element.47.s0_ref), channel_id=1, source_target_pairs={{0,1},{1,2},{2,3},{3,0},{4,5},{5,6},{6,7},{7,4},{8,9},{9,10},{10,1... | collective-permute-start | bytes 405512 | tf_op jit(solution)/shard_map/ppermute | solution.py:399
  124.6 10.4 %collective-permute-start.11 = (f32[264,128]{1,0:T(8,128)}, f32[264,128]{1,0:T(8,128)S(1)}, u32[]{:S(2)}, u32[]{:S(2)}) collective-permute-start(f32[264,128]{1,0:T(8,128)} %get-tuple-element.47.s0_ref), channel_id=1, source_target_pairs={{0,2},{1,3},{2,0},{3,1},{4,6},{5,7},{6,4},{7,5},{8,10},{9,11},{10,... | collective-permute-start | bytes 405512 | tf_op jit(solution)/shard_map/ppermute | solution.py:399
  128.0 7.0 %collective-permute-start.12 = (f32[264,128]{1,0:T(8,128)}, f32[264,128]{1,0:T(8,128)S(1)}, u32[]{:S(2)}, u32[]{:S(2)}) collective-permute-start(f32[264,128]{1,0:T(8,128)} %get-tuple-element.47.s0_ref), channel_id=1, source_target_pairs={{0,3},{1,0},{2,1},{3,2},{4,7},{5,4},{6,5},{7,6},{8,11},{9,8},{10,9... | collective-permute-start | bytes 405512 | tf_op jit(solution)/shard_map/ppermute | solution.py:399
  131.2 3.8 %copy-start.11 = (f32[264,128]{1,0:T(8,128)}, f32[264,128]{1,0:T(8,128)S(1)}, u32[]{:S(2)}) copy-start(f32[264,128]{1,0:T(8,128)S(1)} %collective-permute-done.10.s1_ref) | copy-start | bytes 405508
  135.0 0.7 copy-start.13
  135.0 0.7 copy-start.15
  135.7 10.6 %copy-start.5 = (bf16[16,4,64,128]{3,2,1,0:T(8,128)(2,1)S(1)}, bf16[16,4,64,128]{3,2,1,0:T(8,128)(2,1)}, u32[]{:S(2)}) copy-start(bf16[16,4,64,128]{3,2,1,0:T(8,128)(2,1)} %get-tuple-element.60) | copy-start | bytes 3145732
  146.2 11.3 %collective-permute-start.13 = (bf16[16,4,96,128]{3,2,1,0:T(8,128)(2,1)}, bf16[16,4,96,128]{3,2,1,0:T(8,128)(2,1)}, u32[]{:S(2)}, u32[]{:S(2)}) collective-permute-start(bf16[16,4,96,128]{3,2,1,0:T(8,128)(2,1)} %get-tuple-element.59), channel_id=1, source_target_pairs={{0,4},{4,0},{8,12},{12,8},{16,20},{20,16},{24,28},{28,24},{32,36},... | collective-permute-start | bytes 4718600 | tf_op jit(solution)/shard_map/ppermute | solution.py:408
  147.8 9.7 %copy-start.4 = (bf16[16,4,96,128]{3,2,1,0:T(8,128)(2,1)S(1)}, bf16[16,4,96,128]{3,2,1,0:T(8,128)(2,1)}, u32[]{:S(2)}) copy-start(bf16[16,4,96,128]{3,2,1,0:T(8,128)(2,1)} %get-tuple-element.58) | copy-start | bytes 4718596
  147.8 26.7 %all-to-all-start.3 = ((bf16[64,64,128]{2,1,0:T(8,128)(2,1)}), bf16[64,64,128]{2,1,0:T(8,128)(2,1)S(1)}, u32[]{:S(2)}, u32[]{:S(2)}) async-start(bf16[64,64,128]{2,1,0:T(8,128)(2,1)} %bitcast.13), calls=%async_computation.3 | async-start | bytes 2097152 | tf_op jit(solution)/shard_map/all_to_all | solution.py:414
  160.5 21.1 %copy-start.24 = (f32[8,128]{1,0:T(8,128)S(1)}, f32[8,128]{1,0:T(8,128)}, u32[]{:S(2)}) copy-start(f32[8,128]{1,0:T(8,128)} %get-tuple-element.62) | copy-start | bytes 12292
  174.4 28.2 %all-to-all-start.2 = ((bf16[64,96,128]{2,1,0:T(8,128)(2,1)}), bf16[64,96,128]{2,1,0:T(8,128)(2,1)S(1)}, u32[]{:S(2)}, u32[]{:S(2)}) async-start(bf16[64,96,128]{2,1,0:T(8,128)(2,1)} %bitcast.12), calls=%async_computation.2 | async-start | bytes 3145728 | tf_op jit(solution)/shard_map/all_to_all | solution.py:414
  204.0 17.3 %all-to-all-start.4 = ((bf16[32,80,128]{2,1,0:T(8,128)(2,1)}), bf16[32,80,128]{2,1,0:T(8,128)(2,1)S(1)}, u32[]{:S(2)}, u32[]{:S(2)}) async-start(bf16[32,80,128]{2,1,0:T(8,128)(2,1)} %broadcast_in_dim.10), calls=%async_computation.4 | async-start | bytes 1310720 | tf_op jit(solution)/shard_map/all_to_all | solution.py:404
  210.6 10.7 %copy-start.10 = (f32[96,128]{1,0:T(8,128)}, f32[96,128]{1,0:T(8,128)S(1)}, u32[]{:S(2)}) copy-start(f32[96,128]{1,0:T(8,128)S(1)} %pad_maximum_fusion.1.r0_ref) | copy-start | bytes 147460
  210.6 5.9 %collective-permute-start.15 = (f32[96,128]{1,0:T(8,128)S(1)}, f32[96,128]{1,0:T(8,128)S(1)}, u32[]{:S(2)}, u32[]{:S(2)}) collective-permute-start(f32[96,128]{1,0:T(8,128)S(1)} %pad_maximum_fusion.1.r0_ref), channel_id=1, source_target_pairs={{0,1},{1,2},{2,3},{3,0},{4,5},{5,6},{6,7},{7,4},{8,9},{9,10},{10,1... | collective-permute-start | bytes 147464 | tf_op jit(solution)/shard_map/ppermute | solution.py:399
  211.5 5.6 %collective-permute-start.16 = (f32[96,128]{1,0:T(8,128)S(1)}, f32[96,128]{1,0:T(8,128)S(1)}, u32[]{:S(2)}, u32[]{:S(2)}) collective-permute-start(f32[96,128]{1,0:T(8,128)S(1)} %pad_maximum_fusion.1.r0_ref), channel_id=1, source_target_pairs={{0,2},{1,3},{2,0},{3,1},{4,6},{5,7},{6,4},{7,5},{8,10},{9,11},{10,... | collective-permute-start | bytes 147464 | tf_op jit(solution)/shard_map/ppermute | solution.py:399
  213.1 4.2 %collective-permute-start.17 = (f32[96,128]{1,0:T(8,128)S(1)}, f32[96,128]{1,0:T(8,128)S(1)}, u32[]{:S(2)}, u32[]{:S(2)}) collective-permute-start(f32[96,128]{1,0:T(8,128)S(1)} %pad_maximum_fusion.1.r0_ref), channel_id=1, source_target_pairs={{0,3},{1,0},{2,1},{3,2},{4,7},{5,4},{6,5},{7,6},{8,11},{9,8},{10,9... | collective-permute-start | bytes 147464 | tf_op jit(solution)/shard_map/ppermute | solution.py:399
  216.5 4.8 %copy-start.19 = (f32[96,128]{1,0:T(8,128)}, f32[96,128]{1,0:T(8,128)S(1)}, u32[]{:S(2)}) copy-start(f32[96,128]{1,0:T(8,128)S(1)} %collective-permute-done.15.r1_ref) | copy-start | bytes 147460
  217.1 4.2 %copy-start.20 = (f32[96,128]{1,0:T(8,128)}, f32[96,128]{1,0:T(8,128)S(1)}, u32[]{:S(2)}) copy-start(f32[96,128]{1,0:T(8,128)S(1)} %collective-permute-done.16.r2_ref) | copy-start | bytes 147460
  217.4 3.9 %copy-start.21 = (f32[96,128]{1,0:T(8,128)}, f32[96,128]{1,0:T(8,128)S(1)}, u32[]{:S(2)}) copy-start(f32[96,128]{1,0:T(8,128)S(1)} %collective-permute-done.17.r3_ref) | copy-start | bytes 147460
  221.3 0.9 copy-start.2

commit v2 on v1

--- a/solution.py
+++ b/solution.py
@@ -12,6 +12,7 @@
 F32 = jnp.float32
 BF16 = jnp.bfloat16
 CHUNK = 256
+UNROLL = 2
 
 
 def iota(shape, dim):
@@ -56,7 +57,7 @@
     pair_ref[...] = jnp.where(col == 8 * (row & 63) + (row >> 6), 1.0, 0.0).astype(BF16)
 
 
-def cut_patches(load, pick_ref, out_ref, once_ref, pair_ref, turn_ref, whole_ref, rest_ref):
+def cut_patches(load, pick_ref, slot_ref, out_ref, once_ref, pair_ref, turn_ref, whole_ref, rest_ref):
     row, col = iota((128, 256), 0), iota((128, 256), 1)
     turn_pair = jnp.where(col == (row & 31) * 8 + 2 * (row >> 5), 1.0, 0.0).astype(BF16)
 
@@ -77,18 +78,15 @@
                 rest_ref[at, x * 128 : (x + 1) * 128] = rest[x * 32 : (x + 1) * 32, lanes]
         return carry
 
-    lax.fori_loop(0, 8, strips, 0)
-
-    def place(i, carry):
-        at = pl.ds(pl.multiple_of(i * CHUNK, CHUNK), CHUNK)
-        pick = pick_ref[at, :]
-        picked = dot(pick, whole_ref[...]).astype(BF16)
-        out_ref[at, 0:1024] = dot(picked, once_ref[...]).astype(BF16)
-        picked = dot(pick, rest_ref[...]).astype(BF16)
-        out_ref[at, 1024:1536] = dot(picked, pair_ref[...]).astype(BF16)
-        return carry
-
-    lax.fori_loop(0, 512 // CHUNK, place, 0)
+    lax.fori_loop(0, 8, strips, 0, unroll=UNROLL)
+
+    for part_ref, turn_back_ref, lanes in (
+        (whole_ref, once_ref, slice(0, 1024)),
+        (rest_ref, pair_ref, slice(1024, 1536)),
+    ):
+        picked = dot(pick_ref[...], part_ref[...]).astype(BF16)
+        picked = dot(picked, turn_back_ref[...]).astype(BF16)
+        out_ref[:, lanes] = dot(slot_ref[...], picked).astype(BF16)
 
 
 CUT_SCRATCH = [
@@ -100,21 +98,23 @@
 ]
 
 
-def old_kernel(field_hbm, anchor_ref, dest_ref, out_ref, pick_ref, field_ref, sem, *scratch):
+def old_kernel(field_hbm, anchor_ref, dest_ref, out_ref, pick_ref, slot_ref, field_ref, sem, *scratch):
     fetch = pltpu.make_async_copy(field_hbm, field_ref, sem)
     fetch.start()
     selections(*scratch[:3])
     target = dest_ref[...].astype(F32)
-    wide = jnp.broadcast_to(target, (256, 256))
     row, col = iota((256, 256), 0), iota((256, 256), 1)
-    tall = jnp.sum(jnp.where(row == col, wide, 0.0), axis=1, keepdims=True)
-    ahead = jnp.where((tall == wide) & (row < col), 1.0, 0.0)
+
+    def upright(line):
+        return jnp.sum(jnp.where(row == col, jnp.broadcast_to(line, (256, 256)), 0.0), axis=1, keepdims=True)
+
+    ahead = jnp.where((upright(target) == target) & (row < col), 1.0, 0.0)
     slot = target * 16.0 + jnp.sum(ahead, axis=0, keepdims=True)
     patch = ((anchor_ref[1] >> 3) & 15) * 32 + ((anchor_ref[2] >> 3) & 31)
-    row = iota((512, 256), 0)
-    sent = jnp.where(row == slot.astype(jnp.int32), 1.0, 0.0)
-    taken = jnp.where(row == patch, 1.0, 0.0).astype(BF16)
-    pick_ref[...] = dot(sent.astype(BF16), taken, (1, 1)).astype(BF16)
+    patch = upright(patch.astype(F32)).astype(jnp.int32)
+    pick_ref[...] = jnp.where(iota((256, 512), 1) == patch, 1.0, 0.0).astype(BF16)
+    sent = jnp.where(iota((512, 256), 0) == slot.astype(jnp.int32), 1.0, 0.0)
+    slot_ref[...] = sent.astype(BF16)
     tag = jnp.sum(sent, axis=1, keepdims=True)
     out_ref[:, 1536:1664] = jnp.broadcast_to(tag, (512, 128)).astype(BF16)
     fetch.wait()
@@ -123,11 +123,11 @@
         at = pl.ds(pl.multiple_of(by * 8, 8), 8)
         return field_ref[:, :, at, :].reshape(192, 256)
 
-    cut_patches(load, pick_ref, out_ref, *scratch)
+    cut_patches(load, pick_ref, slot_ref, out_ref, *scratch)
 
 
 def new_kernel(
-    field_hbm, z_prev_ref, z_next_ref, y_prev_ref, y_next_ref, pick_ref,
+    field_hbm, z_prev_ref, z_next_ref, y_prev_ref, y_next_ref, pick_ref, slot_ref,
     new_hbm, out_ref, pad_ref, new_ref, sem, *scratch,
 ):
     fetch = pltpu.make_async_copy(field_hbm, pad_ref.at[:, 1:9, 8:136, :], sem.at[0])
@@ -170,7 +170,7 @@
         at = pl.ds(pl.multiple_of(by * 8, 8), 8)
         return new_ref[:, :, at, :].reshape(192, 256)
 
-    cut_patches(load, pick_ref, out_ref, *scratch)
+    cut_patches(load, pick_ref, slot_ref, out_ref, *scratch)
     store.wait()
 
 
@@ -247,9 +247,9 @@
 
 
 def middle_kernel(
-    place_ref, s0_ref, s1_ref, s2_ref, s3_ref, lifted_ref, query_ref, new_ref, out_w_ref, proj_w_ref,
-    mine_ref, theirs_ref, d_query_ref, d_hidden_ref, sums_ref, count_ref,
-    hidden_ref, d_guess_ref, attended_ref, d_tokens_ref, acc_ref, high_ref, low_ref, loss_ref,
+    s0_ref, s1_ref, s2_ref, s3_ref, lifted_ref, query_ref, new_ref, out_w_ref, proj_w_ref,
+    hidden_ref, d_guess_ref, attended_ref, d_tokens_ref, d_query_ref, d_hidden_ref, sums_ref, count_ref,
+    acc_ref, high_ref, low_ref, loss_ref,
 ):
     total = (s0_ref[...] + s1_ref[...]) + (s2_ref[...] + s3_ref[...])
     count = total[256:264, :]
@@ -300,6 +300,9 @@
     sums_ref[128:256, :] = pack((acc_ref[2], acc_ref[3]))
     loss = jnp.sum(loss_ref[...], axis=(0, 1), keepdims=True) * (1.0 / 50331648)
     sums_ref[256:264, :] = jnp.broadcast_to(loss, (8, 128))
+
+
+def product_kernel(place_ref, hidden_ref, d_guess_ref, attended_ref, d_tokens_ref, mine_ref, theirs_ref):
     deal = dealer(place_ref, mine_ref, theirs_ref)
     grad = dot(hidden_ref[...], d_guess_ref[...], (0, 0))
     for n in range(4):
@@ -363,6 +366,24 @@
         deal(grad[:, n * 128 : (n + 1) * 128], 48, n, 0)
 
 
+def merge_kernel(in_ref, in_got_ref, out_ref, out_got_ref, send_ref):
+    send_ref[:, 0:96, :] = (in_ref[...].astype(F32) + in_got_ref[...].astype(F32)).astype(BF16)
+    send_ref[:, 96:160, :] = (out_ref[...].astype(F32) + out_got_ref[...].astype(F32)).astype(BF16)
+
+
+def merge(*parts):
+    def block(rows):
+        return pl.BlockSpec((16, rows, 128), lambda i: (i, 0, 0))
+
+    return pl.pallas_call(
+        merge_kernel,
+        grid=(4,),
+        out_shape=jax.ShapeDtypeStruct((64, 160, 128), BF16),
+        in_specs=[block(96), block(96), block(64), block(64)],
+        out_specs=block(160),
+    )(*[part.reshape(64, -1, 128) for part in parts])
+
+
 def last_kernel(
     place_ref, r0_ref, r1_ref, r2_ref, r3_ref, heads_ref,
     lift_ref, query_ref, key_ref, value_ref, out_ref, proj_ref, loss_ref,
@@ -404,20 +425,14 @@
     return lax.all_to_all(value, axes, split_axis=0, concat_axis=0, tiled=True)
 
 
-def pair_sum(mine, theirs):
-    got = lax.ppermute(theirs, "slab", [(i, i ^ 1) for i in range(32)])
-    return (mine.astype(F32) + got.astype(F32)).astype(BF16)
+def swap(theirs):
+    return lax.ppermute(theirs, "slab", [(i, i ^ 1) for i in range(32)])
 
 
 def total(partial):
     groups = [[(2 * q + c) * 4 + n for q in range(16) for n in range(4)] for c in range(2)]
     got = lax.all_to_all(
-        partial.reshape(64, -1, 128),
-        ("slab", "mp"),
-        split_axis=0,
-        concat_axis=0,
-        axis_index_groups=groups,
-        tiled=True,
+        partial, ("slab", "mp"), split_axis=0, concat_axis=0, axis_index_groups=groups, tiled=True
     )
     return jnp.sum(got.astype(F32), axis=0)
 
@@ -434,9 +449,9 @@
     tall = jnp.concatenate([w_out[:, k * 128 : (k + 1) * 128] for k in range(4)], axis=0)
     heads_w = around(jnp.stack([w_query, w_key, w_value, tall]))
 
-    send_old, pick = call(
+    send_old, pick, slot = call(
         old_kernel,
-        [((512, 1664), BF16), ((512, 512), BF16)],
+        [((512, 1664), BF16), ((256, 512), BF16), ((512, 256), BF16)],
         [pltpu.VMEM((3, 8, 128, 256), F32), pltpu.SemaphoreType.DMA] + CUT_SCRATCH,
         "hvv",
     )(velocity, anchors.reshape(3, 1, 256), dest.reshape(1, 256))
@@ -450,9 +465,9 @@
             pltpu.SemaphoreType.DMA((2,)),
         ]
         + CUT_SCRATCH,
-        "hvvvvv",
+        "hvvvvvv",
         "hv",
-    )(velocity, z_prev, z_next, y_prev, y_next, pick)
+    )(velocity, z_prev, z_next, y_prev, y_next, pick, slot)
     new = exchange(send_new, "slab")
 
     wide, wide_f = ((512, 512), BF16), ((512, 512), F32)
@@ -463,23 +478,22 @@
         "svvvvvv",
     )(place, old, w_lift, *heads_w)
     sums = around(sums)
-    mine, theirs, d_query, d_hidden, d_sums, count = call(
+    hidden, d_guess, attended, d_tokens, d_query, d_hidden, d_sums, count = call(
         middle_kernel,
-        [((16, 4, 64, 128), BF16), ((16, 4, 64, 128), BF16), wide, wide_f, ((264, 128), F32), ((8, 128), F32)],
+        [wide, ((512, 1536), BF16), wide, wide, wide, wide_f, ((264, 128), F32), ((8, 128), F32)],
         [
-            pltpu.VMEM((512, 512), BF16),
-            pltpu.VMEM((512, 1536), BF16),
-            pltpu.VMEM((512, 512), BF16),
-            pltpu.VMEM((512, 512), BF16),
             pltpu.VMEM((4, 128, 128), F32),
             pltpu.VMEM((4, 128, 128), BF16),
             pltpu.VMEM((4, 128, 128), BF16),
             pltpu.VMEM((8, 1536), F32),
         ],
-        "svvvvvvvvv",
-    )(place, *sums, lifted, query, new, wo, w_proj)
+        "vvvvvvvvv",
+    )(*sums, lifted, query, new, wo, w_proj)
     d_sums = around(d_sums)
-    total_out = total(pair_sum(mine, theirs))
+    mine_out, theirs_out = call(
+        product_kernel, [((16, 4, 64, 128), BF16), ((16, 4, 64, 128), BF16)], (), "svvvv"
+    )(place, hidden, d_guess, attended, d_tokens)
+    got_out = swap(theirs_out)
     mine, theirs, loss_part = call(
         backward_kernel,
         [((16, 4, 96, 128), BF16), ((16, 4, 96, 128), BF16), ((8, 128), F32)],
@@ -493,11 +507,13 @@
         ],
         "svvvvvhvvvvvvvvvv",
     )(place, *d_sums, count, old, lifted, key, key_spread, value, value_spread, d_query, d_hidden, wq, wk, wv)
-    total_in = total(pair_sum(mine, theirs))
-    blocks = jnp.concatenate([total_in[0:48], total_out[0:48]], axis=0)
+    got = swap(theirs)
+    partial = merge(mine, got, mine_out, got_out)
+    sums = total(partial)
+    blocks = jnp.concatenate([sums[0:48], sums[96:144]], axis=0)
     loss_high = loss_part.astype(BF16)
     loss_low = (loss_part - loss_high.astype(F32)).astype(BF16)
-    heads = jnp.concatenate([total_in[48:96], total_out[48:64]], axis=0).astype(BF16)
+    heads = jnp.concatenate([sums[48:96], sums[144:160]], axis=0).astype(BF16)
     heads = jnp.concatenate([heads, loss_high[0:1], loss_low[0:1], jnp.zeros((14, 128), BF16)], axis=0)
     heads = exchange(jnp.broadcast_to(heads[None], (32, 80, 128)), "slab")
     lift, g_query, g_key, g_value, g_out, proj, loss = call(

time: 229 us -> 223 us (0.974)
  starting transfers between devices: 63.1 us -> 57.8 us
  other arithmetic: 6.5 us -> 2.1 us
  Pallas kernels: 52.9 us -> 57 us
    all_to_all x2 -> x1, starting transfers between devices: 16.8 us -> 9.54 us  [total(): lax.all_to_all(partial, ('slab', 'mp'), split_axis=0, concat_axis=0, axis...]
    pallas_call x2 -> x4, Pallas kernels: 18.5 us -> 24.4 us  [the longest x1 8.13 us: step(): call(middle_kernel, [wide, ((512, 1536), BF16), wide, wide, wide, wide_f,...]
    convert_element_type x2 -> x0, other arithmetic: 4.45 us -> none  [pair_sum(): return (mine.astype(F32) + got.astype(F32)).astype(BF16)]
    ppermute x2, waiting for transfers between devices: 0.01 us -> 2.5 us  [swap(): return lax.ppermute(theirs, 'slab', [(i, i ^ 1) for i in range(32)])]
    all_to_all x2 -> x1, waiting for transfers between devices: 34.8 us -> 33.2 us  [total(): lax.all_to_all(partial, ('slab', 'mp'), split_axis=0, concat_axis=0, axis...]
  transfers between devices with their start and end apart: 23 -> 22, of which waited for: 15 -> 15; matrix products, arithmetic and copies ran while one was open for 4% -> 2% of each run, Pallas kernels for 14% -> 11%
where the time goes in v2:
time: 223 us; the launch traced here: 219 us
  waiting for transfers between devices  92.2 us (41%)
  starting transfers between devices  57.8 us (26%)
  Pallas kernels  57 us (26%)
  local copies, waits for them, and re-layouts  9.32 us (4%)
    ppermute x12, waiting for transfers between devices, around(): got.append(lax.ppermute(value, 'mp', [(i, (i + d) % 4) for i in range(4)]))  35.3 us
    all_to_all x1, waiting for transfers between devices, total(): lax.all_to_all(partial, ('slab', 'mp'), split_axis=0, concat_axis=0, axis...  33.2 us
    all_to_all x3, starting transfers between devices, exchange(): return lax.all_to_all(value, axes, split_axis=0, concat_axis=0, tiled=True)  22.6 us
    ppermute x12, starting transfers between devices, around(): got.append(lax.ppermute(value, 'mp', [(i, (i + d) % 4) for i in range(4)]))  19.1 us
    ppermute x1, waiting for transfers between devices, step(): z_prev = lax.ppermute(velocity[:, 7:8], 'slab', up)  15.6 us
    pallas_call x1, Pallas kernels, step(): call(new_kernel, [((3, 8, 128, 256), F32), ((512, 1536), BF16)], [pltpu.V...  10.5 us
    pallas_call x1, Pallas kernels, step(): call(backward_kernel, [((16, 4, 96, 128), BF16), ((16, 4, 96, 128), BF16)...  10.4 us
    all_to_all x1, starting transfers between devices, total(): lax.all_to_all(partial, ('slab', 'mp'), split_axis=0, concat_axis=0, axis...  9.54 us
  transfers between devices with their start and end apart: 22, of which 15 were waited for; matrix products, arithmetic and copies ran while one was open for 2% of the time, Pallas kernels for 11%

profile of v2, /device:TPU:6, one launch (start us, length us, event | category | flops | bytes accessed | tf_op | source)
XLA Modules:
  0.0 219.4 jit_solution(17313588315401154071)
XLA Ops:
  0.6 7.1 %shard_map.152 = (bf16[512,1664]{1,0:T(8,128)(2,1)}, bf16[256,512]{1,0:T(8,128)(2,1)}, bf16[512,256]{1,0:T(8,128)(2,1)}) custom-call(f32[3,8,128,256]{3,2,1,0:T(8,128)} %field_hbm.3, s32[3,1,256]{2,1,0:T(1,128)} %bitcast.30, s32[1,256]{1,0:T(1,128)} %bitcast.31), custom_call_target="tpu_custom_call" | custom-call | tf_op jit(solution)/shard_map/pallas_call | solution.py:452
  7.7 7.6 %all-to-all-start = ((bf16[32,16,1664]{2,1,0:T(8,128)(2,1)}), bf16[32,16,1664]{2,1,0:T(8,128)(2,1)S(1)}, u32[]{:S(2)}, u32[]{:S(2)}) async-start(bf16[32,16,1664]{2,1,0:T(8,128)(2,1)} %bitcast.21), calls=%async_computation | async-start | bytes 3407872 | tf_op jit(solution)/shard_map/all_to_all | solution.py:425
  15.3 1.2 fusion.1
  16.5 0.2 collective-permute-start
  16.7 1.6 collective-permute-start.1
  18.3 1.1 fusion
  19.4 2.0 collective-permute-start.2
  21.4 2.2 collective-permute-start.3
  23.5 1.7 collective-permute-done.2.y_prev_ref
  25.3 15.6 %collective-permute-done.z_prev_ref = f32[3,1,128,256]{3,2,1,0:T(8,128)S(1)} collective-permute-done((f32[3,1,128,256]{3,2,1,0:T(8,128)S(1)}, f32[3,1,128,256]{3,2,1,0:T(8,128)S(1)}, u32[]{:S(2)}, u32[]{:S(2)}) %collective-permute-start) | collective-permute-done | bytes 393248 | tf_op jit(solution)/shard_map/ppermute | solution.py:444
  40.9 0.7 copy-done.8
  41.6 0.1 copy-done.9
  41.8 10.5 %shard_map.153 = (f32[3,8,128,256]{3,2,1,0:T(8,128)}, bf16[512,1536]{1,0:T(8,128)(2,1)}) custom-call(f32[3,8,128,256]{3,2,1,0:T(8,128)} %field_hbm.3, f32[3,1,128,256]{3,2,1,0:T(8,128)} %copy-done.8, f32[3,1,128,256]{3,2,1,0:T(8,128)} %copy-done.9, f32[3,8,1,256]{3,2,1,0:T(1,128)} %copy-done.22, f32[3,8,1,256]{3,2,1,0:T(1,128)} %copy-done.23, ...), custom_call_target="tpu_custom_call" | custom-call | tf_op jit(solution)/shard_map/pallas_call | solution.py:459
  52.3 0.0 copy-start.17
  52.3 7.3 %all-to-all-start.1 = ((bf16[32,16,1536]{2,1,0:T(8,128)(2,1)}), bf16[32,16,1536]{2,1,0:T(8,128)(2,1)S(1)}, u32[]{:S(2)}, u32[]{:S(2)}) async-start(bf16[32,16,1536]{2,1,0:T(8,128)(2,1)} %bitcast.22), calls=%async_computation.1 | async-start | bytes 3145728 | tf_op jit(solution)/shard_map/all_to_all | solution.py:425
  59.7 1.0 pad_maximum_fusion.w0_ref
  60.7 2.0 collective-permute-start.4
  62.7 3.6 %collective-permute-start.5 = (bf16[4,512,128]{2,1,0:T(8,128)(2,1)S(1)}, bf16[4,512,128]{2,1,0:T(8,128)(2,1)S(1)}, u32[]{:S(2)}, u32[]{:S(2)}) collective-permute-start(bf16[4,512,128]{2,1,0:T(8,128)(2,1)S(1)} %pad_maximum_fusion.w0_ref), channel_id=1, source_target_pairs={{0,2},{1,3},{2,0},{3,1},{4,6},{5,7},{6,4},{7,5},{8,10},{9,11},{10,... | collective-permute-start | bytes 1572872 | tf_op jit(solution)/shard_map/ppermute | solution.py:420
  66.3 1.0 collective-permute-start.6
  67.3 0.7 pad_add_fusion.place_ref
  68.0 9.1 %collective-permute-done.4.w1_ref = bf16[4,512,128]{2,1,0:T(8,128)(2,1)S(1)} collective-permute-done((bf16[4,512,128]{2,1,0:T(8,128)(2,1)S(1)}, bf16[4,512,128]{2,1,0:T(8,128)(2,1)S(1)}, u32[]{:S(2)}, u32[]{:S(2)}) %collective-permute-start.4) | collective-permute-done | bytes 524320 | tf_op jit(solution)/shard_map/ppermute | solution.py:420
  77.0 12.4 %collective-permute-done.5.w2_ref = bf16[4,512,128]{2,1,0:T(8,128)(2,1)S(1)} collective-permute-done((bf16[4,512,128]{2,1,0:T(8,128)(2,1)S(1)}, bf16[4,512,128]{2,1,0:T(8,128)(2,1)S(1)}, u32[]{:S(2)}, u32[]{:S(2)}) %collective-permute-start.5) | collective-permute-done | bytes 524320 | tf_op jit(solution)/shard_map/ppermute | solution.py:420
  89.5 0.8 copy-done.7
  90.2 9.5 %shard_map.154 = (bf16[512,512]{1,0:T(8,128)(2,1)}, bf16[512,512]{1,0:T(8,128)(2,1)}, bf16[512,512]{1,0:T(8,128)(2,1)}, f32[512,512]{1,0:T(8,128)}, bf16[512,512...) custom-call(s32[2]{0:T(128)} %pad_add_fusion.place_ref, ...), custom_call_target="tpu_custom_call" | custom-call | tf_op jit(solution)/shard_map/pallas_call | solution.py:474
  99.7 0.6 collective-permute-start.7
  100.3 2.4 %collective-permute-start.8 = (f32[264,128]{1,0:T(8,128)}, f32[264,128]{1,0:T(8,128)S(1)}, u32[]{:S(2)}, u32[]{:S(2)}) collective-permute-start(f32[264,128]{1,0:T(8,128)} %get-tuple-element.48.s0_ref), channel_id=1, source_target_pairs={{0,2},{1,3},{2,0},{3,1},{4,6},{5,7},{6,4},{7,5},{8,10},{9,11},{10,... | collective-permute-start | bytes 405512 | tf_op jit(solution)/shard_map/ppermute | solution.py:420
  102.7 1.2 collective-permute-start.9
  104.0 3.0 %collective-permute-done.7.s1_ref = f32[264,128]{1,0:T(8,128)S(1)} collective-permute-done((f32[264,128]{1,0:T(8,128)}, f32[264,128]{1,0:T(8,128)S(1)}, u32[]{:S(2)}, u32[]{:S(2)}) %collective-permute-start.7) | collective-permute-done | bytes 135200 | tf_op jit(solution)/shard_map/ppermute | solution.py:420
  107.0 2.3 %collective-permute-done.8.s2_ref = f32[264,128]{1,0:T(8,128)S(1)} collective-permute-done((f32[264,128]{1,0:T(8,128)}, f32[264,128]{1,0:T(8,128)S(1)}, u32[]{:S(2)}, u32[]{:S(2)}) %collective-permute-start.8) | collective-permute-done | bytes 135200 | tf_op jit(solution)/shard_map/ppermute | solution.py:420
  109.3 0.1 collective-permute-done.9.s3_ref
  109.4 0.5 copy-done.12
  110.0 0.1 copy-done.13
  110.1 0.5 copy-done.1
  110.6 8.1 %shard_map.155 = (bf16[512,512]{1,0:T(8,128)(2,1)}, bf16[512,1536]{1,0:T(8,128)(2,1)}, bf16[512,512]{1,0:T(8,128)(2,1)}, bf16[512,512]{1,0:T(8,128)(2,1)}, bf16[...) custom-call(f32[264,128]{1,0:T(8,128)} %get-tuple-element.48.s0_ref, ...), custom_call_target="tpu_custom_call" | custom-call | tf_op jit(solution)/shard_map/pallas_call | solution.py:481
  118.7 0.8 collective-permute-start.10
  119.5 3.4 %collective-permute-start.11 = (f32[264,128]{1,0:T(8,128)}, f32[264,128]{1,0:T(8,128)S(1)}, u32[]{:S(2)}, u32[]{:S(2)}) collective-permute-start(f32[264,128]{1,0:T(8,128)} %get-tuple-element.53.s0_ref), channel_id=1, source_target_pairs={{0,2},{1,3},{2,0},{3,1},{4,6},{5,7},{6,4},{7,5},{8,10},{9,11},{10,... | collective-permute-start | bytes 405512 | tf_op jit(solution)/shard_map/ppermute | solution.py:420
  122.9 3.4 %collective-permute-done.10.s1_ref = f32[264,128]{1,0:T(8,128)S(1)} collective-permute-done((f32[264,128]{1,0:T(8,128)}, f32[264,128]{1,0:T(8,128)S(1)}, u32[]{:S(2)}, u32[]{:S(2)}) %collective-permute-start.10) | collective-permute-done | bytes 135200 | tf_op jit(solution)/shard_map/ppermute | solution.py:420
  126.3 2.4 %collective-permute-done.11.s2_ref = f32[264,128]{1,0:T(8,128)S(1)} collective-permute-done((f32[264,128]{1,0:T(8,128)}, f32[264,128]{1,0:T(8,128)S(1)}, u32[]{:S(2)}, u32[]{:S(2)}) %collective-permute-start.11) | collective-permute-done | bytes 135200 | tf_op jit(solution)/shard_map/ppermute | solution.py:420
  128.7 0.0 collective-permute-done.12.s3_ref
  128.7 0.6 copy-done.15
  129.3 0.0 copy-done.16
  129.4 10.4 %shard_map.156 = (bf16[16,4,96,128]{3,2,1,0:T(8,128)(2,1)}, bf16[16,4,96,128]{3,2,1,0:T(8,128)(2,1)}, f32[8,128]{1,0:T(8,128)}) custom-call(s32[2]{0:T(128)} %pad_add_fusion.place_ref, f32[264,128]{1,0:T(8,128)} %get-tuple-element.53.s0_ref, f32[264,128]{1,0:T(8,128)} %copy-done.14, f32[264,128]{1,0:T(8,128)} %copy-done.15, f32[264,128]{1,0:T(8,128)} %copy-done.16, ...), custom_call_target="tpu_custom_call" | custom-call | tf_op jit(solution)/shard_map/pallas_call | solution.py:497
  139.8 0.1 collective-permute-start.13
  139.9 4.5 %shard_map.157 = (bf16[16,4,64,128]{3,2,1,0:T(8,128)(2,1)}, bf16[16,4,64,128]{3,2,1,0:T(8,128)(2,1)}) custom-call(s32[2]{0:T(128)} %pad_add_fusion.place_ref, bf16[512,512]{1,0:T(8,128)(2,1)} %get-tuple-element.66.hidden_ref, bf16[512,1536]{1,0:T(8,128)(2,1)} %get-tuple-element.67.d_guess_ref, bf16[512,512]{1,0:T(8,128)(2,1)} %get-tuple-element.68.attended_ref, ...), custom_call_target="tpu_custom_call" | custom-call | tf_op jit(solution)/shard_map/pallas_call | solution.py:493
  144.4 0.5 collective-permute-start.14
  144.9 2.5 %collective-permute-done.14 = bf16[16,4,64,128]{3,2,1,0:T(8,128)(2,1)S(1)} collective-permute-done((bf16[16,4,64,128]{3,2,1,0:T(8,128)(2,1)}, bf16[16,4,64,128]{3,2,1,0:T(8,128)(2,1)S(1)}, u32[]{:S(2)}, u32[]{:S(2)}) %collective-permute-start.14) | collective-permute-done | bytes 1048608 | tf_op jit(solution)/shard_map/ppermute | solution.py:429
  147.4 1.0 copy-done.5
  148.3 0.6 copy-done.4
  148.9 4.6 %shard_map.158 = bf16[64,160,128]{2,1,0:T(8,128)(2,1)} custom-call(bf16[64,96,128]{2,1,0:T(8,128)(2,1)} %bitcast.23, bf16[64,96,128]{2,1,0:T(8,128)(2,1)} %bitcast.24, bf16[64,64,128]{2,1,0:T(8,128)(2,1)} %bitcast.25, bf16[64,64,128]{2,1,0:T(8,128)(2,1)} %bitcast.26), custom_call_target="tpu_custom_call" | custom-call | tf_op jit(solution)/shard_map/pallas_call | solution.py:378
  153.5 9.5 %all-to-all-start.2 = ((bf16[64,160,128]{2,1,0:T(8,128)(2,1)}), bf16[64,160,128]{2,1,0:T(8,128)(2,1)S(1)}, u32[]{:S(2)}, u32[]{:S(2)}) async-start(bf16[64,160,128]{2,1,0:T(8,128)(2,1)} %shard_map.158), calls=%async_computation.2 | async-start | bytes 5242880 | tf_op jit(solution)/shard_map/all_to_all | solution.py:434
  163.1 33.2 %all-to-all-done.2 = bf16[64,160,128]{2,1,0:T(8,128)(2,1)S(1)} async-done(((bf16[64,160,128]{2,1,0:T(8,128)(2,1)}), bf16[64,160,128]{2,1,0:T(8,128)(2,1)S(1)}, u32[]{:S(2)}, u32[]{:S(2)}) %all-to-all-start.2) | async-done | bytes 2621472 | tf_op jit(solution)/shard_map/all_to_all | solution.py:434
  196.3 0.4 convert_reduce_fusion
  196.7 0.2 concatenate.14
  196.9 0.9 broadcast_in_dim.10
  197.8 7.7 %all-to-all-start.3 = ((bf16[32,80,128]{2,1,0:T(8,128)(2,1)}), bf16[32,80,128]{2,1,0:T(8,128)(2,1)S(1)}, u32[]{:S(2)}, u32[]{:S(2)}) async-start(bf16[32,80,128]{2,1,0:T(8,128)(2,1)} %broadcast_in_dim.10), calls=%async_computation.3 | async-start | bytes 1310720 | tf_op jit(solution)/shard_map/all_to_all | solution.py:425
  205.6 0.8 collective-permute-start.15
  206.4 1.7 collective-permute-start.16
  208.1 1.6 collective-permute-start.17
  209.8 1.6 collective-permute-done.15.r1_ref
  211.4 0.6 collective-permute-done.16.r2_ref
  212.0 0.4 collective-permute-done.17.r3_ref
  212.4 3.9 %all-to-all-done.3.heads_ref = bf16[32,80,128]{2,1,0:T(8,128)(2,1)S(1)} async-done(((bf16[32,80,128]{2,1,0:T(8,128)(2,1)}), bf16[32,80,128]{2,1,0:T(8,128)(2,1)S(1)}, u32[]{:S(2)}, u32[]{:S(2)}) %all-to-all-start.3) | async-done | bytes 655392 | tf_op jit(solution)/shard_map/all_to_all | solution.py:425
  216.2 0.8 copy-done.2
  217.1 2.3 %shard_map.159 = (f32[48,512]{1,0:T(8,128)}, f32[512,128]{1,0:T(8,128)}, f32[512,128]{1,0:T(8,128)}, f32[512,128]{1,0:T(8,128)}, f32[128,512]{1,0:T(8,128)}, /*index=5*/f32[16,1536]{1,0:T(8,128)}, f32[1,1]{1,0:T(1,128)}) custom-call(s32[2]{0:T(128)} %pad_add_fusion.place_ref, f32[96,128]{1,0:T(8,128)} %copy-done.10, f32[96,128]{1,0:T(8,128)} %copy-done.19, ...), custom_call_target="tpu_custom_call" | custom-call | tf_op jit(solution)/shard_map/pallas_call | solution.py:519
  (56 shorter events, 0.2 us)
Async XLA Ops:
  7.7 44.5 %all-to-all-start = ((bf16[32,16,1664]{2,1,0:T(8,128)(2,1)}), bf16[32,16,1664]{2,1,0:T(8,128)(2,1)S(1)}, u32[]{:S(2)}, u32[]{:S(2)}) async-start(bf16[32,16,1664]{2,1,0:T(8,128)(2,1)} %bitcast.21), calls=%async_computation | async-start | bytes 3407872 | tf_op jit(solution)/shard_map/all_to_all | solution.py:425
  16.5 24.4 %collective-permute-start = (f32[3,1,128,256]{3,2,1,0:T(8,128)S(1)}, f32[3,1,128,256]{3,2,1,0:T(8,128)S(1)}, u32[]{:S(2)}, u32[]{:S(2)}) collective-permute-start(f32[3,1,128,256]{3,2,1,0:T(8,128)S(1)} %get-tuple-element.85), channel_id=1, source_target_pairs={{0,4},{4,8},{8,12},{12,16},{16,20},{20,24},{24,28},{28,32},{32,36}... | collective-permute-start | bytes 1179656 | tf_op jit(solution)/shard_map/ppermute | solution.py:444
  16.7 24.2 %collective-permute-start.1 = (f32[3,1,128,256]{3,2,1,0:T(8,128)S(1)}, f32[3,1,128,256]{3,2,1,0:T(8,128)S(1)}, u32[]{:S(2)}, u32[]{:S(2)}) collective-permute-start(f32[3,1,128,256]{3,2,1,0:T(8,128)S(1)} %get-tuple-element.84), channel_id=1, source_target_pairs={{4,0},{8,4},{12,8},{16,12},{20,16},{24,20},{28,24},{32,28},{36,32}... | collective-permute-start | bytes 1179656 | tf_op jit(solution)/shard_map/ppermute | solution.py:445
  19.4 5.9 %collective-permute-start.2 = (f32[3,8,1,256]{3,2,1,0:T(1,128)S(1)}, f32[3,8,1,256]{3,2,1,0:T(1,128)S(1)}, u32[]{:S(2)}, u32[]{:S(2)}) collective-permute-start(f32[3,8,1,256]{3,2,1,0:T(1,128)S(1)} %get-tuple-element.83), channel_id=1, source_target_pairs={{0,1},{1,2},{2,3},{3,0},{4,5},{5,6},{6,7},{7,4},{8,9},{9,10},{10,1... | collective-permute-start | bytes 73736 | tf_op jit(solution)/shard_map/ppermute | solution.py:447
  21.4 3.9 %collective-permute-start.3 = (f32[3,8,1,256]{3,2,1,0:T(1,128)S(1)}, f32[3,8,1,256]{3,2,1,0:T(1,128)S(1)}, u32[]{:S(2)}, u32[]{:S(2)}) collective-permute-start(f32[3,8,1,256]{3,2,1,0:T(1,128)S(1)} %get-tuple-element.82), channel_id=1, source_target_pairs={{1,0},{2,1},{3,2},{0,3},{5,4},{6,5},{7,6},{4,7},{9,8},{10,9},{11,1... | collective-permute-start | bytes 73736 | tf_op jit(solution)/shard_map/ppermute | solution.py:448
  25.3 15.6 %copy-start.22 = (f32[3,8,1,256]{3,2,1,0:T(1,128)}, f32[3,8,1,256]{3,2,1,0:T(1,128)S(1)}, u32[]{:S(2)}) copy-start(f32[3,8,1,256]{3,2,1,0:T(1,128)S(1)} %collective-permute-done.2.y_prev_ref) | copy-start | bytes 73732
  25.3 15.6 %copy-start.23 = (f32[3,8,1,256]{3,2,1,0:T(1,128)}, f32[3,8,1,256]{3,2,1,0:T(1,128)S(1)}, u32[]{:S(2)}) copy-start(f32[3,8,1,256]{3,2,1,0:T(1,128)S(1)} %collective-permute-done.3.y_next_ref) | copy-start | bytes 73732
  40.9 0.7 copy-start.8
  40.9 0.9 copy-start.9
  52.3 7.3 %copy-start.17 = (bf16[128,512]{1,0:T(8,128)(2,1)S(1)}, bf16[128,512]{1,0:T(8,128)(2,1)}, u32[]{:S(2)}) copy-start(bf16[128,512]{1,0:T(8,128)(2,1)} %param.16) | copy-start | bytes 393220
  52.3 7.3 %copy-start = (bf16[32,16,1664]{2,1,0:T(8,128)(2,1)}, bf16[32,16,1664]{2,1,0:T(8,128)(2,1)S(1)}, u32[]{:S(2)}) copy-start(bf16[32,16,1664]{2,1,0:T(8,128)(2,1)S(1)} %all-to-all-done) | copy-start | bytes 5111812
  52.3 7.4 %copy-start.18 = (bf16[512,128]{1,0:T(8,128)(2,1)S(1)}, bf16[512,128]{1,0:T(8,128)(2,1)}, u32[]{:S(2)}) copy-start(bf16[512,128]{1,0:T(8,128)(2,1)} %param.15) | copy-start | bytes 393220
  52.3 57.1 %all-to-all-start.1 = ((bf16[32,16,1536]{2,1,0:T(8,128)(2,1)}), bf16[32,16,1536]{2,1,0:T(8,128)(2,1)S(1)}, u32[]{:S(2)}, u32[]{:S(2)}) async-start(bf16[32,16,1536]{2,1,0:T(8,128)(2,1)} %bitcast.22), calls=%async_computation.1 | async-start | bytes 3145728 | tf_op jit(solution)/shard_map/all_to_all | solution.py:425
  60.7 28.7 %copy-start.3 = (bf16[4,512,128]{2,1,0:T(8,128)(2,1)}, bf16[4,512,128]{2,1,0:T(8,128)(2,1)S(1)}, u32[]{:S(2)}) copy-start(bf16[4,512,128]{2,1,0:T(8,128)(2,1)S(1)} %pad_maximum_fusion.w0_ref) | copy-start | bytes 1572868
  60.7 16.3 %collective-permute-start.4 = (bf16[4,512,128]{2,1,0:T(8,128)(2,1)S(1)}, bf16[4,512,128]{2,1,0:T(8,128)(2,1)S(1)}, u32[]{:S(2)}, u32[]{:S(2)}) collective-permute-start(bf16[4,512,128]{2,1,0:T(8,128)(2,1)S(1)} %pad_maximum_fusion.w0_ref), channel_id=1, source_target_pairs={{0,1},{1,2},{2,3},{3,0},{4,5},{5,6},{6,7},{7,4},{8,9},{9,10},{10,1... | collective-permute-start | bytes 1572872 | tf_op jit(solution)/shard_map/ppermute | solution.py:420
  62.7 26.7 %collective-permute-start.5 = (bf16[4,512,128]{2,1,0:T(8,128)(2,1)S(1)}, bf16[4,512,128]{2,1,0:T(8,128)(2,1)S(1)}, u32[]{:S(2)}, u32[]{:S(2)}) collective-permute-start(bf16[4,512,128]{2,1,0:T(8,128)(2,1)S(1)} %pad_maximum_fusion.w0_ref), channel_id=1, source_target_pairs={{0,2},{1,3},{2,0},{3,1},{4,6},{5,7},{6,4},{7,5},{8,10},{9,11},{10,... | collective-permute-start | bytes 1572872 | tf_op jit(solution)/shard_map/ppermute | solution.py:420
  66.3 23.2 %collective-permute-start.6 = (bf16[4,512,128]{2,1,0:T(8,128)(2,1)S(1)}, bf16[4,512,128]{2,1,0:T(8,128)(2,1)}, u32[]{:S(2)}, u32[]{:S(2)}) collective-permute-start(bf16[4,512,128]{2,1,0:T(8,128)(2,1)S(1)} %pad_maximum_fusion.w0_ref), channel_id=1, source_target_pairs={{0,3},{1,0},{2,1},{3,2},{4,7},{5,4},{6,5},{7,6},{8,11},{9,8},{10,9... | collective-permute-start | bytes 1572872 | tf_op jit(solution)/shard_map/ppermute | solution.py:420
  77.0 12.4 %copy-start.6 = (bf16[4,512,128]{2,1,0:T(8,128)(2,1)}, bf16[4,512,128]{2,1,0:T(8,128)(2,1)S(1)}, u32[]{:S(2)}) copy-start(bf16[4,512,128]{2,1,0:T(8,128)(2,1)S(1)} %collective-permute-done.4.w1_ref) | copy-start | bytes 1572868
  89.4 0.8 copy-start.7
  99.7 7.2 %collective-permute-start.7 = (f32[264,128]{1,0:T(8,128)}, f32[264,128]{1,0:T(8,128)S(1)}, u32[]{:S(2)}, u32[]{:S(2)}) collective-permute-start(f32[264,128]{1,0:T(8,128)} %get-tuple-element.48.s0_ref), channel_id=1, source_target_pairs={{0,1},{1,2},{2,3},{3,0},{4,5},{5,6},{6,7},{7,4},{8,9},{9,10},{10,1... | collective-permute-start | bytes 405512 | tf_op jit(solution)/shard_map/ppermute | solution.py:420
  100.3 9.0 %collective-permute-start.8 = (f32[264,128]{1,0:T(8,128)}, f32[264,128]{1,0:T(8,128)S(1)}, u32[]{:S(2)}, u32[]{:S(2)}) collective-permute-start(f32[264,128]{1,0:T(8,128)} %get-tuple-element.48.s0_ref), channel_id=1, source_target_pairs={{0,2},{1,3},{2,0},{3,1},{4,6},{5,7},{6,4},{7,5},{8,10},{9,11},{10,... | collective-permute-start | bytes 405512 | tf_op jit(solution)/shard_map/ppermute | solution.py:420
  102.7 6.7 %collective-permute-start.9 = (f32[264,128]{1,0:T(8,128)}, f32[264,128]{1,0:T(8,128)S(1)}, u32[]{:S(2)}, u32[]{:S(2)}) collective-permute-start(f32[264,128]{1,0:T(8,128)} %get-tuple-element.48.s0_ref), channel_id=1, source_target_pairs={{0,3},{1,0},{2,1},{3,2},{4,7},{5,4},{6,5},{7,6},{8,11},{9,8},{10,9... | collective-permute-start | bytes 405512 | tf_op jit(solution)/shard_map/ppermute | solution.py:420
  107.0 2.5 %copy-start.11 = (f32[264,128]{1,0:T(8,128)}, f32[264,128]{1,0:T(8,128)S(1)}, u32[]{:S(2)}) copy-start(f32[264,128]{1,0:T(8,128)S(1)} %collective-permute-done.7.s1_ref) | copy-start | bytes 405508
  109.3 0.7 copy-start.12
  109.4 0.7 copy-start.13
  109.4 1.2 copy-start.1
  118.7 7.6 %collective-permute-start.10 = (f32[264,128]{1,0:T(8,128)}, f32[264,128]{1,0:T(8,128)S(1)}, u32[]{:S(2)}, u32[]{:S(2)}) collective-permute-start(f32[264,128]{1,0:T(8,128)} %get-tuple-element.53.s0_ref), channel_id=1, source_target_pairs={{0,1},{1,2},{2,3},{3,0},{4,5},{5,6},{6,7},{7,4},{8,9},{9,10},{10,1... | collective-permute-start | bytes 405512 | tf_op jit(solution)/shard_map/ppermute | solution.py:420
  119.5 9.2 %collective-permute-start.11 = (f32[264,128]{1,0:T(8,128)}, f32[264,128]{1,0:T(8,128)S(1)}, u32[]{:S(2)}, u32[]{:S(2)}) collective-permute-start(f32[264,128]{1,0:T(8,128)} %get-tuple-element.53.s0_ref), channel_id=1, source_target_pairs={{0,2},{1,3},{2,0},{3,1},{4,6},{5,7},{6,4},{7,5},{8,10},{9,11},{10,... | collective-permute-start | bytes 405512 | tf_op jit(solution)/shard_map/ppermute | solution.py:420
  122.9 5.8 %collective-permute-start.12 = (f32[264,128]{1,0:T(8,128)}, f32[264,128]{1,0:T(8,128)S(1)}, u32[]{:S(2)}, u32[]{:S(2)}) collective-permute-start(f32[264,128]{1,0:T(8,128)} %get-tuple-element.53.s0_ref), channel_id=1, source_target_pairs={{0,3},{1,0},{2,1},{3,2},{4,7},{5,4},{6,5},{7,6},{8,11},{9,8},{10,9... | collective-permute-start | bytes 405512 | tf_op jit(solution)/shard_map/ppermute | solution.py:420
  126.3 2.4 %copy-start.14 = (f32[264,128]{1,0:T(8,128)}, f32[264,128]{1,0:T(8,128)S(1)}, u32[]{:S(2)}) copy-start(f32[264,128]{1,0:T(8,128)S(1)} %collective-permute-done.10.s1_ref) | copy-start | bytes 405508
  128.7 0.7 copy-start.15
  128.7 0.7 copy-start.16
  139.8 7.6 %collective-permute-start.13 = (bf16[16,4,96,128]{3,2,1,0:T(8,128)(2,1)}, bf16[16,4,96,128]{3,2,1,0:T(8,128)(2,1)S(1)}, u32[]{:S(2)}, u32[]{:S(2)}) collective-permute-start(bf16[16,4,96,128]{3,2,1,0:T(8,128)(2,1)} %get-tuple-element.65), channel_id=1, source_target_pairs={{0,4},{4,0},{8,12},{12,8},{16,20},{20,16},{24,28},{28,24},{32,36},... | collective-permute-start | bytes 4718600 | tf_op jit(solution)/shard_map/ppermute | solution.py:429
  144.4 3.0 %collective-permute-start.14 = (bf16[16,4,64,128]{3,2,1,0:T(8,128)(2,1)}, bf16[16,4,64,128]{3,2,1,0:T(8,128)(2,1)S(1)}, u32[]{:S(2)}, u32[]{:S(2)}) collective-permute-start(bf16[16,4,64,128]{3,2,1,0:T(8,128)(2,1)} %get-tuple-element.71), channel_id=1, source_target_pairs={{0,4},{4,0},{8,12},{12,8},{16,20},{20,16},{24,28},{28,24},{32,36},... | collective-permute-start | bytes 3145736 | tf_op jit(solution)/shard_map/ppermute | solution.py:429
  147.4 1.0 copy-start.5
  147.4 1.5 copy-start.4
  153.5 9.6 %copy-start.24 = (f32[8,128]{1,0:T(8,128)S(1)}, f32[8,128]{1,0:T(8,128)}, u32[]{:S(2)}) copy-start(f32[8,128]{1,0:T(8,128)} %get-tuple-element.72) | copy-start | bytes 12292
  153.5 42.8 %all-to-all-start.2 = ((bf16[64,160,128]{2,1,0:T(8,128)(2,1)}), bf16[64,160,128]{2,1,0:T(8,128)(2,1)S(1)}, u32[]{:S(2)}, u32[]{:S(2)}) async-start(bf16[64,160,128]{2,1,0:T(8,128)(2,1)} %shard_map.158), calls=%async_computation.2 | async-start | bytes 5242880 | tf_op jit(solution)/shard_map/all_to_all | solution.py:434
  197.8 18.4 %all-to-all-start.3 = ((bf16[32,80,128]{2,1,0:T(8,128)(2,1)}), bf16[32,80,128]{2,1,0:T(8,128)(2,1)S(1)}, u32[]{:S(2)}, u32[]{:S(2)}) async-start(bf16[32,80,128]{2,1,0:T(8,128)(2,1)} %broadcast_in_dim.10), calls=%async_computation.3 | async-start | bytes 1310720 | tf_op jit(solution)/shard_map/all_to_all | solution.py:425
  205.6 10.6 %copy-start.10 = (f32[96,128]{1,0:T(8,128)}, f32[96,128]{1,0:T(8,128)S(1)}, u32[]{:S(2)}) copy-start(f32[96,128]{1,0:T(8,128)S(1)} %pad_maximum_fusion.1.r0_ref) | copy-start | bytes 147460
  205.6 5.8 %collective-permute-start.15 = (f32[96,128]{1,0:T(8,128)S(1)}, f32[96,128]{1,0:T(8,128)S(1)}, u32[]{:S(2)}, u32[]{:S(2)}) collective-permute-start(f32[96,128]{1,0:T(8,128)S(1)} %pad_maximum_fusion.1.r0_ref), channel_id=1, source_target_pairs={{0,1},{1,2},{2,3},{3,0},{4,5},{5,6},{6,7},{7,4},{8,9},{9,10},{10,1... | collective-permute-start | bytes 147464 | tf_op jit(solution)/shard_map/ppermute | solution.py:420
  206.4 5.6 %collective-permute-start.16 = (f32[96,128]{1,0:T(8,128)S(1)}, f32[96,128]{1,0:T(8,128)S(1)}, u32[]{:S(2)}, u32[]{:S(2)}) collective-permute-start(f32[96,128]{1,0:T(8,128)S(1)} %pad_maximum_fusion.1.r0_ref), channel_id=1, source_target_pairs={{0,2},{1,3},{2,0},{3,1},{4,6},{5,7},{6,4},{7,5},{8,10},{9,11},{10,... | collective-permute-start | bytes 147464 | tf_op jit(solution)/shard_map/ppermute | solution.py:420
  208.1 4.2 %collective-permute-start.17 = (f32[96,128]{1,0:T(8,128)S(1)}, f32[96,128]{1,0:T(8,128)S(1)}, u32[]{:S(2)}, u32[]{:S(2)}) collective-permute-start(f32[96,128]{1,0:T(8,128)S(1)} %pad_maximum_fusion.1.r0_ref), channel_id=1, source_target_pairs={{0,3},{1,0},{2,1},{3,2},{4,7},{5,4},{6,5},{7,6},{8,11},{9,8},{10,9... | collective-permute-start | bytes 147464 | tf_op jit(solution)/shard_map/ppermute | solution.py:420
  211.4 4.8 %copy-start.19 = (f32[96,128]{1,0:T(8,128)}, f32[96,128]{1,0:T(8,128)S(1)}, u32[]{:S(2)}) copy-start(f32[96,128]{1,0:T(8,128)S(1)} %collective-permute-done.15.r1_ref) | copy-start | bytes 147460
  212.0 4.2 %copy-start.20 = (f32[96,128]{1,0:T(8,128)}, f32[96,128]{1,0:T(8,128)S(1)}, u32[]{:S(2)}) copy-start(f32[96,128]{1,0:T(8,128)S(1)} %collective-permute-done.16.r2_ref) | copy-start | bytes 147460
  212.4 3.9 %copy-start.21 = (f32[96,128]{1,0:T(8,128)}, f32[96,128]{1,0:T(8,128)S(1)}, u32[]{:S(2)}) copy-start(f32[96,128]{1,0:T(8,128)S(1)} %collective-permute-done.17.r3_ref) | copy-start | bytes 147460
  216.2 0.9 copy-start.2

commit v3 on v1

--- a/solution.py
+++ b/solution.py
@@ -12,6 +12,7 @@
 F32 = jnp.float32
 BF16 = jnp.bfloat16
 CHUNK = 256
+UNROLL = 2
 
 
 def iota(shape, dim):
@@ -28,11 +29,11 @@
     return high, (a - high.astype(F32)).astype(BF16)
 
 
-def head_mean(a, mix):
-    high, low = split(a)
-    halves = [
-        dot(high[:, at : at + 256], mix) + dot(low[:, at : at + 256], mix) for at in (0, 256)
-    ]
+def head_mean(a, mix, terms=2):
+    halves = []
+    for at in (0, 256):
+        parts = split(a[:, at : at + 256])[:terms]
+        halves.append(sum(dot(part, mix) for part in parts))
     return jnp.concatenate(halves, axis=1)
 
 
@@ -56,7 +57,7 @@
     pair_ref[...] = jnp.where(col == 8 * (row & 63) + (row >> 6), 1.0, 0.0).astype(BF16)
 
 
-def cut_patches(load, pick_ref, out_ref, once_ref, pair_ref, turn_ref, whole_ref, rest_ref):
+def cut_patches(load, pick_ref, slot_ref, out_ref, once_ref, pair_ref, turn_ref, whole_ref, rest_ref):
     row, col = iota((128, 256), 0), iota((128, 256), 1)
     turn_pair = jnp.where(col == (row & 31) * 8 + 2 * (row >> 5), 1.0, 0.0).astype(BF16)
 
@@ -77,18 +78,15 @@
                 rest_ref[at, x * 128 : (x + 1) * 128] = rest[x * 32 : (x + 1) * 32, lanes]
         return carry
 
-    lax.fori_loop(0, 8, strips, 0)
-
-    def place(i, carry):
-        at = pl.ds(pl.multiple_of(i * CHUNK, CHUNK), CHUNK)
-        pick = pick_ref[at, :]
-        picked = dot(pick, whole_ref[...]).astype(BF16)
-        out_ref[at, 0:1024] = dot(picked, once_ref[...]).astype(BF16)
-        picked = dot(pick, rest_ref[...]).astype(BF16)
-        out_ref[at, 1024:1536] = dot(picked, pair_ref[...]).astype(BF16)
-        return carry
-
-    lax.fori_loop(0, 512 // CHUNK, place, 0)
+    lax.fori_loop(0, 8, strips, 0, unroll=UNROLL)
+
+    for part_ref, turn_back_ref, lanes in (
+        (whole_ref, once_ref, slice(0, 1024)),
+        (rest_ref, pair_ref, slice(1024, 1536)),
+    ):
+        picked = dot(pick_ref[...], part_ref[...]).astype(BF16)
+        picked = dot(picked, turn_back_ref[...]).astype(BF16)
+        out_ref[:, lanes] = dot(slot_ref[...], picked).astype(BF16)
 
 
 CUT_SCRATCH = [
@@ -100,21 +98,23 @@
 ]
 
 
-def old_kernel(field_hbm, anchor_ref, dest_ref, out_ref, pick_ref, field_ref, sem, *scratch):
+def old_kernel(field_hbm, anchor_ref, dest_ref, out_ref, pick_ref, slot_ref, field_ref, sem, *scratch):
     fetch = pltpu.make_async_copy(field_hbm, field_ref, sem)
     fetch.start()
     selections(*scratch[:3])
     target = dest_ref[...].astype(F32)
-    wide = jnp.broadcast_to(target, (256, 256))
     row, col = iota((256, 256), 0), iota((256, 256), 1)
-    tall = jnp.sum(jnp.where(row == col, wide, 0.0), axis=1, keepdims=True)
-    ahead = jnp.where((tall == wide) & (row < col), 1.0, 0.0)
+
+    def upright(line):
+        return jnp.sum(jnp.where(row == col, jnp.broadcast_to(line, (256, 256)), 0.0), axis=1, keepdims=True)
+
+    ahead = jnp.where((upright(target) == target) & (row < col), 1.0, 0.0)
     slot = target * 16.0 + jnp.sum(ahead, axis=0, keepdims=True)
     patch = ((anchor_ref[1] >> 3) & 15) * 32 + ((anchor_ref[2] >> 3) & 31)
-    row = iota((512, 256), 0)
-    sent = jnp.where(row == slot.astype(jnp.int32), 1.0, 0.0)
-    taken = jnp.where(row == patch, 1.0, 0.0).astype(BF16)
-    pick_ref[...] = dot(sent.astype(BF16), taken, (1, 1)).astype(BF16)
+    patch = upright(patch.astype(F32)).astype(jnp.int32)
+    pick_ref[...] = jnp.where(iota((256, 512), 1) == patch, 1.0, 0.0).astype(BF16)
+    sent = jnp.where(iota((512, 256), 0) == slot.astype(jnp.int32), 1.0, 0.0)
+    slot_ref[...] = sent.astype(BF16)
     tag = jnp.sum(sent, axis=1, keepdims=True)
     out_ref[:, 1536:1664] = jnp.broadcast_to(tag, (512, 128)).astype(BF16)
     fetch.wait()
@@ -123,11 +123,11 @@
         at = pl.ds(pl.multiple_of(by * 8, 8), 8)
         return field_ref[:, :, at, :].reshape(192, 256)
 
-    cut_patches(load, pick_ref, out_ref, *scratch)
+    cut_patches(load, pick_ref, slot_ref, out_ref, *scratch)
 
 
 def new_kernel(
-    field_hbm, z_prev_ref, z_next_ref, y_prev_ref, y_next_ref, pick_ref,
+    field_hbm, z_prev_ref, z_next_ref, y_prev_ref, y_next_ref, pick_ref, slot_ref,
     new_hbm, out_ref, pad_ref, new_ref, sem, *scratch,
 ):
     fetch = pltpu.make_async_copy(field_hbm, pad_ref.at[:, 1:9, 8:136, :], sem.at[0])
@@ -170,7 +170,7 @@
         at = pl.ds(pl.multiple_of(by * 8, 8), 8)
         return new_ref[:, :, at, :].reshape(192, 256)
 
-    cut_patches(load, pick_ref, out_ref, *scratch)
+    cut_patches(load, pick_ref, slot_ref, out_ref, *scratch)
     store.wait()
 
 
@@ -183,6 +183,16 @@
     row, col = iota((128, 128), 0), iota((128, 128), 1)
     own = row // 64 == col // 64
     return jnp.where(own, packed, 0.0), jnp.where(own, pltpu.roll(packed, 64, 1), 0.0)
+
+
+def quartets(packed, high_ref, low_ref):
+    blank = jnp.zeros((128, 128), F32)
+    for p in range(2):
+        one, two = unpack(packed[p * 128 : (p + 1) * 128])
+        whole = jnp.concatenate(
+            [jnp.concatenate([one, blank], axis=1), jnp.concatenate([blank, two], axis=1)], axis=0
+        )
+        high_ref[p], low_ref[p] = split(whole)
 
 
 def absolute(m, j):
@@ -217,7 +227,7 @@
         ):
             heads = dot(lifted, w_ref[...])
             shifted = heads - head_mean(heads, mix)
-            spread = jnp.sqrt(head_mean(shifted * shifted, mix) + EPSILON)
+            spread = jnp.sqrt(head_mean(shifted * shifted, mix, 1) + EPSILON)
             hat = shifted / spread
             normed.append(hat.astype(BF16))
             hat_ref[at, :] = normed[-1]
@@ -254,10 +264,7 @@
     total = (s0_ref[...] + s1_ref[...]) + (s2_ref[...] + s3_ref[...])
     count = total[256:264, :]
     count_ref[...] = count
-    for p in range(2):
-        blocks = unpack(total[p * 128 : (p + 1) * 128] / count[0:1, :])
-        for q in range(2):
-            high_ref[2 * p + q], low_ref[2 * p + q] = split(blocks[q])
+    quartets(total[0:256] / count[0:1, :], high_ref, low_ref)
     acc_ref[...] = jnp.zeros_like(acc_ref)
     loss_ref[...] = jnp.zeros_like(loss_ref)
 
@@ -265,8 +272,8 @@
         at = pl.ds(pl.multiple_of(i * CHUNK, CHUNK), CHUNK)
         query = query_ref[at, :]
         parts = []
-        for p in range(4):
-            part = query[:, p * 128 : (p + 1) * 128]
+        for p in range(2):
+            part = query[:, p * 256 : (p + 1) * 256]
             parts.append(dot(part, high_ref[p]) + dot(part, low_ref[p]))
         attended = jnp.concatenate(parts, axis=1).astype(BF16)
         attended_ref[at, :] = attended
@@ -282,14 +289,16 @@
         d_tokens = d_hidden.astype(BF16)
         d_tokens_ref[at, :] = d_tokens
         high, low = split(dot(d_tokens, out_w_ref[...], (1, 1)))
-        for p in range(4):
-            part = slice(p * 128, (p + 1) * 128)
+        for p in range(2):
+            part = slice(p * 256, (p + 1) * 256)
             back = (
                 dot(high[:, part], high_ref[p], (1, 1))
                 + dot(high[:, part], low_ref[p], (1, 1))
                 + dot(low[:, part], high_ref[p], (1, 1))
             )
             d_query_ref[at, part] = back.astype(BF16)
+        for p in range(4):
+            part = slice(p * 128, (p + 1) * 128)
             acc_ref[p] += dot(query[:, part], high[:, part], (0, 0)) + dot(
                 query[:, part], low[:, part], (0, 0)
             )
@@ -320,10 +329,7 @@
     fetch.start()
     total = (s0_ref[...] + s1_ref[...]) + (s2_ref[...] + s3_ref[...])
     loss_ref[...] = total[256:264, :]
-    for p in range(2):
-        blocks = unpack(total[p * 128 : (p + 1) * 128] / count_ref[0:1, :])
-        for q in range(2):
-            high_ref[2 * p + q], low_ref[2 * p + q] = split(blocks[q])
+    quartets(total[0:256] / count_ref[0:1, :], high_ref, low_ref)
     mix = mean_matrix()
 
     def rows(i, carry):
@@ -337,8 +343,8 @@
         ):
             other = other_ref[at, :]
             parts = []
-            for p in range(4):
-                part = other[:, p * 128 : (p + 1) * 128]
+            for p in range(2):
+                part = other[:, p * 256 : (p + 1) * 256]
                 parts.append(dot(part, high_ref[p], across) + dot(part, low_ref[p], across))
             grad = jnp.concatenate(parts, axis=1)
             hat = hat_ref[at, :].astype(F32)
@@ -434,9 +440,9 @@
     tall = jnp.concatenate([w_out[:, k * 128 : (k + 1) * 128] for k in range(4)], axis=0)
     heads_w = around(jnp.stack([w_query, w_key, w_value, tall]))
 
-    send_old, pick = call(
+    send_old, pick, slot = call(
         old_kernel,
-        [((512, 1664), BF16), ((512, 512), BF16)],
+        [((512, 1664), BF16), ((256, 512), BF16), ((512, 256), BF16)],
         [pltpu.VMEM((3, 8, 128, 256), F32), pltpu.SemaphoreType.DMA] + CUT_SCRATCH,
         "hvv",
     )(velocity, anchors.reshape(3, 1, 256), dest.reshape(1, 256))
@@ -450,9 +456,9 @@
             pltpu.SemaphoreType.DMA((2,)),
         ]
         + CUT_SCRATCH,
-        "hvvvvv",
+        "hvvvvvv",
         "hv",
-    )(velocity, z_prev, z_next, y_prev, y_next, pick)
+    )(velocity, z_prev, z_next, y_prev, y_next, pick, slot)
     new = exchange(send_new, "slab")
 
     wide, wide_f = ((512, 512), BF16), ((512, 512), F32)
@@ -472,8 +478,8 @@
             pltpu.VMEM((512, 512), BF16),
             pltpu.VMEM((512, 512), BF16),
             pltpu.VMEM((4, 128, 128), F32),
-            pltpu.VMEM((4, 128, 128), BF16),
-            pltpu.VMEM((4, 128, 128), BF16),
+            pltpu.VMEM((2, 256, 256), BF16),
+            pltpu.VMEM((2, 256, 256), BF16),
             pltpu.VMEM((8, 1536), F32),
         ],
         "svvvvvvvvv",
@@ -484,8 +490,8 @@
         backward_kernel,
         [((16, 4, 96, 128), BF16), ((16, 4, 96, 128), BF16), ((8, 128), F32)],
         [
-            pltpu.VMEM((4, 128, 128), BF16),
-            pltpu.VMEM((4, 128, 128), BF16),
+            pltpu.VMEM((2, 256, 256), BF16),
+            pltpu.VMEM((2, 256, 256), BF16),
             pltpu.VMEM((512, 1536), BF16),
             pltpu.VMEM((512, 512), BF16),
             pltpu.VMEM((512, 1536), BF16),

time: 229 us -> 225 us (0.983)
  Pallas kernels: 52.9 us -> 49.6 us
where the time goes in v3:
time: 225 us; the launch traced here: 221 us
  waiting for transfers between devices  93 us (41%)
  starting transfers between devices  63.1 us (28%)
  Pallas kernels  49.6 us (22%)
  local copies, waits for them, and re-layouts  7.88 us (4%)
  other arithmetic  6.46 us (3%)
    ppermute x12, waiting for transfers between devices, around(): got.append(lax.ppermute(value, 'mp', [(i, (i + d) % 4) for i in range(4)]))  37 us
    all_to_all x2, waiting for transfers between devices, total(): lax.all_to_all(partial.reshape(64, -1, 128), ('slab', 'mp'), split_axis=0...  34.8 us
    all_to_all x3, starting transfers between devices, exchange(): return lax.all_to_all(value, axes, split_axis=0, concat_axis=0, tiled=True)  21.3 us
    ppermute x12, starting transfers between devices, around(): got.append(lax.ppermute(value, 'mp', [(i, (i + d) % 4) for i in range(4)]))  18.8 us
    all_to_all x2, starting transfers between devices, total(): lax.all_to_all(partial.reshape(64, -1, 128), ('slab', 'mp'), split_axis=0...  16.8 us
    ppermute x1, waiting for transfers between devices, step(): z_prev = lax.ppermute(velocity[:, 7:8], 'slab', up)  15.6 us
    pallas_call x1, Pallas kernels, step(): call(backward_kernel, [((16, 4, 96, 128), BF16), ((16, 4, 96, 128), BF16)...  10.9 us
    pallas_call x1, Pallas kernels, step(): call(new_kernel, [((3, 8, 128, 256), F32), ((512, 1536), BF16)], [pltpu.V...  10.5 us
  transfers between devices with their start and end apart: 23, of which 15 were waited for; matrix products, arithmetic and copies ran while one was open for 4% of the time, Pallas kernels for 14%

profile of v3, /device:TPU:6, one launch (start us, length us, event | category | flops | bytes accessed | tf_op | source)
XLA Modules:
  0.0 221.1 jit_solution(7689698925987009407)
XLA Ops:
  0.6 7.1 %shard_map.152 = (bf16[512,1664]{1,0:T(8,128)(2,1)}, bf16[256,512]{1,0:T(8,128)(2,1)}, bf16[512,256]{1,0:T(8,128)(2,1)}) custom-call(f32[3,8,128,256]{3,2,1,0:T(8,128)} %field_hbm.3, s32[3,1,256]{2,1,0:T(1,128)} %bitcast.24, s32[1,256]{1,0:T(1,128)} %bitcast.25), custom_call_target="tpu_custom_call" | custom-call | tf_op jit(solution)/shard_map/pallas_call | solution.py:443
  7.8 7.6 %all-to-all-start = ((bf16[32,16,1664]{2,1,0:T(8,128)(2,1)}), bf16[32,16,1664]{2,1,0:T(8,128)(2,1)S(1)}, u32[]{:S(2)}, u32[]{:S(2)}) async-start(bf16[32,16,1664]{2,1,0:T(8,128)(2,1)} %bitcast.19), calls=%async_computation | async-start | bytes 3407872 | tf_op jit(solution)/shard_map/all_to_all | solution.py:410
  15.3 1.2 fusion.1
  16.5 0.2 collective-permute-start
  16.7 1.6 collective-permute-start.1
  18.3 1.1 fusion
  19.4 2.0 collective-permute-start.2
  21.4 2.2 collective-permute-start.3
  23.6 1.7 collective-permute-done.2.y_prev_ref
  25.3 15.6 %collective-permute-done.z_prev_ref = f32[3,1,128,256]{3,2,1,0:T(8,128)S(1)} collective-permute-done((f32[3,1,128,256]{3,2,1,0:T(8,128)S(1)}, f32[3,1,128,256]{3,2,1,0:T(8,128)S(1)}, u32[]{:S(2)}, u32[]{:S(2)}) %collective-permute-start) | collective-permute-done | bytes 393248 | tf_op jit(solution)/shard_map/ppermute | solution.py:435
  40.9 0.7 copy-done.8
  41.7 0.1 copy-done.9
  41.8 10.5 %shard_map.153 = (f32[3,8,128,256]{3,2,1,0:T(8,128)}, bf16[512,1536]{1,0:T(8,128)(2,1)}) custom-call(f32[3,8,128,256]{3,2,1,0:T(8,128)} %field_hbm.3, f32[3,1,128,256]{3,2,1,0:T(8,128)} %copy-done.8, f32[3,1,128,256]{3,2,1,0:T(8,128)} %copy-done.9, f32[3,8,1,256]{3,2,1,0:T(1,128)} %copy-done.22, f32[3,8,1,256]{3,2,1,0:T(1,128)} %copy-done.23, ...), custom_call_target="tpu_custom_call" | custom-call | tf_op jit(solution)/shard_map/pallas_call | solution.py:450
  52.3 0.0 copy-start.17
  52.3 0.0 copy-start.18
  52.3 7.2 %all-to-all-start.1 = ((bf16[32,16,1536]{2,1,0:T(8,128)(2,1)}), bf16[32,16,1536]{2,1,0:T(8,128)(2,1)S(1)}, u32[]{:S(2)}, u32[]{:S(2)}) async-start(bf16[32,16,1536]{2,1,0:T(8,128)(2,1)} %bitcast.20), calls=%async_computation.1 | async-start | bytes 3145728 | tf_op jit(solution)/shard_map/all_to_all | solution.py:410
  59.7 1.0 pad_maximum_fusion.w0_ref
  60.7 2.0 collective-permute-start.4
  62.7 3.6 %collective-permute-start.5 = (bf16[4,512,128]{2,1,0:T(8,128)(2,1)S(1)}, bf16[4,512,128]{2,1,0:T(8,128)(2,1)S(1)}, u32[]{:S(2)}, u32[]{:S(2)}) collective-permute-start(bf16[4,512,128]{2,1,0:T(8,128)(2,1)S(1)} %pad_maximum_fusion.w0_ref), channel_id=1, source_target_pairs={{0,2},{1,3},{2,0},{3,1},{4,6},{5,7},{6,4},{7,5},{8,10},{9,11},{10,... | collective-permute-start | bytes 1572872 | tf_op jit(solution)/shard_map/ppermute | solution.py:405
  66.3 1.0 collective-permute-start.6
  67.3 0.6 pad_add_fusion.place_ref
  67.9 9.1 %collective-permute-done.4.w1_ref = bf16[4,512,128]{2,1,0:T(8,128)(2,1)S(1)} collective-permute-done((bf16[4,512,128]{2,1,0:T(8,128)(2,1)S(1)}, bf16[4,512,128]{2,1,0:T(8,128)(2,1)S(1)}, u32[]{:S(2)}, u32[]{:S(2)}) %collective-permute-start.4) | collective-permute-done | bytes 524320 | tf_op jit(solution)/shard_map/ppermute | solution.py:405
  77.0 12.4 %collective-permute-done.5.w2_ref = bf16[4,512,128]{2,1,0:T(8,128)(2,1)S(1)} collective-permute-done((bf16[4,512,128]{2,1,0:T(8,128)(2,1)S(1)}, bf16[4,512,128]{2,1,0:T(8,128)(2,1)S(1)}, u32[]{:S(2)}, u32[]{:S(2)}) %collective-permute-start.5) | collective-permute-done | bytes 524320 | tf_op jit(solution)/shard_map/ppermute | solution.py:405
  89.5 0.8 copy-done.7
  90.3 9.2 %shard_map.154 = (bf16[512,512]{1,0:T(8,128)(2,1)}, bf16[512,512]{1,0:T(8,128)(2,1)}, bf16[512,512]{1,0:T(8,128)(2,1)}, f32[512,512]{1,0:T(8,128)}, bf16[512,512...) custom-call(s32[2]{0:T(128)} %pad_add_fusion.place_ref, ...), custom_call_target="tpu_custom_call" | custom-call | tf_op jit(solution)/shard_map/pallas_call | solution.py:465
  99.5 0.6 collective-permute-start.7
  100.0 2.4 %collective-permute-start.8 = (f32[264,128]{1,0:T(8,128)}, f32[264,128]{1,0:T(8,128)S(1)}, u32[]{:S(2)}, u32[]{:S(2)}) collective-permute-start(f32[264,128]{1,0:T(8,128)} %get-tuple-element.44.s0_ref), channel_id=1, source_target_pairs={{0,2},{1,3},{2,0},{3,1},{4,6},{5,7},{6,4},{7,5},{8,10},{9,11},{10,... | collective-permute-start | bytes 405512 | tf_op jit(solution)/shard_map/ppermute | solution.py:405
  102.4 1.3 collective-permute-start.9
  103.7 3.1 %collective-permute-done.7.s1_ref = f32[264,128]{1,0:T(8,128)S(1)} collective-permute-done((f32[264,128]{1,0:T(8,128)}, f32[264,128]{1,0:T(8,128)S(1)}, u32[]{:S(2)}, u32[]{:S(2)}) %collective-permute-start.7) | collective-permute-done | bytes 135200 | tf_op jit(solution)/shard_map/ppermute | solution.py:405
  106.8 2.2 %collective-permute-done.8.s2_ref = f32[264,128]{1,0:T(8,128)S(1)} collective-permute-done((f32[264,128]{1,0:T(8,128)}, f32[264,128]{1,0:T(8,128)S(1)}, u32[]{:S(2)}, u32[]{:S(2)}) %collective-permute-start.8) | collective-permute-done | bytes 135200 | tf_op jit(solution)/shard_map/ppermute | solution.py:405
  109.0 0.1 collective-permute-done.9.s3_ref
  109.1 0.5 copy-done.14
  109.7 0.1 copy-done.16
  109.8 0.5 copy-done.1
  110.3 9.7 %shard_map.155 = (bf16[16,4,64,128]{3,2,1,0:T(8,128)(2,1)}, bf16[16,4,64,128]{3,2,1,0:T(8,128)(2,1)}, bf16[512,512]{1,0:T(8,128)(2,1)}, f32[512,512]{1,0:T(8,128...) custom-call(s32[2]{0:T(128)} %pad_add_fusion.place_ref, f32[264,128]{1,0:T(8,128)} %get-tuple-element.44.s0_ref, ...), custom_call_target="tpu_custom_call" | custom-call | tf_op jit(solution)/shard_map/pallas_call | solution.py:472
  120.1 0.0 collective-permute-start.14
  120.1 0.8 collective-permute-start.10
  120.9 3.4 %collective-permute-start.11 = (f32[264,128]{1,0:T(8,128)}, f32[264,128]{1,0:T(8,128)S(1)}, u32[]{:S(2)}, u32[]{:S(2)}) collective-permute-start(f32[264,128]{1,0:T(8,128)} %get-tuple-element.49.s0_ref), channel_id=1, source_target_pairs={{0,2},{1,3},{2,0},{3,1},{4,6},{5,7},{6,4},{7,5},{8,10},{9,11},{10,... | collective-permute-start | bytes 405512 | tf_op jit(solution)/shard_map/ppermute | solution.py:405
  124.3 3.2 %collective-permute-done.10.s1_ref = f32[264,128]{1,0:T(8,128)S(1)} collective-permute-done((f32[264,128]{1,0:T(8,128)}, f32[264,128]{1,0:T(8,128)S(1)}, u32[]{:S(2)}, u32[]{:S(2)}) %collective-permute-start.10) | collective-permute-done | bytes 135200 | tf_op jit(solution)/shard_map/ppermute | solution.py:405
  127.5 3.8 %collective-permute-done.11.s2_ref = f32[264,128]{1,0:T(8,128)S(1)} collective-permute-done((f32[264,128]{1,0:T(8,128)}, f32[264,128]{1,0:T(8,128)S(1)}, u32[]{:S(2)}, u32[]{:S(2)}) %collective-permute-start.11) | collective-permute-done | bytes 135200 | tf_op jit(solution)/shard_map/ppermute | solution.py:405
  131.3 0.6 copy-done.13
  132.0 0.0 copy-done.15
  132.0 10.9 %shard_map.156 = (bf16[16,4,96,128]{3,2,1,0:T(8,128)(2,1)}, bf16[16,4,96,128]{3,2,1,0:T(8,128)(2,1)}, f32[8,128]{1,0:T(8,128)}) custom-call(s32[2]{0:T(128)} %pad_add_fusion.place_ref, f32[264,128]{1,0:T(8,128)} %get-tuple-element.49.s0_ref, f32[264,128]{1,0:T(8,128)} %copy-done.11, f32[264,128]{1,0:T(8,128)} %copy-done.13, f32[264,128]{1,0:T(8,128)} %copy-done.15, ...), custom_call_target="tpu_custom_call" | custom-call | tf_op jit(solution)/shard_map/pallas_call | solution.py:489
  142.9 0.1 collective-permute-start.13
  143.0 1.4 add_convert_fusion.1
  144.4 9.7 %all-to-all-start.3 = ((bf16[64,64,128]{2,1,0:T(8,128)(2,1)}), bf16[64,64,128]{2,1,0:T(8,128)(2,1)S(1)}, u32[]{:S(2)}, u32[]{:S(2)}) async-start(bf16[64,64,128]{2,1,0:T(8,128)(2,1)} %bitcast.13), calls=%async_computation.3 | async-start | bytes 2097152 | tf_op jit(solution)/shard_map/all_to_all | solution.py:420
  154.1 3.0 %add_convert_fusion = bf16[16,4,96,128]{3,2,1,0:T(8,128)(2,1)} fusion(bf16[16,4,96,128]{3,2,1,0:T(8,128)(2,1)} %collective-permute-done.13, bf16[16,4,96,128]{3,2,1,0:T(8,128)(2,1)S(1)} %copy-done.4), kind=kLoop, calls=%fused_computation.1 | loop fusion | flops 3145728 | bytes 4718592 | tf_op jit(solution)/shard_map/convert_element_type | solution.py:415
  157.1 13.9 %all-to-all-done.3 = bf16[64,64,128]{2,1,0:T(8,128)(2,1)S(1)} async-done(((bf16[64,64,128]{2,1,0:T(8,128)(2,1)}), bf16[64,64,128]{2,1,0:T(8,128)(2,1)S(1)}, u32[]{:S(2)}, u32[]{:S(2)}) %all-to-all-start.3) | async-done | bytes 1048608 | tf_op jit(solution)/shard_map/all_to_all | solution.py:420
  171.0 7.2 %all-to-all-start.2 = ((bf16[64,96,128]{2,1,0:T(8,128)(2,1)}), bf16[64,96,128]{2,1,0:T(8,128)(2,1)S(1)}, u32[]{:S(2)}, u32[]{:S(2)}) async-start(bf16[64,96,128]{2,1,0:T(8,128)(2,1)} %bitcast.12), calls=%async_computation.2 | async-start | bytes 3145728 | tf_op jit(solution)/shard_map/all_to_all | solution.py:420
  178.2 0.2 convert_reduce_fusion.1
  178.4 20.9 %all-to-all-done.2 = bf16[64,96,128]{2,1,0:T(8,128)(2,1)S(1)} async-done(((bf16[64,96,128]{2,1,0:T(8,128)(2,1)}), bf16[64,96,128]{2,1,0:T(8,128)(2,1)S(1)}, u32[]{:S(2)}, u32[]{:S(2)}) %all-to-all-start.2) | async-done | bytes 1572896 | tf_op jit(solution)/shard_map/all_to_all | solution.py:420
  199.3 0.2 convert_reduce_fusion
  199.5 0.2 concatenate.14
  199.7 0.9 broadcast_in_dim.10
  200.6 6.5 %all-to-all-start.4 = ((bf16[32,80,128]{2,1,0:T(8,128)(2,1)}), bf16[32,80,128]{2,1,0:T(8,128)(2,1)S(1)}, u32[]{:S(2)}, u32[]{:S(2)}) async-start(bf16[32,80,128]{2,1,0:T(8,128)(2,1)} %broadcast_in_dim.10), calls=%async_computation.4 | async-start | bytes 1310720 | tf_op jit(solution)/shard_map/all_to_all | solution.py:410
  207.2 0.9 collective-permute-start.15
  208.1 1.6 collective-permute-start.16
  209.7 1.3 collective-permute-start.17
  211.0 2.1 collective-permute-done.15.r1_ref
  213.1 0.6 collective-permute-done.16.r2_ref
  213.7 0.3 collective-permute-done.17.r3_ref
  214.0 3.9 %all-to-all-done.4.heads_ref = bf16[32,80,128]{2,1,0:T(8,128)(2,1)S(1)} async-done(((bf16[32,80,128]{2,1,0:T(8,128)(2,1)}), bf16[32,80,128]{2,1,0:T(8,128)(2,1)S(1)}, u32[]{:S(2)}, u32[]{:S(2)}) %all-to-all-start.4) | async-done | bytes 655392 | tf_op jit(solution)/shard_map/all_to_all | solution.py:410
  217.9 0.8 copy-done.2
  218.8 2.3 %shard_map.157 = (f32[48,512]{1,0:T(8,128)}, f32[512,128]{1,0:T(8,128)}, f32[512,128]{1,0:T(8,128)}, f32[512,128]{1,0:T(8,128)}, f32[128,512]{1,0:T(8,128)}, /*index=5*/f32[16,1536]{1,0:T(8,128)}, f32[1,1]{1,0:T(1,128)}) custom-call(s32[2]{0:T(128)} %pad_add_fusion.place_ref, f32[96,128]{1,0:T(8,128)} %copy-done.10, f32[96,128]{1,0:T(8,128)} %copy-done.19, ...), custom_call_target="tpu_custom_call" | custom-call | tf_op jit(solution)/shard_map/pallas_call | solution.py:509
  (59 shorter events, 0.2 us)
Async XLA Ops:
  7.8 44.5 %all-to-all-start = ((bf16[32,16,1664]{2,1,0:T(8,128)(2,1)}), bf16[32,16,1664]{2,1,0:T(8,128)(2,1)S(1)}, u32[]{:S(2)}, u32[]{:S(2)}) async-start(bf16[32,16,1664]{2,1,0:T(8,128)(2,1)} %bitcast.19), calls=%async_computation | async-start | bytes 3407872 | tf_op jit(solution)/shard_map/all_to_all | solution.py:410
  16.5 24.4 %collective-permute-start = (f32[3,1,128,256]{3,2,1,0:T(8,128)S(1)}, f32[3,1,128,256]{3,2,1,0:T(8,128)S(1)}, u32[]{:S(2)}, u32[]{:S(2)}) collective-permute-start(f32[3,1,128,256]{3,2,1,0:T(8,128)S(1)} %get-tuple-element.77), channel_id=1, source_target_pairs={{0,4},{4,8},{8,12},{12,16},{16,20},{20,24},{24,28},{28,32},{32,36}... | collective-permute-start | bytes 1179656 | tf_op jit(solution)/shard_map/ppermute | solution.py:435
  16.7 24.2 %collective-permute-start.1 = (f32[3,1,128,256]{3,2,1,0:T(8,128)S(1)}, f32[3,1,128,256]{3,2,1,0:T(8,128)S(1)}, u32[]{:S(2)}, u32[]{:S(2)}) collective-permute-start(f32[3,1,128,256]{3,2,1,0:T(8,128)S(1)} %get-tuple-element.76), channel_id=1, source_target_pairs={{4,0},{8,4},{12,8},{16,12},{20,16},{24,20},{28,24},{32,28},{36,32}... | collective-permute-start | bytes 1179656 | tf_op jit(solution)/shard_map/ppermute | solution.py:436
  19.4 5.9 %collective-permute-start.2 = (f32[3,8,1,256]{3,2,1,0:T(1,128)S(1)}, f32[3,8,1,256]{3,2,1,0:T(1,128)S(1)}, u32[]{:S(2)}, u32[]{:S(2)}) collective-permute-start(f32[3,8,1,256]{3,2,1,0:T(1,128)S(1)} %get-tuple-element.75), channel_id=1, source_target_pairs={{0,1},{1,2},{2,3},{3,0},{4,5},{5,6},{6,7},{7,4},{8,9},{9,10},{10,1... | collective-permute-start | bytes 73736 | tf_op jit(solution)/shard_map/ppermute | solution.py:438
  21.4 3.9 %collective-permute-start.3 = (f32[3,8,1,256]{3,2,1,0:T(1,128)S(1)}, f32[3,8,1,256]{3,2,1,0:T(1,128)S(1)}, u32[]{:S(2)}, u32[]{:S(2)}) collective-permute-start(f32[3,8,1,256]{3,2,1,0:T(1,128)S(1)} %get-tuple-element.74), channel_id=1, source_target_pairs={{1,0},{2,1},{3,2},{0,3},{5,4},{6,5},{7,6},{4,7},{9,8},{10,9},{11,1... | collective-permute-start | bytes 73736 | tf_op jit(solution)/shard_map/ppermute | solution.py:439
  25.3 15.6 %copy-start.22 = (f32[3,8,1,256]{3,2,1,0:T(1,128)}, f32[3,8,1,256]{3,2,1,0:T(1,128)S(1)}, u32[]{:S(2)}) copy-start(f32[3,8,1,256]{3,2,1,0:T(1,128)S(1)} %collective-permute-done.2.y_prev_ref) | copy-start | bytes 73732
  25.3 15.6 %copy-start.23 = (f32[3,8,1,256]{3,2,1,0:T(1,128)}, f32[3,8,1,256]{3,2,1,0:T(1,128)S(1)}, u32[]{:S(2)}) copy-start(f32[3,8,1,256]{3,2,1,0:T(1,128)S(1)} %collective-permute-done.3.y_next_ref) | copy-start | bytes 73732
  40.9 0.7 copy-start.8
  40.9 0.9 copy-start.9
  52.3 7.3 %copy-start.17 = (bf16[128,512]{1,0:T(8,128)(2,1)S(1)}, bf16[128,512]{1,0:T(8,128)(2,1)}, u32[]{:S(2)}) copy-start(bf16[128,512]{1,0:T(8,128)(2,1)} %param.16) | copy-start | bytes 393220
  52.3 7.3 %copy-start = (bf16[32,16,1664]{2,1,0:T(8,128)(2,1)}, bf16[32,16,1664]{2,1,0:T(8,128)(2,1)S(1)}, u32[]{:S(2)}) copy-start(bf16[32,16,1664]{2,1,0:T(8,128)(2,1)S(1)} %all-to-all-done) | copy-start | bytes 5111812
  52.3 7.3 %copy-start.18 = (bf16[512,128]{1,0:T(8,128)(2,1)S(1)}, bf16[512,128]{1,0:T(8,128)(2,1)}, u32[]{:S(2)}) copy-start(bf16[512,128]{1,0:T(8,128)(2,1)} %param.15) | copy-start | bytes 393220
  52.3 56.8 %all-to-all-start.1 = ((bf16[32,16,1536]{2,1,0:T(8,128)(2,1)}), bf16[32,16,1536]{2,1,0:T(8,128)(2,1)S(1)}, u32[]{:S(2)}, u32[]{:S(2)}) async-start(bf16[32,16,1536]{2,1,0:T(8,128)(2,1)} %bitcast.20), calls=%async_computation.1 | async-start | bytes 3145728 | tf_op jit(solution)/shard_map/all_to_all | solution.py:410
  60.7 28.7 %copy-start.3 = (bf16[4,512,128]{2,1,0:T(8,128)(2,1)}, bf16[4,512,128]{2,1,0:T(8,128)(2,1)S(1)}, u32[]{:S(2)}) copy-start(bf16[4,512,128]{2,1,0:T(8,128)(2,1)S(1)} %pad_maximum_fusion.w0_ref) | copy-start | bytes 1572868
  60.7 16.3 %collective-permute-start.4 = (bf16[4,512,128]{2,1,0:T(8,128)(2,1)S(1)}, bf16[4,512,128]{2,1,0:T(8,128)(2,1)S(1)}, u32[]{:S(2)}, u32[]{:S(2)}) collective-permute-start(bf16[4,512,128]{2,1,0:T(8,128)(2,1)S(1)} %pad_maximum_fusion.w0_ref), channel_id=1, source_target_pairs={{0,1},{1,2},{2,3},{3,0},{4,5},{5,6},{6,7},{7,4},{8,9},{9,10},{10,1... | collective-permute-start | bytes 1572872 | tf_op jit(solution)/shard_map/ppermute | solution.py:405
  62.7 26.7 %collective-permute-start.5 = (bf16[4,512,128]{2,1,0:T(8,128)(2,1)S(1)}, bf16[4,512,128]{2,1,0:T(8,128)(2,1)S(1)}, u32[]{:S(2)}, u32[]{:S(2)}) collective-permute-start(bf16[4,512,128]{2,1,0:T(8,128)(2,1)S(1)} %pad_maximum_fusion.w0_ref), channel_id=1, source_target_pairs={{0,2},{1,3},{2,0},{3,1},{4,6},{5,7},{6,4},{7,5},{8,10},{9,11},{10,... | collective-permute-start | bytes 1572872 | tf_op jit(solution)/shard_map/ppermute | solution.py:405
  66.3 23.2 %collective-permute-start.6 = (bf16[4,512,128]{2,1,0:T(8,128)(2,1)S(1)}, bf16[4,512,128]{2,1,0:T(8,128)(2,1)}, u32[]{:S(2)}, u32[]{:S(2)}) collective-permute-start(bf16[4,512,128]{2,1,0:T(8,128)(2,1)S(1)} %pad_maximum_fusion.w0_ref), channel_id=1, source_target_pairs={{0,3},{1,0},{2,1},{3,2},{4,7},{5,4},{6,5},{7,6},{8,11},{9,8},{10,9... | collective-permute-start | bytes 1572872 | tf_op jit(solution)/shard_map/ppermute | solution.py:405
  77.0 12.4 %copy-start.6 = (bf16[4,512,128]{2,1,0:T(8,128)(2,1)}, bf16[4,512,128]{2,1,0:T(8,128)(2,1)S(1)}, u32[]{:S(2)}) copy-start(bf16[4,512,128]{2,1,0:T(8,128)(2,1)S(1)} %collective-permute-done.4.w1_ref) | copy-start | bytes 1572868
  89.4 0.8 copy-start.7
  99.5 7.3 %collective-permute-start.7 = (f32[264,128]{1,0:T(8,128)}, f32[264,128]{1,0:T(8,128)S(1)}, u32[]{:S(2)}, u32[]{:S(2)}) collective-permute-start(f32[264,128]{1,0:T(8,128)} %get-tuple-element.44.s0_ref), channel_id=1, source_target_pairs={{0,1},{1,2},{2,3},{3,0},{4,5},{5,6},{6,7},{7,4},{8,9},{9,10},{10,1... | collective-permute-start | bytes 405512 | tf_op jit(solution)/shard_map/ppermute | solution.py:405
  100.0 9.0 %collective-permute-start.8 = (f32[264,128]{1,0:T(8,128)}, f32[264,128]{1,0:T(8,128)S(1)}, u32[]{:S(2)}, u32[]{:S(2)}) collective-permute-start(f32[264,128]{1,0:T(8,128)} %get-tuple-element.44.s0_ref), channel_id=1, source_target_pairs={{0,2},{1,3},{2,0},{3,1},{4,6},{5,7},{6,4},{7,5},{8,10},{9,11},{10,... | collective-permute-start | bytes 405512 | tf_op jit(solution)/shard_map/ppermute | solution.py:405
  102.4 6.7 %collective-permute-start.9 = (f32[264,128]{1,0:T(8,128)}, f32[264,128]{1,0:T(8,128)S(1)}, u32[]{:S(2)}, u32[]{:S(2)}) collective-permute-start(f32[264,128]{1,0:T(8,128)} %get-tuple-element.44.s0_ref), channel_id=1, source_target_pairs={{0,3},{1,0},{2,1},{3,2},{4,7},{5,4},{6,5},{7,6},{8,11},{9,8},{10,9... | collective-permute-start | bytes 405512 | tf_op jit(solution)/shard_map/ppermute | solution.py:405
  106.8 2.4 %copy-start.12 = (f32[264,128]{1,0:T(8,128)}, f32[264,128]{1,0:T(8,128)S(1)}, u32[]{:S(2)}) copy-start(f32[264,128]{1,0:T(8,128)S(1)} %collective-permute-done.7.s1_ref) | copy-start | bytes 405508
  109.0 0.7 copy-start.14
  109.1 0.7 copy-start.16
  109.1 1.2 copy-start.1
  120.1 22.9 %collective-permute-start.14 = (bf16[16,4,64,128]{3,2,1,0:T(8,128)(2,1)}, bf16[16,4,64,128]{3,2,1,0:T(8,128)(2,1)S(1)}, u32[]{:S(2)}, u32[]{:S(2)}) collective-permute-start(bf16[16,4,64,128]{3,2,1,0:T(8,128)(2,1)} %get-tuple-element.63), channel_id=1, source_target_pairs={{0,4},{4,0},{8,12},{12,8},{16,20},{20,16},{24,28},{28,24},{32,36},... | collective-permute-start | bytes 3145736 | tf_op jit(solution)/shard_map/ppermute | solution.py:414
  120.1 7.4 %collective-permute-start.10 = (f32[264,128]{1,0:T(8,128)}, f32[264,128]{1,0:T(8,128)S(1)}, u32[]{:S(2)}, u32[]{:S(2)}) collective-permute-start(f32[264,128]{1,0:T(8,128)} %get-tuple-element.49.s0_ref), channel_id=1, source_target_pairs={{0,1},{1,2},{2,3},{3,0},{4,5},{5,6},{6,7},{7,4},{8,9},{9,10},{10,1... | collective-permute-start | bytes 405512 | tf_op jit(solution)/shard_map/ppermute | solution.py:405
  120.9 10.4 %collective-permute-start.11 = (f32[264,128]{1,0:T(8,128)}, f32[264,128]{1,0:T(8,128)S(1)}, u32[]{:S(2)}, u32[]{:S(2)}) collective-permute-start(f32[264,128]{1,0:T(8,128)} %get-tuple-element.49.s0_ref), channel_id=1, source_target_pairs={{0,2},{1,3},{2,0},{3,1},{4,6},{5,7},{6,4},{7,5},{8,10},{9,11},{10,... | collective-permute-start | bytes 405512 | tf_op jit(solution)/shard_map/ppermute | solution.py:405
  124.3 7.0 %collective-permute-start.12 = (f32[264,128]{1,0:T(8,128)}, f32[264,128]{1,0:T(8,128)S(1)}, u32[]{:S(2)}, u32[]{:S(2)}) collective-permute-start(f32[264,128]{1,0:T(8,128)} %get-tuple-element.49.s0_ref), channel_id=1, source_target_pairs={{0,3},{1,0},{2,1},{3,2},{4,7},{5,4},{6,5},{7,6},{8,11},{9,8},{10,9... | collective-permute-start | bytes 405512 | tf_op jit(solution)/shard_map/ppermute | solution.py:405
  127.5 3.8 %copy-start.11 = (f32[264,128]{1,0:T(8,128)}, f32[264,128]{1,0:T(8,128)S(1)}, u32[]{:S(2)}) copy-start(f32[264,128]{1,0:T(8,128)S(1)} %collective-permute-done.10.s1_ref) | copy-start | bytes 405508
  131.3 0.7 copy-start.13
  131.3 0.7 copy-start.15
  132.0 11.0 %copy-start.5 = (bf16[16,4,64,128]{3,2,1,0:T(8,128)(2,1)S(1)}, bf16[16,4,64,128]{3,2,1,0:T(8,128)(2,1)}, u32[]{:S(2)}) copy-start(bf16[16,4,64,128]{3,2,1,0:T(8,128)(2,1)} %get-tuple-element.62) | copy-start | bytes 3145732
  142.9 11.2 %collective-permute-start.13 = (bf16[16,4,96,128]{3,2,1,0:T(8,128)(2,1)}, bf16[16,4,96,128]{3,2,1,0:T(8,128)(2,1)}, u32[]{:S(2)}, u32[]{:S(2)}) collective-permute-start(bf16[16,4,96,128]{3,2,1,0:T(8,128)(2,1)} %get-tuple-element.61), channel_id=1, source_target_pairs={{0,4},{4,0},{8,12},{12,8},{16,20},{20,16},{24,28},{28,24},{32,36},... | collective-permute-start | bytes 4718600 | tf_op jit(solution)/shard_map/ppermute | solution.py:414
  144.4 9.7 %copy-start.4 = (bf16[16,4,96,128]{3,2,1,0:T(8,128)(2,1)S(1)}, bf16[16,4,96,128]{3,2,1,0:T(8,128)(2,1)}, u32[]{:S(2)}) copy-start(bf16[16,4,96,128]{3,2,1,0:T(8,128)(2,1)} %get-tuple-element.60) | copy-start | bytes 4718596
  144.4 26.6 %all-to-all-start.3 = ((bf16[64,64,128]{2,1,0:T(8,128)(2,1)}), bf16[64,64,128]{2,1,0:T(8,128)(2,1)S(1)}, u32[]{:S(2)}, u32[]{:S(2)}) async-start(bf16[64,64,128]{2,1,0:T(8,128)(2,1)} %bitcast.13), calls=%async_computation.3 | async-start | bytes 2097152 | tf_op jit(solution)/shard_map/all_to_all | solution.py:420
  157.1 21.1 %copy-start.24 = (f32[8,128]{1,0:T(8,128)S(1)}, f32[8,128]{1,0:T(8,128)}, u32[]{:S(2)}) copy-start(f32[8,128]{1,0:T(8,128)} %get-tuple-element.64) | copy-start | bytes 12292
  171.0 28.2 %all-to-all-start.2 = ((bf16[64,96,128]{2,1,0:T(8,128)(2,1)}), bf16[64,96,128]{2,1,0:T(8,128)(2,1)S(1)}, u32[]{:S(2)}, u32[]{:S(2)}) async-start(bf16[64,96,128]{2,1,0:T(8,128)(2,1)} %bitcast.12), calls=%async_computation.2 | async-start | bytes 3145728 | tf_op jit(solution)/shard_map/all_to_all | solution.py:420
  200.6 17.3 %all-to-all-start.4 = ((bf16[32,80,128]{2,1,0:T(8,128)(2,1)}), bf16[32,80,128]{2,1,0:T(8,128)(2,1)S(1)}, u32[]{:S(2)}, u32[]{:S(2)}) async-start(bf16[32,80,128]{2,1,0:T(8,128)(2,1)} %broadcast_in_dim.10), calls=%async_computation.4 | async-start | bytes 1310720 | tf_op jit(solution)/shard_map/all_to_all | solution.py:410
  207.2 10.7 %copy-start.10 = (f32[96,128]{1,0:T(8,128)}, f32[96,128]{1,0:T(8,128)S(1)}, u32[]{:S(2)}) copy-start(f32[96,128]{1,0:T(8,128)S(1)} %pad_maximum_fusion.1.r0_ref) | copy-start | bytes 147460
  207.2 5.9 %collective-permute-start.15 = (f32[96,128]{1,0:T(8,128)S(1)}, f32[96,128]{1,0:T(8,128)S(1)}, u32[]{:S(2)}, u32[]{:S(2)}) collective-permute-start(f32[96,128]{1,0:T(8,128)S(1)} %pad_maximum_fusion.1.r0_ref), channel_id=1, source_target_pairs={{0,1},{1,2},{2,3},{3,0},{4,5},{5,6},{6,7},{7,4},{8,9},{9,10},{10,1... | collective-permute-start | bytes 147464 | tf_op jit(solution)/shard_map/ppermute | solution.py:405
  208.1 5.6 %collective-permute-start.16 = (f32[96,128]{1,0:T(8,128)S(1)}, f32[96,128]{1,0:T(8,128)S(1)}, u32[]{:S(2)}, u32[]{:S(2)}) collective-permute-start(f32[96,128]{1,0:T(8,128)S(1)} %pad_maximum_fusion.1.r0_ref), channel_id=1, source_target_pairs={{0,2},{1,3},{2,0},{3,1},{4,6},{5,7},{6,4},{7,5},{8,10},{9,11},{10,... | collective-permute-start | bytes 147464 | tf_op jit(solution)/shard_map/ppermute | solution.py:405
  209.7 4.2 %collective-permute-start.17 = (f32[96,128]{1,0:T(8,128)S(1)}, f32[96,128]{1,0:T(8,128)S(1)}, u32[]{:S(2)}, u32[]{:S(2)}) collective-permute-start(f32[96,128]{1,0:T(8,128)S(1)} %pad_maximum_fusion.1.r0_ref), channel_id=1, source_target_pairs={{0,3},{1,0},{2,1},{3,2},{4,7},{5,4},{6,5},{7,6},{8,11},{9,8},{10,9... | collective-permute-start | bytes 147464 | tf_op jit(solution)/shard_map/ppermute | solution.py:405
  213.1 4.8 %copy-start.19 = (f32[96,128]{1,0:T(8,128)}, f32[96,128]{1,0:T(8,128)S(1)}, u32[]{:S(2)}) copy-start(f32[96,128]{1,0:T(8,128)S(1)} %collective-permute-done.15.r1_ref) | copy-start | bytes 147460
  213.7 4.2 %copy-start.20 = (f32[96,128]{1,0:T(8,128)}, f32[96,128]{1,0:T(8,128)S(1)}, u32[]{:S(2)}) copy-start(f32[96,128]{1,0:T(8,128)S(1)} %collective-permute-done.16.r2_ref) | copy-start | bytes 147460
  214.0 3.9 %copy-start.21 = (f32[96,128]{1,0:T(8,128)}, f32[96,128]{1,0:T(8,128)S(1)}, u32[]{:S(2)}) copy-start(f32[96,128]{1,0:T(8,128)S(1)} %collective-permute-done.17.r3_ref) | copy-start | bytes 147460
  217.9 0.9 copy-start.2

commit v4 on v3

--- a/solution.py
+++ b/solution.py
@@ -11,7 +11,7 @@
 EPSILON = 1e-05
 F32 = jnp.float32
 BF16 = jnp.bfloat16
-CHUNK = 256
+CHUNK = 512
 UNROLL = 2
 
 
@@ -133,28 +133,28 @@
     fetch = pltpu.make_async_copy(field_hbm, pad_ref.at[:, 1:9, 8:136, :], sem.at[0])
     fetch.start()
     selections(*scratch[:3])
-    pad_ref[:, 0:1, 8:136, :] = z_prev_ref[...]
-    pad_ref[:, 9:10, 8:136, :] = z_next_ref[...]
+    pad_ref[:, 0:1, 8:136, :] = z_prev_ref[...].astype(F32)
+    pad_ref[:, 9:10, 8:136, :] = z_next_ref[...].astype(F32)
     pad_ref[:, 1:9, 7:8, :] = y_prev_ref[...]
     pad_ref[:, 1:9, 136:137, :] = y_next_ref[...]
     fetch.wait()
     near = VISCOSITY * TIME_STEP
 
     def layer(z, carry):
-        for y in range(0, 128, 32):
-            along = [pad_ref[c, z + 1, 8 + y : 40 + y, :] for c in range(3)]
+        for y in range(0, 128, 16):
+            along = [pad_ref[c, z + 1, 8 + y : 24 + y, :] for c in range(3)]
             drift = [(0.5 * TIME_STEP) * v for v in along]
             ahead = [near - v for v in drift]
             behind = [near + v for v in drift]
             for c in range(3):
                 centre = along[c]
-                z_next = pad_ref[c, z + 2, 8 + y : 40 + y, :]
-                z_prev = pad_ref[c, z, 8 + y : 40 + y, :]
-                y_next = pad_ref[c, z + 1, 9 + y : 41 + y, :]
-                y_prev = pad_ref[c, z + 1, 7 + y : 39 + y, :]
+                z_next = pad_ref[c, z + 2, 8 + y : 24 + y, :]
+                z_prev = pad_ref[c, z, 8 + y : 24 + y, :]
+                y_next = pad_ref[c, z + 1, 9 + y : 25 + y, :]
+                y_prev = pad_ref[c, z + 1, 7 + y : 23 + y, :]
                 x_next = pltpu.roll(centre, 255, 1)
                 x_prev = pltpu.roll(centre, 1, 1)
-                new_ref[c, z, y : y + 32, :] = (
+                new_ref[c, z, y : y + 16, :] = (
                     (1.0 - 6.0 * near) * centre
                     + (ahead[0] * x_next + behind[0] * x_prev)
                     + (ahead[1] * y_next + behind[1] * y_prev)
@@ -305,10 +305,10 @@
         return carry
 
     lax.fori_loop(0, 512 // CHUNK, rows, 0)
-    sums_ref[0:128, :] = pack((acc_ref[0], acc_ref[1]))
-    sums_ref[128:256, :] = pack((acc_ref[2], acc_ref[3]))
+    sums_ref[0:128, :] = pack((acc_ref[0], acc_ref[1])).astype(BF16)
+    sums_ref[128:256, :] = pack((acc_ref[2], acc_ref[3])).astype(BF16)
     loss = jnp.sum(loss_ref[...], axis=(0, 1), keepdims=True) * (1.0 / 50331648)
-    sums_ref[256:264, :] = jnp.broadcast_to(loss, (8, 128))
+    sums_ref[256:272, :], sums_ref[272:288, :] = split(jnp.broadcast_to(loss, (16, 128)))
     deal = dealer(place_ref, mine_ref, theirs_ref)
     grad = dot(hidden_ref[...], d_guess_ref[...], (0, 0))
     for n in range(4):
@@ -327,8 +327,9 @@
 ):
     fetch = pltpu.make_async_copy(old_hbm.at[:, 0:1536], old_ref, sem)
     fetch.start()
-    total = (s0_ref[...] + s1_ref[...]) + (s2_ref[...] + s3_ref[...])
-    loss_ref[...] = total[256:264, :]
+    s0, s1, s2, s3 = [ref[...].astype(F32) for ref in (s0_ref, s1_ref, s2_ref, s3_ref)]
+    total = (s0 + s1) + (s2 + s3)
+    loss_ref[...] = total[256:264, :] + total[272:280, :]
     quartets(total[0:256] / count_ref[0:1, :], high_ref, low_ref)
     mix = mean_matrix()
 
@@ -432,8 +433,8 @@
     slabs = lax.axis_size("slab")
     place = jnp.stack([lax.axis_index("mp"), lax.axis_index("slab") & 1])
     up = [(i, (i + 1) % slabs) for i in range(slabs)]
-    z_prev = lax.ppermute(velocity[:, 7:8], "slab", up)
-    z_next = lax.ppermute(velocity[:, 0:1], "slab", [(j, i) for i, j in up])
+    z_prev = lax.ppermute(velocity[:, 7:8].astype(BF16), "slab", up)
+    z_next = lax.ppermute(velocity[:, 0:1].astype(BF16), "slab", [(j, i) for i, j in up])
     up = [(i, (i + 1) % 4) for i in range(4)]
     y_prev = lax.ppermute(velocity[:, :, 127:128], "mp", up)
     y_next = lax.ppermute(velocity[:, :, 0:1], "mp", [(j, i) for i, j in up])
@@ -471,7 +472,7 @@
     sums = around(sums)
     mine, theirs, d_query, d_hidden, d_sums, count = call(
         middle_kernel,
-        [((16, 4, 64, 128), BF16), ((16, 4, 64, 128), BF16), wide, wide_f, ((264, 128), F32), ((8, 128), F32)],
+        [((16, 4, 64, 128), BF16), ((16, 4, 64, 128), BF16), wide, wide_f, ((288, 128), BF16), ((8, 128), F32)],
         [
             pltpu.VMEM((512, 512), BF16),
             pltpu.VMEM((512, 1536), BF16),

time: 225 us -> 216 us (0.960)
  Pallas kernels: 49.6 us -> 46.6 us
  local copies, waits for them, and re-layouts: 7.88 us -> 4.98 us
  waiting for transfers between devices: 93 us -> 90.5 us
    ppermute x12, waiting for transfers between devices: 37 us -> 34.4 us  [around(): got.append(lax.ppermute(value, 'mp', [(i, (i + d) % 4) for i in range(4)]))]
  transfers between devices with their start and end apart: 23 -> 23, of which waited for: 15 -> 16; matrix products, arithmetic and copies ran while one was open for 4% -> 3% of each run, Pallas kernels for 14% -> 14%
where the time goes in v4:
time: 216 us; the launch traced here: 212 us
  waiting for transfers between devices  90.5 us (42%)
  starting transfers between devices  63.2 us (29%)
  Pallas kernels  46.6 us (22%)
  other arithmetic  5.83 us (3%)
  local copies, waits for them, and re-layouts  4.98 us (2%)
    all_to_all x2, waiting for transfers between devices, total(): lax.all_to_all(partial.reshape(64, -1, 128), ('slab', 'mp'), split_axis=0...  34.7 us
    ppermute x12, waiting for transfers between devices, around(): got.append(lax.ppermute(value, 'mp', [(i, (i + d) % 4) for i in range(4)]))  34.4 us
    all_to_all x3, starting transfers between devices, exchange(): return lax.all_to_all(value, axes, split_axis=0, concat_axis=0, tiled=True)  21.4 us
    ppermute x12, starting transfers between devices, around(): got.append(lax.ppermute(value, 'mp', [(i, (i + d) % 4) for i in range(4)]))  18.8 us
    all_to_all x2, starting transfers between devices, total(): lax.all_to_all(partial.reshape(64, -1, 128), ('slab', 'mp'), split_axis=0...  16.8 us
    ppermute x1, waiting for transfers between devices, step(): z_prev = lax.ppermute(velocity[:, 7:8].astype(BF16), 'slab', up)  15.6 us
    pallas_call x1, Pallas kernels, step(): call(new_kernel, [((3, 8, 128, 256), F32), ((512, 1536), BF16)], [pltpu.V...  10.3 us
    pallas_call x1, Pallas kernels, step(): call(backward_kernel, [((16, 4, 96, 128), BF16), ((16, 4, 96, 128), BF16)...  9.47 us
  transfers between devices with their start and end apart: 23, of which 16 were waited for; matrix products, arithmetic and copies ran while one was open for 3% of the time, Pallas kernels for 14%

profile of v4, /device:TPU:6, one launch (start us, length us, event | category | flops | bytes accessed | tf_op | source)
XLA Modules:
  0.0 212.1 jit_solution(16669393425051362553)
XLA Ops:
  0.6 7.1 %shard_map.152 = (bf16[512,1664]{1,0:T(8,128)(2,1)}, bf16[256,512]{1,0:T(8,128)(2,1)}, bf16[512,256]{1,0:T(8,128)(2,1)}) custom-call(f32[3,8,128,256]{3,2,1,0:T(8,128)} %field_hbm.3, s32[3,1,256]{2,1,0:T(1,128)} %bitcast.22, s32[1,256]{1,0:T(1,128)} %bitcast.23), custom_call_target="tpu_custom_call" | custom-call | tf_op jit(solution)/shard_map/pallas_call | solution.py:444
  7.7 0.0 copy-start
  7.7 7.9 %all-to-all-start = ((bf16[32,16,1664]{2,1,0:T(8,128)(2,1)}), bf16[32,16,1664]{2,1,0:T(8,128)(2,1)}, u32[]{:S(2)}, u32[]{:S(2)}) async-start(bf16[32,16,1664]{2,1,0:T(8,128)(2,1)} %bitcast.17), calls=%async_computation | async-start | bytes 3407872 | tf_op jit(solution)/shard_map/all_to_all | solution.py:411
  15.6 0.2 convert.12
  15.9 0.2 collective-permute-start
  16.1 1.6 collective-permute-start.1
  17.7 2.0 collective-permute-start.2
  19.7 2.2 %collective-permute-start.3 = (f32[3,8,1,256]{3,2,1,0:T(1,128)S(1)}, f32[3,8,1,256]{3,2,1,0:T(1,128)S(1)}, u32[]{:S(2)}, u32[]{:S(2)}) collective-permute-start(f32[3,8,1,256]{3,2,1,0:T(1,128)S(1)} %get-tuple-element.74), channel_id=1, source_target_pairs={{1,0},{2,1},{3,2},{0,3},{5,4},{6,5},{7,6},{4,7},{9,8},{10,9},{11,1... | collective-permute-start | bytes 73736 | tf_op jit(solution)/shard_map/ppermute | solution.py:440
  21.9 1.7 collective-permute-done.2.y_prev_ref
  23.6 15.6 %collective-permute-done.z_prev_ref = bf16[3,1,128,256]{3,2,1,0:T(8,128)(2,1)S(1)} collective-permute-done((bf16[3,1,128,256]{3,2,1,0:T(8,128)(2,1)S(1)}, bf16[3,1,128,256]{3,2,1,0:T(8,128)(2,1)S(1)}, u32[]{:S(2)}, u32[]{:S(2)}) %collective-permute-start) | collective-permute-done | bytes 196640 | tf_op jit(solution)/shard_map/ppermute | solution.py:436
  39.3 0.7 copy-done.8
  40.0 0.1 copy-done.9
  40.0 10.3 %shard_map.153 = (f32[3,8,128,256]{3,2,1,0:T(8,128)}, bf16[512,1536]{1,0:T(8,128)(2,1)}) custom-call(f32[3,8,128,256]{3,2,1,0:T(8,128)} %field_hbm.3, bf16[3,1,128,256]{3,2,1,0:T(8,128)(2,1)} %copy-done.8, bf16[3,1,128,256]{3,2,1,0:T(8,128)(2,1)} %copy-done.9, f32[3,8,1,256]{3,2,1,0:T(1,128)} %copy-done.24, f32[3,8,1,256]{3,2,1,0:T(1,128)} %copy-done.25, ...), custom_call_target="tpu_custom_call" | custom-call | tf_op jit(solution)/shard_map/pallas_call | solution.py:451
  50.4 0.0 copy-start.14
  50.4 0.0 copy-start.15
  50.4 7.0 %all-to-all-start.1 = ((bf16[32,16,1536]{2,1,0:T(8,128)(2,1)}), bf16[32,16,1536]{2,1,0:T(8,128)(2,1)S(1)}, u32[]{:S(2)}, u32[]{:S(2)}) async-start(bf16[32,16,1536]{2,1,0:T(8,128)(2,1)} %bitcast.18), calls=%async_computation.1 | async-start | bytes 3145728 | tf_op jit(solution)/shard_map/all_to_all | solution.py:411
  57.6 0.1 pad_maximum_fusion.w0_ref
  57.7 2.0 collective-permute-start.4
  59.7 3.6 %collective-permute-start.5 = (bf16[4,512,128]{2,1,0:T(8,128)(2,1)S(1)}, bf16[4,512,128]{2,1,0:T(8,128)(2,1)S(1)}, u32[]{:S(2)}, u32[]{:S(2)}) collective-permute-start(bf16[4,512,128]{2,1,0:T(8,128)(2,1)S(1)} %pad_maximum_fusion.w0_ref), channel_id=1, source_target_pairs={{0,2},{1,3},{2,0},{3,1},{4,6},{5,7},{6,4},{7,5},{8,10},{9,11},{10,... | collective-permute-start | bytes 1572872 | tf_op jit(solution)/shard_map/ppermute | solution.py:406
  63.2 1.0 collective-permute-start.6
  64.2 0.6 pad_add_fusion.place_ref
  64.9 9.1 %collective-permute-done.4.w1_ref = bf16[4,512,128]{2,1,0:T(8,128)(2,1)S(1)} collective-permute-done((bf16[4,512,128]{2,1,0:T(8,128)(2,1)S(1)}, bf16[4,512,128]{2,1,0:T(8,128)(2,1)S(1)}, u32[]{:S(2)}, u32[]{:S(2)}) %collective-permute-start.4) | collective-permute-done | bytes 524320 | tf_op jit(solution)/shard_map/ppermute | solution.py:406
  74.0 12.4 %collective-permute-done.5.w2_ref = bf16[4,512,128]{2,1,0:T(8,128)(2,1)S(1)} collective-permute-done((bf16[4,512,128]{2,1,0:T(8,128)(2,1)S(1)}, bf16[4,512,128]{2,1,0:T(8,128)(2,1)S(1)}, u32[]{:S(2)}, u32[]{:S(2)}) %collective-permute-start.5) | collective-permute-done | bytes 524320 | tf_op jit(solution)/shard_map/ppermute | solution.py:406
  86.4 0.8 copy-done.7
  87.2 8.8 %shard_map.154 = (bf16[512,512]{1,0:T(8,128)(2,1)}, bf16[512,512]{1,0:T(8,128)(2,1)}, bf16[512,512]{1,0:T(8,128)(2,1)}, f32[512,512]{1,0:T(8,128)}, bf16[512,512...) custom-call(s32[2]{0:T(128)} %pad_add_fusion.place_ref, ...), custom_call_target="tpu_custom_call" | custom-call | tf_op jit(solution)/shard_map/pallas_call | solution.py:466
  96.0 0.6 collective-permute-start.7
  96.6 2.4 %collective-permute-start.8 = (f32[264,128]{1,0:T(8,128)}, f32[264,128]{1,0:T(8,128)S(1)}, u32[]{:S(2)}, u32[]{:S(2)}) collective-permute-start(f32[264,128]{1,0:T(8,128)} %get-tuple-element.44.s0_ref), channel_id=1, source_target_pairs={{0,2},{1,3},{2,0},{3,1},{4,6},{5,7},{6,4},{7,5},{8,10},{9,11},{10,... | collective-permute-start | bytes 405512 | tf_op jit(solution)/shard_map/ppermute | solution.py:406
  99.0 1.3 collective-permute-start.9
  100.2 3.0 %collective-permute-done.7.s1_ref = f32[264,128]{1,0:T(8,128)S(1)} collective-permute-done((f32[264,128]{1,0:T(8,128)}, f32[264,128]{1,0:T(8,128)S(1)}, u32[]{:S(2)}, u32[]{:S(2)}) %collective-permute-start.7) | collective-permute-done | bytes 135200 | tf_op jit(solution)/shard_map/ppermute | solution.py:406
  103.2 2.4 %collective-permute-done.8.s2_ref = f32[264,128]{1,0:T(8,128)S(1)} collective-permute-done((f32[264,128]{1,0:T(8,128)}, f32[264,128]{1,0:T(8,128)S(1)}, u32[]{:S(2)}, u32[]{:S(2)}) %collective-permute-start.8) | collective-permute-done | bytes 135200 | tf_op jit(solution)/shard_map/ppermute | solution.py:406
  105.6 0.1 collective-permute-done.9.s3_ref
  105.7 0.5 copy-done.12
  106.2 0.1 copy-done.13
  106.3 8.6 %shard_map.155 = (bf16[16,4,64,128]{3,2,1,0:T(8,128)(2,1)}, bf16[16,4,64,128]{3,2,1,0:T(8,128)(2,1)}, bf16[512,512]{1,0:T(8,128)(2,1)}, f32[512,512]{1,0:T(8,128...) custom-call(s32[2]{0:T(128)} %pad_add_fusion.place_ref, f32[264,128]{1,0:T(8,128)} %get-tuple-element.44.s0_ref, ...), custom_call_target="tpu_custom_call" | custom-call | tf_op jit(solution)/shard_map/pallas_call | solution.py:473
  115.0 0.0 collective-permute-start.14
  115.0 0.8 collective-permute-start.10
  115.8 3.4 %collective-permute-start.11 = (bf16[288,128]{1,0:T(8,128)(2,1)}, bf16[288,128]{1,0:T(8,128)(2,1)S(1)}, u32[]{:S(2)}, u32[]{:S(2)}) collective-permute-start(bf16[288,128]{1,0:T(8,128)(2,1)} %get-tuple-element.49.s0_ref), channel_id=1, source_target_pairs={{0,2},{1,3},{2,0},{3,1},{4,6},{5,7},{6,4},{7,5},{8,10},{9,11},{10,... | collective-permute-start | bytes 221192 | tf_op jit(solution)/shard_map/ppermute | solution.py:406
  119.2 1.9 collective-permute-done.10.s1_ref
  121.1 2.5 %collective-permute-done.11.s2_ref = bf16[288,128]{1,0:T(8,128)(2,1)S(1)} collective-permute-done((bf16[288,128]{1,0:T(8,128)(2,1)}, bf16[288,128]{1,0:T(8,128)(2,1)S(1)}, u32[]{:S(2)}, u32[]{:S(2)}) %collective-permute-start.11) | collective-permute-done | bytes 73760 | tf_op jit(solution)/shard_map/ppermute | solution.py:406
  123.6 0.2 collective-permute-done.12.s3_ref
  123.8 0.4 copy-done.19
  124.2 0.2 copy-done.20
  124.4 9.5 %shard_map.156 = (bf16[16,4,96,128]{3,2,1,0:T(8,128)(2,1)}, bf16[16,4,96,128]{3,2,1,0:T(8,128)(2,1)}, f32[8,128]{1,0:T(8,128)}) custom-call(s32[2]{0:T(128)} %pad_add_fusion.place_ref, bf16[288,128]{1,0:T(8,128)(2,1)} %get-tuple-element.49.s0_ref, bf16[288,128]{1,0:T(8,128)(2,1)} %copy-done.18, bf16[288,128]{1,0:T(8,128)(2,1)} %copy-done.19, ...), custom_call_target="tpu_custom_call" | custom-call | tf_op jit(solution)/shard_map/pallas_call | solution.py:490
  133.9 0.1 collective-permute-start.13
  134.0 1.4 add_convert_fusion.1
  135.4 9.5 %all-to-all-start.3 = ((bf16[64,64,128]{2,1,0:T(8,128)(2,1)}), bf16[64,64,128]{2,1,0:T(8,128)(2,1)S(1)}, u32[]{:S(2)}, u32[]{:S(2)}) async-start(bf16[64,64,128]{2,1,0:T(8,128)(2,1)} %bitcast.13), calls=%async_computation.3 | async-start | bytes 2097152 | tf_op jit(solution)/shard_map/all_to_all | solution.py:421
  145.0 3.1 %add_convert_fusion = bf16[16,4,96,128]{3,2,1,0:T(8,128)(2,1)} fusion(bf16[16,4,96,128]{3,2,1,0:T(8,128)(2,1)} %collective-permute-done.13, bf16[16,4,96,128]{3,2,1,0:T(8,128)(2,1)S(1)} %copy-done.4), kind=kLoop, calls=%fused_computation.1 | loop fusion | flops 3145728 | bytes 4718592 | tf_op jit(solution)/shard_map/convert_element_type | solution.py:416
  148.0 13.9 %all-to-all-done.3 = bf16[64,64,128]{2,1,0:T(8,128)(2,1)S(1)} async-done(((bf16[64,64,128]{2,1,0:T(8,128)(2,1)}), bf16[64,64,128]{2,1,0:T(8,128)(2,1)S(1)}, u32[]{:S(2)}, u32[]{:S(2)}) %all-to-all-start.3) | async-done | bytes 1048608 | tf_op jit(solution)/shard_map/all_to_all | solution.py:421
  161.9 7.3 %all-to-all-start.2 = ((bf16[64,96,128]{2,1,0:T(8,128)(2,1)}), bf16[64,96,128]{2,1,0:T(8,128)(2,1)S(1)}, u32[]{:S(2)}, u32[]{:S(2)}) async-start(bf16[64,96,128]{2,1,0:T(8,128)(2,1)} %bitcast.12), calls=%async_computation.2 | async-start | bytes 3145728 | tf_op jit(solution)/shard_map/all_to_all | solution.py:421
  169.2 0.2 convert_reduce_fusion.1
  169.4 20.9 %all-to-all-done.2 = bf16[64,96,128]{2,1,0:T(8,128)(2,1)S(1)} async-done(((bf16[64,96,128]{2,1,0:T(8,128)(2,1)}), bf16[64,96,128]{2,1,0:T(8,128)(2,1)S(1)}, u32[]{:S(2)}, u32[]{:S(2)}) %all-to-all-start.2) | async-done | bytes 1572896 | tf_op jit(solution)/shard_map/all_to_all | solution.py:421
  190.3 0.2 convert_reduce_fusion
  190.5 0.2 concatenate.14
  190.7 1.0 broadcast_in_dim.10
  191.7 6.5 %all-to-all-start.4 = ((bf16[32,80,128]{2,1,0:T(8,128)(2,1)}), bf16[32,80,128]{2,1,0:T(8,128)(2,1)S(1)}, u32[]{:S(2)}, u32[]{:S(2)}) async-start(bf16[32,80,128]{2,1,0:T(8,128)(2,1)} %broadcast_in_dim.10), calls=%async_computation.4 | async-start | bytes 1310720 | tf_op jit(solution)/shard_map/all_to_all | solution.py:411
  198.3 0.9 collective-permute-start.15
  199.2 1.6 collective-permute-start.16
  200.8 1.3 collective-permute-start.17
  202.1 2.1 collective-permute-done.15.r1_ref
  204.2 0.6 collective-permute-done.16.r2_ref
  204.8 0.3 collective-permute-done.17.r3_ref
  205.0 3.9 %all-to-all-done.4.heads_ref = bf16[32,80,128]{2,1,0:T(8,128)(2,1)S(1)} async-done(((bf16[32,80,128]{2,1,0:T(8,128)(2,1)}), bf16[32,80,128]{2,1,0:T(8,128)(2,1)S(1)}, u32[]{:S(2)}, u32[]{:S(2)}) %all-to-all-start.4) | async-done | bytes 655392 | tf_op jit(solution)/shard_map/all_to_all | solution.py:411
  209.0 0.9 copy-done.2
  209.9 2.3 %shard_map.157 = (f32[48,512]{1,0:T(8,128)}, f32[512,128]{1,0:T(8,128)}, f32[512,128]{1,0:T(8,128)}, f32[512,128]{1,0:T(8,128)}, f32[128,512]{1,0:T(8,128)}, /*index=5*/f32[16,1536]{1,0:T(8,128)}, f32[1,1]{1,0:T(1,128)}) custom-call(s32[2]{0:T(128)} %pad_add_fusion.place_ref, f32[96,128]{1,0:T(8,128)} %copy-done.10, f32[96,128]{1,0:T(8,128)} %copy-done.21, ...), custom_call_target="tpu_custom_call" | custom-call | tf_op jit(solution)/shard_map/pallas_call | solution.py:510
  (64 shorter events, 0.2 us)
Async XLA Ops:
  7.7 7.9 %copy-start = (f32[3,8,128,256]{3,2,1,0:T(8,128)S(1)}, f32[3,8,128,256]{3,2,1,0:T(8,128)}, u32[]{:S(2)}) copy-start(f32[3,8,128,256]{3,2,1,0:T(8,128)} %field_hbm.3) | copy-start | bytes 9437188
  7.7 42.7 %all-to-all-start = ((bf16[32,16,1664]{2,1,0:T(8,128)(2,1)}), bf16[32,16,1664]{2,1,0:T(8,128)(2,1)}, u32[]{:S(2)}, u32[]{:S(2)}) async-start(bf16[32,16,1664]{2,1,0:T(8,128)(2,1)} %bitcast.17), calls=%async_computation | async-start | bytes 3407872 | tf_op jit(solution)/shard_map/all_to_all | solution.py:411
  15.9 23.4 %collective-permute-start = (bf16[3,1,128,256]{3,2,1,0:T(8,128)(2,1)S(1)}, bf16[3,1,128,256]{3,2,1,0:T(8,128)(2,1)S(1)}, u32[]{:S(2)}, u32[]{:S(2)}) collective-permute-start(bf16[3,1,128,256]{3,2,1,0:T(8,128)(2,1)S(1)} %get-tuple-element.77), channel_id=1, source_target_pairs={{0,4},{4,8},{8,12},{12,16},{16,20},{20,24},{24,28},{28,32},{32,36}... | collective-permute-start | bytes 589832 | tf_op jit(solution)/shard_map/ppermute | solution.py:436
  16.1 23.2 %collective-permute-start.1 = (bf16[3,1,128,256]{3,2,1,0:T(8,128)(2,1)S(1)}, bf16[3,1,128,256]{3,2,1,0:T(8,128)(2,1)S(1)}, u32[]{:S(2)}, u32[]{:S(2)}) collective-permute-start(bf16[3,1,128,256]{3,2,1,0:T(8,128)(2,1)S(1)} %get-tuple-element.76), channel_id=1, source_target_pairs={{4,0},{8,4},{12,8},{16,12},{20,16},{24,20},{28,24},{32,28},{36,32}... | collective-permute-start | bytes 589832 | tf_op jit(solution)/shard_map/ppermute | solution.py:437
  17.7 5.9 %collective-permute-start.2 = (f32[3,8,1,256]{3,2,1,0:T(1,128)S(1)}, f32[3,8,1,256]{3,2,1,0:T(1,128)S(1)}, u32[]{:S(2)}, u32[]{:S(2)}) collective-permute-start(f32[3,8,1,256]{3,2,1,0:T(1,128)S(1)} %get-tuple-element.75), channel_id=1, source_target_pairs={{0,1},{1,2},{2,3},{3,0},{4,5},{5,6},{6,7},{7,4},{8,9},{9,10},{10,1... | collective-permute-start | bytes 73736 | tf_op jit(solution)/shard_map/ppermute | solution.py:439
  19.7 3.9 %collective-permute-start.3 = (f32[3,8,1,256]{3,2,1,0:T(1,128)S(1)}, f32[3,8,1,256]{3,2,1,0:T(1,128)S(1)}, u32[]{:S(2)}, u32[]{:S(2)}) collective-permute-start(f32[3,8,1,256]{3,2,1,0:T(1,128)S(1)} %get-tuple-element.74), channel_id=1, source_target_pairs={{1,0},{2,1},{3,2},{0,3},{5,4},{6,5},{7,6},{4,7},{9,8},{10,9},{11,1... | collective-permute-start | bytes 73736 | tf_op jit(solution)/shard_map/ppermute | solution.py:440
  23.6 15.7 %copy-start.24 = (f32[3,8,1,256]{3,2,1,0:T(1,128)}, f32[3,8,1,256]{3,2,1,0:T(1,128)S(1)}, u32[]{:S(2)}) copy-start(f32[3,8,1,256]{3,2,1,0:T(1,128)S(1)} %collective-permute-done.2.y_prev_ref) | copy-start | bytes 73732
  23.6 15.7 %copy-start.25 = (f32[3,8,1,256]{3,2,1,0:T(1,128)}, f32[3,8,1,256]{3,2,1,0:T(1,128)S(1)}, u32[]{:S(2)}) copy-start(f32[3,8,1,256]{3,2,1,0:T(1,128)S(1)} %collective-permute-done.3.y_next_ref) | copy-start | bytes 73732
  39.3 0.7 copy-start.8
  39.3 0.7 copy-start.9
  50.4 7.1 %copy-start.14 = (bf16[128,512]{1,0:T(8,128)(2,1)S(1)}, bf16[128,512]{1,0:T(8,128)(2,1)}, u32[]{:S(2)}) copy-start(bf16[128,512]{1,0:T(8,128)(2,1)} %param.16) | copy-start | bytes 393220
  50.4 7.1 %copy-start.15 = (bf16[512,128]{1,0:T(8,128)(2,1)S(1)}, bf16[512,128]{1,0:T(8,128)(2,1)}, u32[]{:S(2)}) copy-start(bf16[512,128]{1,0:T(8,128)(2,1)} %param.15) | copy-start | bytes 393220
  50.4 7.1 %copy-start.16 = (bf16[512,128]{1,0:T(8,128)(2,1)S(1)}, bf16[512,128]{1,0:T(8,128)(2,1)}, u32[]{:S(2)}) copy-start(bf16[512,128]{1,0:T(8,128)(2,1)} %param.14) | copy-start | bytes 393220
  50.4 7.1 %copy-start.17 = (bf16[512,128]{1,0:T(8,128)(2,1)S(1)}, bf16[512,128]{1,0:T(8,128)(2,1)}, u32[]{:S(2)}) copy-start(bf16[512,128]{1,0:T(8,128)(2,1)} %param.13) | copy-start | bytes 393220
  50.4 49.8 %all-to-all-start.1 = ((bf16[32,16,1536]{2,1,0:T(8,128)(2,1)}), bf16[32,16,1536]{2,1,0:T(8,128)(2,1)S(1)}, u32[]{:S(2)}, u32[]{:S(2)}) async-start(bf16[32,16,1536]{2,1,0:T(8,128)(2,1)} %bitcast.18), calls=%async_computation.1 | async-start | bytes 3145728 | tf_op jit(solution)/shard_map/all_to_all | solution.py:411
  57.6 28.7 %copy-start.3 = (bf16[4,512,128]{2,1,0:T(8,128)(2,1)}, bf16[4,512,128]{2,1,0:T(8,128)(2,1)S(1)}, u32[]{:S(2)}) copy-start(bf16[4,512,128]{2,1,0:T(8,128)(2,1)S(1)} %pad_maximum_fusion.w0_ref) | copy-start | bytes 1572868
  57.7 16.3 %collective-permute-start.4 = (bf16[4,512,128]{2,1,0:T(8,128)(2,1)S(1)}, bf16[4,512,128]{2,1,0:T(8,128)(2,1)S(1)}, u32[]{:S(2)}, u32[]{:S(2)}) collective-permute-start(bf16[4,512,128]{2,1,0:T(8,128)(2,1)S(1)} %pad_maximum_fusion.w0_ref), channel_id=1, source_target_pairs={{0,1},{1,2},{2,3},{3,0},{4,5},{5,6},{6,7},{7,4},{8,9},{9,10},{10,1... | collective-permute-start | bytes 1572872 | tf_op jit(solution)/shard_map/ppermute | solution.py:406
  59.7 26.7 %collective-permute-start.5 = (bf16[4,512,128]{2,1,0:T(8,128)(2,1)S(1)}, bf16[4,512,128]{2,1,0:T(8,128)(2,1)S(1)}, u32[]{:S(2)}, u32[]{:S(2)}) collective-permute-start(bf16[4,512,128]{2,1,0:T(8,128)(2,1)S(1)} %pad_maximum_fusion.w0_ref), channel_id=1, source_target_pairs={{0,2},{1,3},{2,0},{3,1},{4,6},{5,7},{6,4},{7,5},{8,10},{9,11},{10,... | collective-permute-start | bytes 1572872 | tf_op jit(solution)/shard_map/ppermute | solution.py:406
  63.2 23.2 %collective-permute-start.6 = (bf16[4,512,128]{2,1,0:T(8,128)(2,1)S(1)}, bf16[4,512,128]{2,1,0:T(8,128)(2,1)}, u32[]{:S(2)}, u32[]{:S(2)}) collective-permute-start(bf16[4,512,128]{2,1,0:T(8,128)(2,1)S(1)} %pad_maximum_fusion.w0_ref), channel_id=1, source_target_pairs={{0,3},{1,0},{2,1},{3,2},{4,7},{5,4},{6,5},{7,6},{8,11},{9,8},{10,9... | collective-permute-start | bytes 1572872 | tf_op jit(solution)/shard_map/ppermute | solution.py:406
  74.0 12.4 %copy-start.6 = (bf16[4,512,128]{2,1,0:T(8,128)(2,1)}, bf16[4,512,128]{2,1,0:T(8,128)(2,1)S(1)}, u32[]{:S(2)}) copy-start(bf16[4,512,128]{2,1,0:T(8,128)(2,1)S(1)} %collective-permute-done.4.w1_ref) | copy-start | bytes 1572868
  86.4 0.8 copy-start.7
  96.0 7.2 %collective-permute-start.7 = (f32[264,128]{1,0:T(8,128)}, f32[264,128]{1,0:T(8,128)S(1)}, u32[]{:S(2)}, u32[]{:S(2)}) collective-permute-start(f32[264,128]{1,0:T(8,128)} %get-tuple-element.44.s0_ref), channel_id=1, source_target_pairs={{0,1},{1,2},{2,3},{3,0},{4,5},{5,6},{6,7},{7,4},{8,9},{9,10},{10,1... | collective-permute-start | bytes 405512 | tf_op jit(solution)/shard_map/ppermute | solution.py:406
  96.6 9.0 %collective-permute-start.8 = (f32[264,128]{1,0:T(8,128)}, f32[264,128]{1,0:T(8,128)S(1)}, u32[]{:S(2)}, u32[]{:S(2)}) collective-permute-start(f32[264,128]{1,0:T(8,128)} %get-tuple-element.44.s0_ref), channel_id=1, source_target_pairs={{0,2},{1,3},{2,0},{3,1},{4,6},{5,7},{6,4},{7,5},{8,10},{9,11},{10,... | collective-permute-start | bytes 405512 | tf_op jit(solution)/shard_map/ppermute | solution.py:406
  99.0 6.7 %collective-permute-start.9 = (f32[264,128]{1,0:T(8,128)}, f32[264,128]{1,0:T(8,128)S(1)}, u32[]{:S(2)}, u32[]{:S(2)}) collective-permute-start(f32[264,128]{1,0:T(8,128)} %get-tuple-element.44.s0_ref), channel_id=1, source_target_pairs={{0,3},{1,0},{2,1},{3,2},{4,7},{5,4},{6,5},{7,6},{8,11},{9,8},{10,9... | collective-permute-start | bytes 405512 | tf_op jit(solution)/shard_map/ppermute | solution.py:406
  100.2 5.4 %copy-start.1 = (bf16[32,16,1536]{2,1,0:T(8,128)(2,1)}, bf16[32,16,1536]{2,1,0:T(8,128)(2,1)S(1)}, u32[]{:S(2)}) copy-start(bf16[32,16,1536]{2,1,0:T(8,128)(2,1)S(1)} %all-to-all-done.1) | copy-start | bytes 4718596
  103.2 2.5 %copy-start.11 = (f32[264,128]{1,0:T(8,128)}, f32[264,128]{1,0:T(8,128)S(1)}, u32[]{:S(2)}) copy-start(f32[264,128]{1,0:T(8,128)S(1)} %collective-permute-done.7.s1_ref) | copy-start | bytes 405508
  105.6 0.7 copy-start.12
  105.7 0.7 copy-start.13
  115.0 19.0 %collective-permute-start.14 = (bf16[16,4,64,128]{3,2,1,0:T(8,128)(2,1)}, bf16[16,4,64,128]{3,2,1,0:T(8,128)(2,1)S(1)}, u32[]{:S(2)}, u32[]{:S(2)}) collective-permute-start(bf16[16,4,64,128]{3,2,1,0:T(8,128)(2,1)} %get-tuple-element.63), channel_id=1, source_target_pairs={{0,4},{4,0},{8,12},{12,8},{16,20},{20,16},{24,28},{28,24},{32,36},... | collective-permute-start | bytes 3145736 | tf_op jit(solution)/shard_map/ppermute | solution.py:415
  115.0 6.1 %collective-permute-start.10 = (bf16[288,128]{1,0:T(8,128)(2,1)}, bf16[288,128]{1,0:T(8,128)(2,1)S(1)}, u32[]{:S(2)}, u32[]{:S(2)}) collective-permute-start(bf16[288,128]{1,0:T(8,128)(2,1)} %get-tuple-element.49.s0_ref), channel_id=1, source_target_pairs={{0,1},{1,2},{2,3},{3,0},{4,5},{5,6},{6,7},{7,4},{8,9},{9,10},{10,1... | collective-permute-start | bytes 221192 | tf_op jit(solution)/shard_map/ppermute | solution.py:406
  115.8 7.7 %collective-permute-start.11 = (bf16[288,128]{1,0:T(8,128)(2,1)}, bf16[288,128]{1,0:T(8,128)(2,1)S(1)}, u32[]{:S(2)}, u32[]{:S(2)}) collective-permute-start(bf16[288,128]{1,0:T(8,128)(2,1)} %get-tuple-element.49.s0_ref), channel_id=1, source_target_pairs={{0,2},{1,3},{2,0},{3,1},{4,6},{5,7},{6,4},{7,5},{8,10},{9,11},{10,... | collective-permute-start | bytes 221192 | tf_op jit(solution)/shard_map/ppermute | solution.py:406
  119.2 4.6 %collective-permute-start.12 = (bf16[288,128]{1,0:T(8,128)(2,1)}, bf16[288,128]{1,0:T(8,128)(2,1)S(1)}, u32[]{:S(2)}, u32[]{:S(2)}) collective-permute-start(bf16[288,128]{1,0:T(8,128)(2,1)} %get-tuple-element.49.s0_ref), channel_id=1, source_target_pairs={{0,3},{1,0},{2,1},{3,2},{4,7},{5,4},{6,5},{7,6},{8,11},{9,8},{10,9... | collective-permute-start | bytes 221192 | tf_op jit(solution)/shard_map/ppermute | solution.py:406
  121.1 2.7 %copy-start.18 = (bf16[288,128]{1,0:T(8,128)(2,1)}, bf16[288,128]{1,0:T(8,128)(2,1)S(1)}, u32[]{:S(2)}) copy-start(bf16[288,128]{1,0:T(8,128)(2,1)S(1)} %collective-permute-done.10.s1_ref) | copy-start | bytes 221188
  123.6 0.6 copy-start.19
  123.7 0.6 copy-start.20
  124.4 9.6 %copy-start.5 = (bf16[16,4,64,128]{3,2,1,0:T(8,128)(2,1)S(1)}, bf16[16,4,64,128]{3,2,1,0:T(8,128)(2,1)}, u32[]{:S(2)}) copy-start(bf16[16,4,64,128]{3,2,1,0:T(8,128)(2,1)} %get-tuple-element.62) | copy-start | bytes 3145732
  133.9 11.1 %collective-permute-start.13 = (bf16[16,4,96,128]{3,2,1,0:T(8,128)(2,1)}, bf16[16,4,96,128]{3,2,1,0:T(8,128)(2,1)}, u32[]{:S(2)}, u32[]{:S(2)}) collective-permute-start(bf16[16,4,96,128]{3,2,1,0:T(8,128)(2,1)} %get-tuple-element.61), channel_id=1, source_target_pairs={{0,4},{4,0},{8,12},{12,8},{16,20},{20,16},{24,28},{28,24},{32,36},... | collective-permute-start | bytes 4718600 | tf_op jit(solution)/shard_map/ppermute | solution.py:415
  135.4 9.6 %copy-start.4 = (bf16[16,4,96,128]{3,2,1,0:T(8,128)(2,1)S(1)}, bf16[16,4,96,128]{3,2,1,0:T(8,128)(2,1)}, u32[]{:S(2)}) copy-start(bf16[16,4,96,128]{3,2,1,0:T(8,128)(2,1)} %get-tuple-element.60) | copy-start | bytes 4718596
  135.4 26.5 %all-to-all-start.3 = ((bf16[64,64,128]{2,1,0:T(8,128)(2,1)}), bf16[64,64,128]{2,1,0:T(8,128)(2,1)S(1)}, u32[]{:S(2)}, u32[]{:S(2)}) async-start(bf16[64,64,128]{2,1,0:T(8,128)(2,1)} %bitcast.13), calls=%async_computation.3 | async-start | bytes 2097152 | tf_op jit(solution)/shard_map/all_to_all | solution.py:421
  161.9 7.3 %copy-start.26 = (f32[8,128]{1,0:T(8,128)S(1)}, f32[8,128]{1,0:T(8,128)}, u32[]{:S(2)}) copy-start(f32[8,128]{1,0:T(8,128)} %get-tuple-element.64) | copy-start | bytes 12292
  161.9 28.4 %all-to-all-start.2 = ((bf16[64,96,128]{2,1,0:T(8,128)(2,1)}), bf16[64,96,128]{2,1,0:T(8,128)(2,1)S(1)}, u32[]{:S(2)}, u32[]{:S(2)}) async-start(bf16[64,96,128]{2,1,0:T(8,128)(2,1)} %bitcast.12), calls=%async_computation.2 | async-start | bytes 3145728 | tf_op jit(solution)/shard_map/all_to_all | solution.py:421
  191.7 17.3 %all-to-all-start.4 = ((bf16[32,80,128]{2,1,0:T(8,128)(2,1)}), bf16[32,80,128]{2,1,0:T(8,128)(2,1)S(1)}, u32[]{:S(2)}, u32[]{:S(2)}) async-start(bf16[32,80,128]{2,1,0:T(8,128)(2,1)} %broadcast_in_dim.10), calls=%async_computation.4 | async-start | bytes 1310720 | tf_op jit(solution)/shard_map/all_to_all | solution.py:411
  198.3 10.7 %copy-start.10 = (f32[96,128]{1,0:T(8,128)}, f32[96,128]{1,0:T(8,128)S(1)}, u32[]{:S(2)}) copy-start(f32[96,128]{1,0:T(8,128)S(1)} %pad_maximum_fusion.1.r0_ref) | copy-start | bytes 147460
  198.3 5.9 %collective-permute-start.15 = (f32[96,128]{1,0:T(8,128)S(1)}, f32[96,128]{1,0:T(8,128)S(1)}, u32[]{:S(2)}, u32[]{:S(2)}) collective-permute-start(f32[96,128]{1,0:T(8,128)S(1)} %pad_maximum_fusion.1.r0_ref), channel_id=1, source_target_pairs={{0,1},{1,2},{2,3},{3,0},{4,5},{5,6},{6,7},{7,4},{8,9},{9,10},{10,1... | collective-permute-start | bytes 147464 | tf_op jit(solution)/shard_map/ppermute | solution.py:406
  199.2 5.6 %collective-permute-start.16 = (f32[96,128]{1,0:T(8,128)S(1)}, f32[96,128]{1,0:T(8,128)S(1)}, u32[]{:S(2)}, u32[]{:S(2)}) collective-permute-start(f32[96,128]{1,0:T(8,128)S(1)} %pad_maximum_fusion.1.r0_ref), channel_id=1, source_target_pairs={{0,2},{1,3},{2,0},{3,1},{4,6},{5,7},{6,4},{7,5},{8,10},{9,11},{10,... | collective-permute-start | bytes 147464 | tf_op jit(solution)/shard_map/ppermute | solution.py:406
  200.8 4.2 %collective-permute-start.17 = (f32[96,128]{1,0:T(8,128)S(1)}, f32[96,128]{1,0:T(8,128)S(1)}, u32[]{:S(2)}, u32[]{:S(2)}) collective-permute-start(f32[96,128]{1,0:T(8,128)S(1)} %pad_maximum_fusion.1.r0_ref), channel_id=1, source_target_pairs={{0,3},{1,0},{2,1},{3,2},{4,7},{5,4},{6,5},{7,6},{8,11},{9,8},{10,9... | collective-permute-start | bytes 147464 | tf_op jit(solution)/shard_map/ppermute | solution.py:406
  204.2 4.8 %copy-start.21 = (f32[96,128]{1,0:T(8,128)}, f32[96,128]{1,0:T(8,128)S(1)}, u32[]{:S(2)}) copy-start(f32[96,128]{1,0:T(8,128)S(1)} %collective-permute-done.15.r1_ref) | copy-start | bytes 147460
  204.8 4.2 %copy-start.22 = (f32[96,128]{1,0:T(8,128)}, f32[96,128]{1,0:T(8,128)S(1)}, u32[]{:S(2)}) copy-start(f32[96,128]{1,0:T(8,128)S(1)} %collective-permute-done.16.r2_ref) | copy-start | bytes 147460
  205.0 3.9 %copy-start.23 = (f32[96,128]{1,0:T(8,128)}, f32[96,128]{1,0:T(8,128)S(1)}, u32[]{:S(2)}) copy-start(f32[96,128]{1,0:T(8,128)S(1)} %collective-permute-done.17.r3_ref) | copy-start | bytes 147460
  209.0 0.9 copy-start.2

commit v5 on v3

--- a/solution.py
+++ b/solution.py
@@ -11,7 +11,7 @@
 EPSILON = 1e-05
 F32 = jnp.float32
 BF16 = jnp.bfloat16
-CHUNK = 256
+CHUNK = 512
 UNROLL = 2
 
 
@@ -141,20 +141,20 @@
     near = VISCOSITY * TIME_STEP
 
     def layer(z, carry):
-        for y in range(0, 128, 32):
-            along = [pad_ref[c, z + 1, 8 + y : 40 + y, :] for c in range(3)]
+        for y in range(0, 128, 16):
+            along = [pad_ref[c, z + 1, 8 + y : 24 + y, :] for c in range(3)]
             drift = [(0.5 * TIME_STEP) * v for v in along]
             ahead = [near - v for v in drift]
             behind = [near + v for v in drift]
             for c in range(3):
                 centre = along[c]
-                z_next = pad_ref[c, z + 2, 8 + y : 40 + y, :]
-                z_prev = pad_ref[c, z, 8 + y : 40 + y, :]
-                y_next = pad_ref[c, z + 1, 9 + y : 41 + y, :]
-                y_prev = pad_ref[c, z + 1, 7 + y : 39 + y, :]
+                z_next = pad_ref[c, z + 2, 8 + y : 24 + y, :]
+                z_prev = pad_ref[c, z, 8 + y : 24 + y, :]
+                y_next = pad_ref[c, z + 1, 9 + y : 25 + y, :]
+                y_prev = pad_ref[c, z + 1, 7 + y : 23 + y, :]
                 x_next = pltpu.roll(centre, 255, 1)
                 x_prev = pltpu.roll(centre, 1, 1)
-                new_ref[c, z, y : y + 32, :] = (
+                new_ref[c, z, y : y + 16, :] = (
                     (1.0 - 6.0 * near) * centre
                     + (ahead[0] * x_next + behind[0] * x_prev)
                     + (ahead[1] * y_next + behind[1] * y_prev)

time: 225 us -> 222 us (0.987)
  Pallas kernels: 49.6 us -> 46.8 us
  transfers between devices with their start and end apart: 23 -> 23, of which waited for: 15 -> 15; matrix products, arithmetic and copies ran while one was open for 4% -> 4% of each run, Pallas kernels for 14% -> 13%
where the time goes in v5:
time: 222 us; the launch traced here: 218 us
  waiting for transfers between devices  93.1 us (42%)
  starting transfers between devices  63.3 us (29%)
  Pallas kernels  46.8 us (21%)
  local copies, waits for them, and re-layouts  7.88 us (4%)
  other arithmetic  6.46 us (3%)
    ppermute x12, waiting for transfers between devices, around(): got.append(lax.ppermute(value, 'mp', [(i, (i + d) % 4) for i in range(4)]))  37 us
    all_to_all x2, waiting for transfers between devices, total(): lax.all_to_all(partial.reshape(64, -1, 128), ('slab', 'mp'), split_axis=0...  34.8 us
    all_to_all x3, starting transfers between devices, exchange(): return lax.all_to_all(value, axes, split_axis=0, concat_axis=0, tiled=True)  21.4 us
    ppermute x12, starting transfers between devices, around(): got.append(lax.ppermute(value, 'mp', [(i, (i + d) % 4) for i in range(4)]))  18.7 us
    all_to_all x2, starting transfers between devices, total(): lax.all_to_all(partial.reshape(64, -1, 128), ('slab', 'mp'), split_axis=0...  17.1 us
    ppermute x1, waiting for transfers between devices, step(): z_prev = lax.ppermute(velocity[:, 7:8], 'slab', up)  15.6 us
    pallas_call x1, Pallas kernels, step(): call(new_kernel, [((3, 8, 128, 256), F32), ((512, 1536), BF16)], [pltpu.V...  10.3 us
    pallas_call x1, Pallas kernels, step(): call(backward_kernel, [((16, 4, 96, 128), BF16), ((16, 4, 96, 128), BF16)...  9.62 us
  transfers between devices with their start and end apart: 23, of which 15 were waited for; matrix products, arithmetic and copies ran while one was open for 4% of the time, Pallas kernels for 13%

profile of v5, /device:TPU:6, one launch (start us, length us, event | category | flops | bytes accessed | tf_op | source)
XLA Modules:
  0.0 218.4 jit_solution(17246964062932656765)
XLA Ops:
  0.6 7.1 %shard_map.152 = (bf16[512,1664]{1,0:T(8,128)(2,1)}, bf16[256,512]{1,0:T(8,128)(2,1)}, bf16[512,256]{1,0:T(8,128)(2,1)}) custom-call(f32[3,8,128,256]{3,2,1,0:T(8,128)} %field_hbm.3, s32[3,1,256]{2,1,0:T(1,128)} %bitcast.24, s32[1,256]{1,0:T(1,128)} %bitcast.25), custom_call_target="tpu_custom_call" | custom-call | tf_op jit(solution)/shard_map/pallas_call | solution.py:443
  7.8 7.6 %all-to-all-start = ((bf16[32,16,1664]{2,1,0:T(8,128)(2,1)}), bf16[32,16,1664]{2,1,0:T(8,128)(2,1)S(1)}, u32[]{:S(2)}, u32[]{:S(2)}) async-start(bf16[32,16,1664]{2,1,0:T(8,128)(2,1)} %bitcast.19), calls=%async_computation | async-start | bytes 3407872 | tf_op jit(solution)/shard_map/all_to_all | solution.py:410
  15.3 1.2 fusion.1
  16.5 0.2 collective-permute-start
  16.7 1.6 collective-permute-start.1
  18.3 1.1 fusion
  19.4 2.0 collective-permute-start.2
  21.4 2.2 %collective-permute-start.3 = (f32[3,8,1,256]{3,2,1,0:T(1,128)S(1)}, f32[3,8,1,256]{3,2,1,0:T(1,128)S(1)}, u32[]{:S(2)}, u32[]{:S(2)}) collective-permute-start(f32[3,8,1,256]{3,2,1,0:T(1,128)S(1)} %get-tuple-element.74), channel_id=1, source_target_pairs={{1,0},{2,1},{3,2},{0,3},{5,4},{6,5},{7,6},{4,7},{9,8},{10,9},{11,1... | collective-permute-start | bytes 73736 | tf_op jit(solution)/shard_map/ppermute | solution.py:439
  23.6 1.7 collective-permute-done.2.y_prev_ref
  25.3 15.6 %collective-permute-done.z_prev_ref = f32[3,1,128,256]{3,2,1,0:T(8,128)S(1)} collective-permute-done((f32[3,1,128,256]{3,2,1,0:T(8,128)S(1)}, f32[3,1,128,256]{3,2,1,0:T(8,128)S(1)}, u32[]{:S(2)}, u32[]{:S(2)}) %collective-permute-start) | collective-permute-done | bytes 393248 | tf_op jit(solution)/shard_map/ppermute | solution.py:435
  40.9 0.7 copy-done.8
  41.7 0.1 copy-done.9
  41.8 10.3 %shard_map.153 = (f32[3,8,128,256]{3,2,1,0:T(8,128)}, bf16[512,1536]{1,0:T(8,128)(2,1)}) custom-call(f32[3,8,128,256]{3,2,1,0:T(8,128)} %field_hbm.3, f32[3,1,128,256]{3,2,1,0:T(8,128)} %copy-done.8, f32[3,1,128,256]{3,2,1,0:T(8,128)} %copy-done.9, f32[3,8,1,256]{3,2,1,0:T(1,128)} %copy-done.22, f32[3,8,1,256]{3,2,1,0:T(1,128)} %copy-done.23, ...), custom_call_target="tpu_custom_call" | custom-call | tf_op jit(solution)/shard_map/pallas_call | solution.py:450
  52.1 0.0 copy-start.17
  52.2 0.0 copy-start.18
  52.2 7.3 %all-to-all-start.1 = ((bf16[32,16,1536]{2,1,0:T(8,128)(2,1)}), bf16[32,16,1536]{2,1,0:T(8,128)(2,1)S(1)}, u32[]{:S(2)}, u32[]{:S(2)}) async-start(bf16[32,16,1536]{2,1,0:T(8,128)(2,1)} %bitcast.20), calls=%async_computation.1 | async-start | bytes 3145728 | tf_op jit(solution)/shard_map/all_to_all | solution.py:410
  59.5 1.0 pad_maximum_fusion.w0_ref
  60.6 2.0 collective-permute-start.4
  62.6 3.6 %collective-permute-start.5 = (bf16[4,512,128]{2,1,0:T(8,128)(2,1)S(1)}, bf16[4,512,128]{2,1,0:T(8,128)(2,1)S(1)}, u32[]{:S(2)}, u32[]{:S(2)}) collective-permute-start(bf16[4,512,128]{2,1,0:T(8,128)(2,1)S(1)} %pad_maximum_fusion.w0_ref), channel_id=1, source_target_pairs={{0,2},{1,3},{2,0},{3,1},{4,6},{5,7},{6,4},{7,5},{8,10},{9,11},{10,... | collective-permute-start | bytes 1572872 | tf_op jit(solution)/shard_map/ppermute | solution.py:405
  66.1 1.0 collective-permute-start.6
  67.1 0.6 pad_add_fusion.place_ref
  67.7 9.2 %collective-permute-done.4.w1_ref = bf16[4,512,128]{2,1,0:T(8,128)(2,1)S(1)} collective-permute-done((bf16[4,512,128]{2,1,0:T(8,128)(2,1)S(1)}, bf16[4,512,128]{2,1,0:T(8,128)(2,1)S(1)}, u32[]{:S(2)}, u32[]{:S(2)}) %collective-permute-start.4) | collective-permute-done | bytes 524320 | tf_op jit(solution)/shard_map/ppermute | solution.py:405
  76.9 12.4 %collective-permute-done.5.w2_ref = bf16[4,512,128]{2,1,0:T(8,128)(2,1)S(1)} collective-permute-done((bf16[4,512,128]{2,1,0:T(8,128)(2,1)S(1)}, bf16[4,512,128]{2,1,0:T(8,128)(2,1)S(1)}, u32[]{:S(2)}, u32[]{:S(2)}) %collective-permute-start.5) | collective-permute-done | bytes 524320 | tf_op jit(solution)/shard_map/ppermute | solution.py:405
  89.3 0.8 copy-done.7
  90.1 8.8 %shard_map.154 = (bf16[512,512]{1,0:T(8,128)(2,1)}, bf16[512,512]{1,0:T(8,128)(2,1)}, bf16[512,512]{1,0:T(8,128)(2,1)}, f32[512,512]{1,0:T(8,128)}, bf16[512,512...) custom-call(s32[2]{0:T(128)} %pad_add_fusion.place_ref, ...), custom_call_target="tpu_custom_call" | custom-call | tf_op jit(solution)/shard_map/pallas_call | solution.py:465
  99.0 0.5 collective-permute-start.7
  99.5 2.4 %collective-permute-start.8 = (f32[264,128]{1,0:T(8,128)}, f32[264,128]{1,0:T(8,128)S(1)}, u32[]{:S(2)}, u32[]{:S(2)}) collective-permute-start(f32[264,128]{1,0:T(8,128)} %get-tuple-element.44.s0_ref), channel_id=1, source_target_pairs={{0,2},{1,3},{2,0},{3,1},{4,6},{5,7},{6,4},{7,5},{8,10},{9,11},{10,... | collective-permute-start | bytes 405512 | tf_op jit(solution)/shard_map/ppermute | solution.py:405
  101.9 1.2 collective-permute-start.9
  103.1 3.1 %collective-permute-done.7.s1_ref = f32[264,128]{1,0:T(8,128)S(1)} collective-permute-done((f32[264,128]{1,0:T(8,128)}, f32[264,128]{1,0:T(8,128)S(1)}, u32[]{:S(2)}, u32[]{:S(2)}) %collective-permute-start.7) | collective-permute-done | bytes 135200 | tf_op jit(solution)/shard_map/ppermute | solution.py:405
  106.2 2.3 %collective-permute-done.8.s2_ref = f32[264,128]{1,0:T(8,128)S(1)} collective-permute-done((f32[264,128]{1,0:T(8,128)}, f32[264,128]{1,0:T(8,128)S(1)}, u32[]{:S(2)}, u32[]{:S(2)}) %collective-permute-start.8) | collective-permute-done | bytes 135200 | tf_op jit(solution)/shard_map/ppermute | solution.py:405
  108.5 0.2 collective-permute-done.9.s3_ref
  108.6 0.5 copy-done.14
  109.1 0.2 copy-done.16
  109.3 0.5 copy-done.1
  109.8 8.6 %shard_map.155 = (bf16[16,4,64,128]{3,2,1,0:T(8,128)(2,1)}, bf16[16,4,64,128]{3,2,1,0:T(8,128)(2,1)}, bf16[512,512]{1,0:T(8,128)(2,1)}, f32[512,512]{1,0:T(8,128...) custom-call(s32[2]{0:T(128)} %pad_add_fusion.place_ref, f32[264,128]{1,0:T(8,128)} %get-tuple-element.44.s0_ref, ...), custom_call_target="tpu_custom_call" | custom-call | tf_op jit(solution)/shard_map/pallas_call | solution.py:472
  118.4 0.0 collective-permute-start.14
  118.5 0.8 collective-permute-start.10
  119.2 3.4 %collective-permute-start.11 = (f32[264,128]{1,0:T(8,128)}, f32[264,128]{1,0:T(8,128)S(1)}, u32[]{:S(2)}, u32[]{:S(2)}) collective-permute-start(f32[264,128]{1,0:T(8,128)} %get-tuple-element.49.s0_ref), channel_id=1, source_target_pairs={{0,2},{1,3},{2,0},{3,1},{4,6},{5,7},{6,4},{7,5},{8,10},{9,11},{10,... | collective-permute-start | bytes 405512 | tf_op jit(solution)/shard_map/ppermute | solution.py:405
  122.7 3.2 %collective-permute-done.10.s1_ref = f32[264,128]{1,0:T(8,128)S(1)} collective-permute-done((f32[264,128]{1,0:T(8,128)}, f32[264,128]{1,0:T(8,128)S(1)}, u32[]{:S(2)}, u32[]{:S(2)}) %collective-permute-start.10) | collective-permute-done | bytes 135200 | tf_op jit(solution)/shard_map/ppermute | solution.py:405
  125.9 3.8 %collective-permute-done.11.s2_ref = f32[264,128]{1,0:T(8,128)S(1)} collective-permute-done((f32[264,128]{1,0:T(8,128)}, f32[264,128]{1,0:T(8,128)S(1)}, u32[]{:S(2)}, u32[]{:S(2)}) %collective-permute-start.11) | collective-permute-done | bytes 135200 | tf_op jit(solution)/shard_map/ppermute | solution.py:405
  129.7 0.6 copy-done.13
  130.3 0.0 copy-done.15
  130.4 9.6 %shard_map.156 = (bf16[16,4,96,128]{3,2,1,0:T(8,128)(2,1)}, bf16[16,4,96,128]{3,2,1,0:T(8,128)(2,1)}, f32[8,128]{1,0:T(8,128)}) custom-call(s32[2]{0:T(128)} %pad_add_fusion.place_ref, f32[264,128]{1,0:T(8,128)} %get-tuple-element.49.s0_ref, f32[264,128]{1,0:T(8,128)} %copy-done.11, f32[264,128]{1,0:T(8,128)} %copy-done.13, f32[264,128]{1,0:T(8,128)} %copy-done.15, ...), custom_call_target="tpu_custom_call" | custom-call | tf_op jit(solution)/shard_map/pallas_call | solution.py:489
  140.0 0.1 collective-permute-start.13
  140.1 1.4 add_convert_fusion.1
  141.5 9.7 %all-to-all-start.3 = ((bf16[64,64,128]{2,1,0:T(8,128)(2,1)}), bf16[64,64,128]{2,1,0:T(8,128)(2,1)S(1)}, u32[]{:S(2)}, u32[]{:S(2)}) async-start(bf16[64,64,128]{2,1,0:T(8,128)(2,1)} %bitcast.13), calls=%async_computation.3 | async-start | bytes 2097152 | tf_op jit(solution)/shard_map/all_to_all | solution.py:420
  151.2 3.0 %add_convert_fusion = bf16[16,4,96,128]{3,2,1,0:T(8,128)(2,1)} fusion(bf16[16,4,96,128]{3,2,1,0:T(8,128)(2,1)} %collective-permute-done.13, bf16[16,4,96,128]{3,2,1,0:T(8,128)(2,1)S(1)} %copy-done.4), kind=kLoop, calls=%fused_computation.1 | loop fusion | flops 3145728 | bytes 4718592 | tf_op jit(solution)/shard_map/convert_element_type | solution.py:415
  154.2 13.9 %all-to-all-done.3 = bf16[64,64,128]{2,1,0:T(8,128)(2,1)S(1)} async-done(((bf16[64,64,128]{2,1,0:T(8,128)(2,1)}), bf16[64,64,128]{2,1,0:T(8,128)(2,1)S(1)}, u32[]{:S(2)}, u32[]{:S(2)}) %all-to-all-start.3) | async-done | bytes 1048608 | tf_op jit(solution)/shard_map/all_to_all | solution.py:420
  168.2 7.4 %all-to-all-start.2 = ((bf16[64,96,128]{2,1,0:T(8,128)(2,1)}), bf16[64,96,128]{2,1,0:T(8,128)(2,1)S(1)}, u32[]{:S(2)}, u32[]{:S(2)}) async-start(bf16[64,96,128]{2,1,0:T(8,128)(2,1)} %bitcast.12), calls=%async_computation.2 | async-start | bytes 3145728 | tf_op jit(solution)/shard_map/all_to_all | solution.py:420
  175.6 0.2 convert_reduce_fusion.1
  175.8 20.9 %all-to-all-done.2 = bf16[64,96,128]{2,1,0:T(8,128)(2,1)S(1)} async-done(((bf16[64,96,128]{2,1,0:T(8,128)(2,1)}), bf16[64,96,128]{2,1,0:T(8,128)(2,1)S(1)}, u32[]{:S(2)}, u32[]{:S(2)}) %all-to-all-start.2) | async-done | bytes 1572896 | tf_op jit(solution)/shard_map/all_to_all | solution.py:420
  196.6 0.2 convert_reduce_fusion
  196.9 0.2 concatenate.14
  197.1 0.9 broadcast_in_dim.10
  198.0 6.5 %all-to-all-start.4 = ((bf16[32,80,128]{2,1,0:T(8,128)(2,1)}), bf16[32,80,128]{2,1,0:T(8,128)(2,1)S(1)}, u32[]{:S(2)}, u32[]{:S(2)}) async-start(bf16[32,80,128]{2,1,0:T(8,128)(2,1)} %broadcast_in_dim.10), calls=%async_computation.4 | async-start | bytes 1310720 | tf_op jit(solution)/shard_map/all_to_all | solution.py:410
  204.6 0.9 collective-permute-start.15
  205.5 1.6 collective-permute-start.16
  207.1 1.3 collective-permute-start.17
  208.4 2.1 collective-permute-done.15.r1_ref
  210.5 0.6 collective-permute-done.16.r2_ref
  211.1 0.3 collective-permute-done.17.r3_ref
  211.3 3.9 %all-to-all-done.4.heads_ref = bf16[32,80,128]{2,1,0:T(8,128)(2,1)S(1)} async-done(((bf16[32,80,128]{2,1,0:T(8,128)(2,1)}), bf16[32,80,128]{2,1,0:T(8,128)(2,1)S(1)}, u32[]{:S(2)}, u32[]{:S(2)}) %all-to-all-start.4) | async-done | bytes 655392 | tf_op jit(solution)/shard_map/all_to_all | solution.py:410
  215.3 0.8 copy-done.2
  216.2 2.3 %shard_map.157 = (f32[48,512]{1,0:T(8,128)}, f32[512,128]{1,0:T(8,128)}, f32[512,128]{1,0:T(8,128)}, f32[512,128]{1,0:T(8,128)}, f32[128,512]{1,0:T(8,128)}, /*index=5*/f32[16,1536]{1,0:T(8,128)}, f32[1,1]{1,0:T(1,128)}) custom-call(s32[2]{0:T(128)} %pad_add_fusion.place_ref, f32[96,128]{1,0:T(8,128)} %copy-done.10, f32[96,128]{1,0:T(8,128)} %copy-done.19, ...), custom_call_target="tpu_custom_call" | custom-call | tf_op jit(solution)/shard_map/pallas_call | solution.py:509
  (59 shorter events, 0.2 us)
Async XLA Ops:
  7.8 44.4 %all-to-all-start = ((bf16[32,16,1664]{2,1,0:T(8,128)(2,1)}), bf16[32,16,1664]{2,1,0:T(8,128)(2,1)S(1)}, u32[]{:S(2)}, u32[]{:S(2)}) async-start(bf16[32,16,1664]{2,1,0:T(8,128)(2,1)} %bitcast.19), calls=%async_computation | async-start | bytes 3407872 | tf_op jit(solution)/shard_map/all_to_all | solution.py:410
  16.5 24.4 %collective-permute-start = (f32[3,1,128,256]{3,2,1,0:T(8,128)S(1)}, f32[3,1,128,256]{3,2,1,0:T(8,128)S(1)}, u32[]{:S(2)}, u32[]{:S(2)}) collective-permute-start(f32[3,1,128,256]{3,2,1,0:T(8,128)S(1)} %get-tuple-element.77), channel_id=1, source_target_pairs={{0,4},{4,8},{8,12},{12,16},{16,20},{20,24},{24,28},{28,32},{32,36}... | collective-permute-start | bytes 1179656 | tf_op jit(solution)/shard_map/ppermute | solution.py:435
  16.7 24.2 %collective-permute-start.1 = (f32[3,1,128,256]{3,2,1,0:T(8,128)S(1)}, f32[3,1,128,256]{3,2,1,0:T(8,128)S(1)}, u32[]{:S(2)}, u32[]{:S(2)}) collective-permute-start(f32[3,1,128,256]{3,2,1,0:T(8,128)S(1)} %get-tuple-element.76), channel_id=1, source_target_pairs={{4,0},{8,4},{12,8},{16,12},{20,16},{24,20},{28,24},{32,28},{36,32}... | collective-permute-start | bytes 1179656 | tf_op jit(solution)/shard_map/ppermute | solution.py:436
  19.4 5.9 %collective-permute-start.2 = (f32[3,8,1,256]{3,2,1,0:T(1,128)S(1)}, f32[3,8,1,256]{3,2,1,0:T(1,128)S(1)}, u32[]{:S(2)}, u32[]{:S(2)}) collective-permute-start(f32[3,8,1,256]{3,2,1,0:T(1,128)S(1)} %get-tuple-element.75), channel_id=1, source_target_pairs={{0,1},{1,2},{2,3},{3,0},{4,5},{5,6},{6,7},{7,4},{8,9},{9,10},{10,1... | collective-permute-start | bytes 73736 | tf_op jit(solution)/shard_map/ppermute | solution.py:438
  21.4 3.9 %collective-permute-start.3 = (f32[3,8,1,256]{3,2,1,0:T(1,128)S(1)}, f32[3,8,1,256]{3,2,1,0:T(1,128)S(1)}, u32[]{:S(2)}, u32[]{:S(2)}) collective-permute-start(f32[3,8,1,256]{3,2,1,0:T(1,128)S(1)} %get-tuple-element.74), channel_id=1, source_target_pairs={{1,0},{2,1},{3,2},{0,3},{5,4},{6,5},{7,6},{4,7},{9,8},{10,9},{11,1... | collective-permute-start | bytes 73736 | tf_op jit(solution)/shard_map/ppermute | solution.py:439
  25.3 15.6 %copy-start.22 = (f32[3,8,1,256]{3,2,1,0:T(1,128)}, f32[3,8,1,256]{3,2,1,0:T(1,128)S(1)}, u32[]{:S(2)}) copy-start(f32[3,8,1,256]{3,2,1,0:T(1,128)S(1)} %collective-permute-done.2.y_prev_ref) | copy-start | bytes 73732
  25.3 15.6 %copy-start.23 = (f32[3,8,1,256]{3,2,1,0:T(1,128)}, f32[3,8,1,256]{3,2,1,0:T(1,128)S(1)}, u32[]{:S(2)}) copy-start(f32[3,8,1,256]{3,2,1,0:T(1,128)S(1)} %collective-permute-done.3.y_next_ref) | copy-start | bytes 73732
  40.9 0.7 copy-start.8
  40.9 0.9 copy-start.9
  52.1 7.3 %copy-start.17 = (bf16[128,512]{1,0:T(8,128)(2,1)S(1)}, bf16[128,512]{1,0:T(8,128)(2,1)}, u32[]{:S(2)}) copy-start(bf16[128,512]{1,0:T(8,128)(2,1)} %param.16) | copy-start | bytes 393220
  52.1 7.3 %copy-start = (bf16[32,16,1664]{2,1,0:T(8,128)(2,1)}, bf16[32,16,1664]{2,1,0:T(8,128)(2,1)S(1)}, u32[]{:S(2)}) copy-start(bf16[32,16,1664]{2,1,0:T(8,128)(2,1)S(1)} %all-to-all-done) | copy-start | bytes 5111812
  52.2 7.4 %copy-start.18 = (bf16[512,128]{1,0:T(8,128)(2,1)S(1)}, bf16[512,128]{1,0:T(8,128)(2,1)}, u32[]{:S(2)}) copy-start(bf16[512,128]{1,0:T(8,128)(2,1)} %param.15) | copy-start | bytes 393220
  52.2 56.5 %all-to-all-start.1 = ((bf16[32,16,1536]{2,1,0:T(8,128)(2,1)}), bf16[32,16,1536]{2,1,0:T(8,128)(2,1)S(1)}, u32[]{:S(2)}, u32[]{:S(2)}) async-start(bf16[32,16,1536]{2,1,0:T(8,128)(2,1)} %bitcast.20), calls=%async_computation.1 | async-start | bytes 3145728 | tf_op jit(solution)/shard_map/all_to_all | solution.py:410
  60.6 28.7 %copy-start.3 = (bf16[4,512,128]{2,1,0:T(8,128)(2,1)}, bf16[4,512,128]{2,1,0:T(8,128)(2,1)S(1)}, u32[]{:S(2)}) copy-start(bf16[4,512,128]{2,1,0:T(8,128)(2,1)S(1)} %pad_maximum_fusion.w0_ref) | copy-start | bytes 1572868
  60.6 16.3 %collective-permute-start.4 = (bf16[4,512,128]{2,1,0:T(8,128)(2,1)S(1)}, bf16[4,512,128]{2,1,0:T(8,128)(2,1)S(1)}, u32[]{:S(2)}, u32[]{:S(2)}) collective-permute-start(bf16[4,512,128]{2,1,0:T(8,128)(2,1)S(1)} %pad_maximum_fusion.w0_ref), channel_id=1, source_target_pairs={{0,1},{1,2},{2,3},{3,0},{4,5},{5,6},{6,7},{7,4},{8,9},{9,10},{10,1... | collective-permute-start | bytes 1572872 | tf_op jit(solution)/shard_map/ppermute | solution.py:405
  62.6 26.7 %collective-permute-start.5 = (bf16[4,512,128]{2,1,0:T(8,128)(2,1)S(1)}, bf16[4,512,128]{2,1,0:T(8,128)(2,1)S(1)}, u32[]{:S(2)}, u32[]{:S(2)}) collective-permute-start(bf16[4,512,128]{2,1,0:T(8,128)(2,1)S(1)} %pad_maximum_fusion.w0_ref), channel_id=1, source_target_pairs={{0,2},{1,3},{2,0},{3,1},{4,6},{5,7},{6,4},{7,5},{8,10},{9,11},{10,... | collective-permute-start | bytes 1572872 | tf_op jit(solution)/shard_map/ppermute | solution.py:405
  66.1 23.2 %collective-permute-start.6 = (bf16[4,512,128]{2,1,0:T(8,128)(2,1)S(1)}, bf16[4,512,128]{2,1,0:T(8,128)(2,1)}, u32[]{:S(2)}, u32[]{:S(2)}) collective-permute-start(bf16[4,512,128]{2,1,0:T(8,128)(2,1)S(1)} %pad_maximum_fusion.w0_ref), channel_id=1, source_target_pairs={{0,3},{1,0},{2,1},{3,2},{4,7},{5,4},{6,5},{7,6},{8,11},{9,8},{10,9... | collective-permute-start | bytes 1572872 | tf_op jit(solution)/shard_map/ppermute | solution.py:405
  76.9 12.4 %copy-start.6 = (bf16[4,512,128]{2,1,0:T(8,128)(2,1)}, bf16[4,512,128]{2,1,0:T(8,128)(2,1)S(1)}, u32[]{:S(2)}) copy-start(bf16[4,512,128]{2,1,0:T(8,128)(2,1)S(1)} %collective-permute-done.4.w1_ref) | copy-start | bytes 1572868
  89.3 0.8 copy-start.7
  99.0 7.2 %collective-permute-start.7 = (f32[264,128]{1,0:T(8,128)}, f32[264,128]{1,0:T(8,128)S(1)}, u32[]{:S(2)}, u32[]{:S(2)}) collective-permute-start(f32[264,128]{1,0:T(8,128)} %get-tuple-element.44.s0_ref), channel_id=1, source_target_pairs={{0,1},{1,2},{2,3},{3,0},{4,5},{5,6},{6,7},{7,4},{8,9},{9,10},{10,1... | collective-permute-start | bytes 405512 | tf_op jit(solution)/shard_map/ppermute | solution.py:405
  99.5 9.0 %collective-permute-start.8 = (f32[264,128]{1,0:T(8,128)}, f32[264,128]{1,0:T(8,128)S(1)}, u32[]{:S(2)}, u32[]{:S(2)}) collective-permute-start(f32[264,128]{1,0:T(8,128)} %get-tuple-element.44.s0_ref), channel_id=1, source_target_pairs={{0,2},{1,3},{2,0},{3,1},{4,6},{5,7},{6,4},{7,5},{8,10},{9,11},{10,... | collective-permute-start | bytes 405512 | tf_op jit(solution)/shard_map/ppermute | solution.py:405
  101.9 6.7 %collective-permute-start.9 = (f32[264,128]{1,0:T(8,128)}, f32[264,128]{1,0:T(8,128)S(1)}, u32[]{:S(2)}, u32[]{:S(2)}) collective-permute-start(f32[264,128]{1,0:T(8,128)} %get-tuple-element.44.s0_ref), channel_id=1, source_target_pairs={{0,3},{1,0},{2,1},{3,2},{4,7},{5,4},{6,5},{7,6},{8,11},{9,8},{10,9... | collective-permute-start | bytes 405512 | tf_op jit(solution)/shard_map/ppermute | solution.py:405
  106.2 2.4 %copy-start.12 = (f32[264,128]{1,0:T(8,128)}, f32[264,128]{1,0:T(8,128)S(1)}, u32[]{:S(2)}) copy-start(f32[264,128]{1,0:T(8,128)S(1)} %collective-permute-done.7.s1_ref) | copy-start | bytes 405508
  108.5 0.7 copy-start.14
  108.6 0.7 copy-start.16
  108.6 1.2 copy-start.1
  118.4 21.7 %collective-permute-start.14 = (bf16[16,4,64,128]{3,2,1,0:T(8,128)(2,1)}, bf16[16,4,64,128]{3,2,1,0:T(8,128)(2,1)S(1)}, u32[]{:S(2)}, u32[]{:S(2)}) collective-permute-start(bf16[16,4,64,128]{3,2,1,0:T(8,128)(2,1)} %get-tuple-element.63), channel_id=1, source_target_pairs={{0,4},{4,0},{8,12},{12,8},{16,20},{20,16},{24,28},{28,24},{32,36},... | collective-permute-start | bytes 3145736 | tf_op jit(solution)/shard_map/ppermute | solution.py:414
  118.5 7.4 %collective-permute-start.10 = (f32[264,128]{1,0:T(8,128)}, f32[264,128]{1,0:T(8,128)S(1)}, u32[]{:S(2)}, u32[]{:S(2)}) collective-permute-start(f32[264,128]{1,0:T(8,128)} %get-tuple-element.49.s0_ref), channel_id=1, source_target_pairs={{0,1},{1,2},{2,3},{3,0},{4,5},{5,6},{6,7},{7,4},{8,9},{9,10},{10,1... | collective-permute-start | bytes 405512 | tf_op jit(solution)/shard_map/ppermute | solution.py:405
  119.2 10.4 %collective-permute-start.11 = (f32[264,128]{1,0:T(8,128)}, f32[264,128]{1,0:T(8,128)S(1)}, u32[]{:S(2)}, u32[]{:S(2)}) collective-permute-start(f32[264,128]{1,0:T(8,128)} %get-tuple-element.49.s0_ref), channel_id=1, source_target_pairs={{0,2},{1,3},{2,0},{3,1},{4,6},{5,7},{6,4},{7,5},{8,10},{9,11},{10,... | collective-permute-start | bytes 405512 | tf_op jit(solution)/shard_map/ppermute | solution.py:405
  122.7 7.0 %collective-permute-start.12 = (f32[264,128]{1,0:T(8,128)}, f32[264,128]{1,0:T(8,128)S(1)}, u32[]{:S(2)}, u32[]{:S(2)}) collective-permute-start(f32[264,128]{1,0:T(8,128)} %get-tuple-element.49.s0_ref), channel_id=1, source_target_pairs={{0,3},{1,0},{2,1},{3,2},{4,7},{5,4},{6,5},{7,6},{8,11},{9,8},{10,9... | collective-permute-start | bytes 405512 | tf_op jit(solution)/shard_map/ppermute | solution.py:405
  125.9 3.8 %copy-start.11 = (f32[264,128]{1,0:T(8,128)}, f32[264,128]{1,0:T(8,128)S(1)}, u32[]{:S(2)}) copy-start(f32[264,128]{1,0:T(8,128)S(1)} %collective-permute-done.10.s1_ref) | copy-start | bytes 405508
  129.7 0.7 copy-start.13
  129.7 0.7 copy-start.15
  130.4 9.7 %copy-start.5 = (bf16[16,4,64,128]{3,2,1,0:T(8,128)(2,1)S(1)}, bf16[16,4,64,128]{3,2,1,0:T(8,128)(2,1)}, u32[]{:S(2)}) copy-start(bf16[16,4,64,128]{3,2,1,0:T(8,128)(2,1)} %get-tuple-element.62) | copy-start | bytes 3145732
  140.0 11.2 %collective-permute-start.13 = (bf16[16,4,96,128]{3,2,1,0:T(8,128)(2,1)}, bf16[16,4,96,128]{3,2,1,0:T(8,128)(2,1)}, u32[]{:S(2)}, u32[]{:S(2)}) collective-permute-start(bf16[16,4,96,128]{3,2,1,0:T(8,128)(2,1)} %get-tuple-element.61), channel_id=1, source_target_pairs={{0,4},{4,0},{8,12},{12,8},{16,20},{20,16},{24,28},{28,24},{32,36},... | collective-permute-start | bytes 4718600 | tf_op jit(solution)/shard_map/ppermute | solution.py:414
  141.5 9.7 %copy-start.4 = (bf16[16,4,96,128]{3,2,1,0:T(8,128)(2,1)S(1)}, bf16[16,4,96,128]{3,2,1,0:T(8,128)(2,1)}, u32[]{:S(2)}) copy-start(bf16[16,4,96,128]{3,2,1,0:T(8,128)(2,1)} %get-tuple-element.60) | copy-start | bytes 4718596
  141.5 26.6 %all-to-all-start.3 = ((bf16[64,64,128]{2,1,0:T(8,128)(2,1)}), bf16[64,64,128]{2,1,0:T(8,128)(2,1)S(1)}, u32[]{:S(2)}, u32[]{:S(2)}) async-start(bf16[64,64,128]{2,1,0:T(8,128)(2,1)} %bitcast.13), calls=%async_computation.3 | async-start | bytes 2097152 | tf_op jit(solution)/shard_map/all_to_all | solution.py:420
  154.2 21.3 %copy-start.24 = (f32[8,128]{1,0:T(8,128)S(1)}, f32[8,128]{1,0:T(8,128)}, u32[]{:S(2)}) copy-start(f32[8,128]{1,0:T(8,128)} %get-tuple-element.64) | copy-start | bytes 12292
  168.2 28.5 %all-to-all-start.2 = ((bf16[64,96,128]{2,1,0:T(8,128)(2,1)}), bf16[64,96,128]{2,1,0:T(8,128)(2,1)S(1)}, u32[]{:S(2)}, u32[]{:S(2)}) async-start(bf16[64,96,128]{2,1,0:T(8,128)(2,1)} %bitcast.12), calls=%async_computation.2 | async-start | bytes 3145728 | tf_op jit(solution)/shard_map/all_to_all | solution.py:420
  198.0 17.3 %all-to-all-start.4 = ((bf16[32,80,128]{2,1,0:T(8,128)(2,1)}), bf16[32,80,128]{2,1,0:T(8,128)(2,1)S(1)}, u32[]{:S(2)}, u32[]{:S(2)}) async-start(bf16[32,80,128]{2,1,0:T(8,128)(2,1)} %broadcast_in_dim.10), calls=%async_computation.4 | async-start | bytes 1310720 | tf_op jit(solution)/shard_map/all_to_all | solution.py:410
  204.6 10.7 %copy-start.10 = (f32[96,128]{1,0:T(8,128)}, f32[96,128]{1,0:T(8,128)S(1)}, u32[]{:S(2)}) copy-start(f32[96,128]{1,0:T(8,128)S(1)} %pad_maximum_fusion.1.r0_ref) | copy-start | bytes 147460
  204.6 5.9 %collective-permute-start.15 = (f32[96,128]{1,0:T(8,128)S(1)}, f32[96,128]{1,0:T(8,128)S(1)}, u32[]{:S(2)}, u32[]{:S(2)}) collective-permute-start(f32[96,128]{1,0:T(8,128)S(1)} %pad_maximum_fusion.1.r0_ref), channel_id=1, source_target_pairs={{0,1},{1,2},{2,3},{3,0},{4,5},{5,6},{6,7},{7,4},{8,9},{9,10},{10,1... | collective-permute-start | bytes 147464 | tf_op jit(solution)/shard_map/ppermute | solution.py:405
  205.5 5.6 %collective-permute-start.16 = (f32[96,128]{1,0:T(8,128)S(1)}, f32[96,128]{1,0:T(8,128)S(1)}, u32[]{:S(2)}, u32[]{:S(2)}) collective-permute-start(f32[96,128]{1,0:T(8,128)S(1)} %pad_maximum_fusion.1.r0_ref), channel_id=1, source_target_pairs={{0,2},{1,3},{2,0},{3,1},{4,6},{5,7},{6,4},{7,5},{8,10},{9,11},{10,... | collective-permute-start | bytes 147464 | tf_op jit(solution)/shard_map/ppermute | solution.py:405
  207.1 4.2 %collective-permute-start.17 = (f32[96,128]{1,0:T(8,128)S(1)}, f32[96,128]{1,0:T(8,128)S(1)}, u32[]{:S(2)}, u32[]{:S(2)}) collective-permute-start(f32[96,128]{1,0:T(8,128)S(1)} %pad_maximum_fusion.1.r0_ref), channel_id=1, source_target_pairs={{0,3},{1,0},{2,1},{3,2},{4,7},{5,4},{6,5},{7,6},{8,11},{9,8},{10,9... | collective-permute-start | bytes 147464 | tf_op jit(solution)/shard_map/ppermute | solution.py:405
  210.5 4.8 %copy-start.19 = (f32[96,128]{1,0:T(8,128)}, f32[96,128]{1,0:T(8,128)S(1)}, u32[]{:S(2)}) copy-start(f32[96,128]{1,0:T(8,128)S(1)} %collective-permute-done.15.r1_ref) | copy-start | bytes 147460
  211.1 4.2 %copy-start.20 = (f32[96,128]{1,0:T(8,128)}, f32[96,128]{1,0:T(8,128)S(1)}, u32[]{:S(2)}) copy-start(f32[96,128]{1,0:T(8,128)S(1)} %collective-permute-done.16.r2_ref) | copy-start | bytes 147460
  211.3 3.9 %copy-start.21 = (f32[96,128]{1,0:T(8,128)}, f32[96,128]{1,0:T(8,128)S(1)}, u32[]{:S(2)}) copy-start(f32[96,128]{1,0:T(8,128)S(1)} %collective-permute-done.17.r3_ref) | copy-start | bytes 147460
  215.3 0.9 copy-start.2

commit v6 on v4

--- a/solution.py
+++ b/solution.py
@@ -133,8 +133,8 @@
     fetch = pltpu.make_async_copy(field_hbm, pad_ref.at[:, 1:9, 8:136, :], sem.at[0])
     fetch.start()
     selections(*scratch[:3])
-    pad_ref[:, 0:1, 8:136, :] = z_prev_ref[...].astype(F32)
-    pad_ref[:, 9:10, 8:136, :] = z_next_ref[...].astype(F32)
+    pad_ref[:, 0:1, 8:136, :] = z_prev_ref[...]
+    pad_ref[:, 9:10, 8:136, :] = z_next_ref[...]
     pad_ref[:, 1:9, 7:8, :] = y_prev_ref[...]
     pad_ref[:, 1:9, 136:137, :] = y_next_ref[...]
     fetch.wait()
@@ -433,8 +433,8 @@
     slabs = lax.axis_size("slab")
     place = jnp.stack([lax.axis_index("mp"), lax.axis_index("slab") & 1])
     up = [(i, (i + 1) % slabs) for i in range(slabs)]
-    z_prev = lax.ppermute(velocity[:, 7:8].astype(BF16), "slab", up)
-    z_next = lax.ppermute(velocity[:, 0:1].astype(BF16), "slab", [(j, i) for i, j in up])
+    z_prev = lax.ppermute(velocity[:, 7:8], "slab", up)
+    z_next = lax.ppermute(velocity[:, 0:1], "slab", [(j, i) for i, j in up])
     up = [(i, (i + 1) % 4) for i in range(4)]
     y_prev = lax.ppermute(velocity[:, :, 127:128], "mp", up)
     y_next = lax.ppermute(velocity[:, :, 0:1], "mp", [(j, i) for i, j in up])

time: 216 us -> 220 us (1.019)
  local copies, waits for them, and re-layouts: 4.98 us -> 7.82 us
    unnamed x54 -> x50, local copies, waits for them, and re-layouts: 3.73 us -> 4.41 us
  transfers between devices with their start and end apart: 23 -> 23, of which waited for: 16 -> 16; matrix products, arithmetic and copies ran while one was open for 3% -> 4% of each run, Pallas kernels for 14% -> 13%
where the time goes in v6:
time: 220 us; the launch traced here: 216 us
  waiting for transfers between devices  90.5 us (41%)
  starting transfers between devices  63.1 us (29%)
  Pallas kernels  46.7 us (21%)
  local copies, waits for them, and re-layouts  7.82 us (4%)
  other arithmetic  6.59 us (3%)
    all_to_all x2, waiting for transfers between devices, total(): lax.all_to_all(partial.reshape(64, -1, 128), ('slab', 'mp'), split_axis=0...  34.8 us
    ppermute x12, waiting for transfers between devices, around(): got.append(lax.ppermute(value, 'mp', [(i, (i + d) % 4) for i in range(4)]))  34.5 us
    all_to_all x3, starting transfers between devices, exchange(): return lax.all_to_all(value, axes, split_axis=0, concat_axis=0, tiled=True)  21.4 us
    ppermute x12, starting transfers between devices, around(): got.append(lax.ppermute(value, 'mp', [(i, (i + d) % 4) for i in range(4)]))  18.7 us
    all_to_all x2, starting transfers between devices, total(): lax.all_to_all(partial.reshape(64, -1, 128), ('slab', 'mp'), split_axis=0...  16.9 us
    ppermute x1, waiting for transfers between devices, step(): z_prev = lax.ppermute(velocity[:, 7:8], 'slab', up)  15.6 us
    pallas_call x1, Pallas kernels, step(): call(new_kernel, [((3, 8, 128, 256), F32), ((512, 1536), BF16)], [pltpu.V...  10.3 us
    pallas_call x1, Pallas kernels, step(): call(backward_kernel, [((16, 4, 96, 128), BF16), ((16, 4, 96, 128), BF16)...  9.53 us
  transfers between devices with their start and end apart: 23, of which 16 were waited for; matrix products, arithmetic and copies ran while one was open for 4% of the time, Pallas kernels for 13%

profile of v6, /device:TPU:6, one launch (start us, length us, event | category | flops | bytes accessed | tf_op | source)
XLA Modules:
  0.0 215.8 jit_solution(17357819693488766044)
XLA Ops:
  0.6 7.1 %shard_map.152 = (bf16[512,1664]{1,0:T(8,128)(2,1)}, bf16[256,512]{1,0:T(8,128)(2,1)}, bf16[512,256]{1,0:T(8,128)(2,1)}) custom-call(f32[3,8,128,256]{3,2,1,0:T(8,128)} %field_hbm.3, s32[3,1,256]{2,1,0:T(1,128)} %bitcast.24, s32[1,256]{1,0:T(1,128)} %bitcast.25), custom_call_target="tpu_custom_call" | custom-call | tf_op jit(solution)/shard_map/pallas_call | solution.py:444
  7.8 7.6 %all-to-all-start = ((bf16[32,16,1664]{2,1,0:T(8,128)(2,1)}), bf16[32,16,1664]{2,1,0:T(8,128)(2,1)S(1)}, u32[]{:S(2)}, u32[]{:S(2)}) async-start(bf16[32,16,1664]{2,1,0:T(8,128)(2,1)} %bitcast.19), calls=%async_computation | async-start | bytes 3407872 | tf_op jit(solution)/shard_map/all_to_all | solution.py:411
  15.3 1.2 fusion.1
  16.5 0.2 collective-permute-start
  16.7 1.6 collective-permute-start.1
  18.3 1.1 fusion
  19.4 2.0 collective-permute-start.2
  21.4 2.2 %collective-permute-start.3 = (f32[3,8,1,256]{3,2,1,0:T(1,128)S(1)}, f32[3,8,1,256]{3,2,1,0:T(1,128)S(1)}, u32[]{:S(2)}, u32[]{:S(2)}) collective-permute-start(f32[3,8,1,256]{3,2,1,0:T(1,128)S(1)} %get-tuple-element.74), channel_id=1, source_target_pairs={{1,0},{2,1},{3,2},{0,3},{5,4},{6,5},{7,6},{4,7},{9,8},{10,9},{11,1... | collective-permute-start | bytes 73736 | tf_op jit(solution)/shard_map/ppermute | solution.py:440
  23.6 1.7 collective-permute-done.2.y_prev_ref
  25.3 15.6 %collective-permute-done.z_prev_ref = f32[3,1,128,256]{3,2,1,0:T(8,128)S(1)} collective-permute-done((f32[3,1,128,256]{3,2,1,0:T(8,128)S(1)}, f32[3,1,128,256]{3,2,1,0:T(8,128)S(1)}, u32[]{:S(2)}, u32[]{:S(2)}) %collective-permute-start) | collective-permute-done | bytes 393248 | tf_op jit(solution)/shard_map/ppermute | solution.py:436
  40.9 0.7 copy-done.8
  41.7 0.1 copy-done.9
  41.8 10.3 %shard_map.153 = (f32[3,8,128,256]{3,2,1,0:T(8,128)}, bf16[512,1536]{1,0:T(8,128)(2,1)}) custom-call(f32[3,8,128,256]{3,2,1,0:T(8,128)} %field_hbm.3, f32[3,1,128,256]{3,2,1,0:T(8,128)} %copy-done.8, f32[3,1,128,256]{3,2,1,0:T(8,128)} %copy-done.9, f32[3,8,1,256]{3,2,1,0:T(1,128)} %copy-done.22, f32[3,8,1,256]{3,2,1,0:T(1,128)} %copy-done.23, ...), custom_call_target="tpu_custom_call" | custom-call | tf_op jit(solution)/shard_map/pallas_call | solution.py:451
  52.2 0.0 copy-start.15
  52.2 7.3 %all-to-all-start.1 = ((bf16[32,16,1536]{2,1,0:T(8,128)(2,1)}), bf16[32,16,1536]{2,1,0:T(8,128)(2,1)S(1)}, u32[]{:S(2)}, u32[]{:S(2)}) async-start(bf16[32,16,1536]{2,1,0:T(8,128)(2,1)} %bitcast.20), calls=%async_computation.1 | async-start | bytes 3145728 | tf_op jit(solution)/shard_map/all_to_all | solution.py:411
  59.5 1.0 pad_maximum_fusion.w0_ref
  60.6 2.0 collective-permute-start.4
  62.6 3.6 %collective-permute-start.5 = (bf16[4,512,128]{2,1,0:T(8,128)(2,1)S(1)}, bf16[4,512,128]{2,1,0:T(8,128)(2,1)S(1)}, u32[]{:S(2)}, u32[]{:S(2)}) collective-permute-start(bf16[4,512,128]{2,1,0:T(8,128)(2,1)S(1)} %pad_maximum_fusion.w0_ref), channel_id=1, source_target_pairs={{0,2},{1,3},{2,0},{3,1},{4,6},{5,7},{6,4},{7,5},{8,10},{9,11},{10,... | collective-permute-start | bytes 1572872 | tf_op jit(solution)/shard_map/ppermute | solution.py:406
  66.1 1.0 collective-permute-start.6
  67.1 0.7 pad_add_fusion.place_ref
  67.8 9.1 %collective-permute-done.4.w1_ref = bf16[4,512,128]{2,1,0:T(8,128)(2,1)S(1)} collective-permute-done((bf16[4,512,128]{2,1,0:T(8,128)(2,1)S(1)}, bf16[4,512,128]{2,1,0:T(8,128)(2,1)S(1)}, u32[]{:S(2)}, u32[]{:S(2)}) %collective-permute-start.4) | collective-permute-done | bytes 524320 | tf_op jit(solution)/shard_map/ppermute | solution.py:406
  76.9 12.4 %collective-permute-done.5.w2_ref = bf16[4,512,128]{2,1,0:T(8,128)(2,1)S(1)} collective-permute-done((bf16[4,512,128]{2,1,0:T(8,128)(2,1)S(1)}, bf16[4,512,128]{2,1,0:T(8,128)(2,1)S(1)}, u32[]{:S(2)}, u32[]{:S(2)}) %collective-permute-start.5) | collective-permute-done | bytes 524320 | tf_op jit(solution)/shard_map/ppermute | solution.py:406
  89.3 0.8 copy-done.7
  90.1 8.8 %shard_map.154 = (bf16[512,512]{1,0:T(8,128)(2,1)}, bf16[512,512]{1,0:T(8,128)(2,1)}, bf16[512,512]{1,0:T(8,128)(2,1)}, f32[512,512]{1,0:T(8,128)}, bf16[512,512...) custom-call(s32[2]{0:T(128)} %pad_add_fusion.place_ref, ...), custom_call_target="tpu_custom_call" | custom-call | tf_op jit(solution)/shard_map/pallas_call | solution.py:466
  99.0 0.5 collective-permute-start.7
  99.5 2.4 %collective-permute-start.8 = (f32[264,128]{1,0:T(8,128)}, f32[264,128]{1,0:T(8,128)S(1)}, u32[]{:S(2)}, u32[]{:S(2)}) collective-permute-start(f32[264,128]{1,0:T(8,128)} %get-tuple-element.44.s0_ref), channel_id=1, source_target_pairs={{0,2},{1,3},{2,0},{3,1},{4,6},{5,7},{6,4},{7,5},{8,10},{9,11},{10,... | collective-permute-start | bytes 405512 | tf_op jit(solution)/shard_map/ppermute | solution.py:406
  101.9 1.2 collective-permute-start.9
  103.1 3.1 %collective-permute-done.7.s1_ref = f32[264,128]{1,0:T(8,128)S(1)} collective-permute-done((f32[264,128]{1,0:T(8,128)}, f32[264,128]{1,0:T(8,128)S(1)}, u32[]{:S(2)}, u32[]{:S(2)}) %collective-permute-start.7) | collective-permute-done | bytes 135200 | tf_op jit(solution)/shard_map/ppermute | solution.py:406
  106.2 2.3 %collective-permute-done.8.s2_ref = f32[264,128]{1,0:T(8,128)S(1)} collective-permute-done((f32[264,128]{1,0:T(8,128)}, f32[264,128]{1,0:T(8,128)S(1)}, u32[]{:S(2)}, u32[]{:S(2)}) %collective-permute-start.8) | collective-permute-done | bytes 135200 | tf_op jit(solution)/shard_map/ppermute | solution.py:406
  108.5 0.2 collective-permute-done.9.s3_ref
  108.6 0.5 copy-done.12
  109.1 0.2 copy-done.13
  109.3 0.5 copy-done.1
  109.8 8.6 %shard_map.155 = (bf16[16,4,64,128]{3,2,1,0:T(8,128)(2,1)}, bf16[16,4,64,128]{3,2,1,0:T(8,128)(2,1)}, bf16[512,512]{1,0:T(8,128)(2,1)}, f32[512,512]{1,0:T(8,128...) custom-call(s32[2]{0:T(128)} %pad_add_fusion.place_ref, f32[264,128]{1,0:T(8,128)} %get-tuple-element.44.s0_ref, ...), custom_call_target="tpu_custom_call" | custom-call | tf_op jit(solution)/shard_map/pallas_call | solution.py:473
  118.4 0.0 collective-permute-start.14
  118.5 0.8 collective-permute-start.10
  119.2 3.4 %collective-permute-start.11 = (bf16[288,128]{1,0:T(8,128)(2,1)}, bf16[288,128]{1,0:T(8,128)(2,1)S(1)}, u32[]{:S(2)}, u32[]{:S(2)}) collective-permute-start(bf16[288,128]{1,0:T(8,128)(2,1)} %get-tuple-element.49.s0_ref), channel_id=1, source_target_pairs={{0,2},{1,3},{2,0},{3,1},{4,6},{5,7},{6,4},{7,5},{8,10},{9,11},{10,... | collective-permute-start | bytes 221192 | tf_op jit(solution)/shard_map/ppermute | solution.py:406
  122.7 1.9 collective-permute-done.10.s1_ref
  124.6 2.5 %collective-permute-done.11.s2_ref = bf16[288,128]{1,0:T(8,128)(2,1)S(1)} collective-permute-done((bf16[288,128]{1,0:T(8,128)(2,1)}, bf16[288,128]{1,0:T(8,128)(2,1)S(1)}, u32[]{:S(2)}, u32[]{:S(2)}) %collective-permute-start.11) | collective-permute-done | bytes 73760 | tf_op jit(solution)/shard_map/ppermute | solution.py:406
  127.0 0.2 collective-permute-done.12.s3_ref
  127.2 0.4 copy-done.17
  127.7 0.2 copy-done.18
  127.9 9.5 %shard_map.156 = (bf16[16,4,96,128]{3,2,1,0:T(8,128)(2,1)}, bf16[16,4,96,128]{3,2,1,0:T(8,128)(2,1)}, f32[8,128]{1,0:T(8,128)}) custom-call(s32[2]{0:T(128)} %pad_add_fusion.place_ref, bf16[288,128]{1,0:T(8,128)(2,1)} %get-tuple-element.49.s0_ref, bf16[288,128]{1,0:T(8,128)(2,1)} %copy-done.16, bf16[288,128]{1,0:T(8,128)(2,1)} %copy-done.17, ...), custom_call_target="tpu_custom_call" | custom-call | tf_op jit(solution)/shard_map/pallas_call | solution.py:490
  137.4 0.1 collective-permute-start.13
  137.5 1.4 add_convert_fusion.1
  139.0 9.5 %all-to-all-start.3 = ((bf16[64,64,128]{2,1,0:T(8,128)(2,1)}), bf16[64,64,128]{2,1,0:T(8,128)(2,1)S(1)}, u32[]{:S(2)}, u32[]{:S(2)}) async-start(bf16[64,64,128]{2,1,0:T(8,128)(2,1)} %bitcast.13), calls=%async_computation.3 | async-start | bytes 2097152 | tf_op jit(solution)/shard_map/all_to_all | solution.py:421
  148.5 3.0 %add_convert_fusion = bf16[16,4,96,128]{3,2,1,0:T(8,128)(2,1)} fusion(bf16[16,4,96,128]{3,2,1,0:T(8,128)(2,1)} %collective-permute-done.13, bf16[16,4,96,128]{3,2,1,0:T(8,128)(2,1)S(1)} %copy-done.4), kind=kLoop, calls=%fused_computation.1 | loop fusion | flops 3145728 | bytes 4718592 | tf_op jit(solution)/shard_map/convert_element_type | solution.py:416
  151.5 13.9 %all-to-all-done.3 = bf16[64,64,128]{2,1,0:T(8,128)(2,1)S(1)} async-done(((bf16[64,64,128]{2,1,0:T(8,128)(2,1)}), bf16[64,64,128]{2,1,0:T(8,128)(2,1)S(1)}, u32[]{:S(2)}, u32[]{:S(2)}) %all-to-all-start.3) | async-done | bytes 1048608 | tf_op jit(solution)/shard_map/all_to_all | solution.py:421
  165.5 7.4 %all-to-all-start.2 = ((bf16[64,96,128]{2,1,0:T(8,128)(2,1)}), bf16[64,96,128]{2,1,0:T(8,128)(2,1)S(1)}, u32[]{:S(2)}, u32[]{:S(2)}) async-start(bf16[64,96,128]{2,1,0:T(8,128)(2,1)} %bitcast.12), calls=%async_computation.2 | async-start | bytes 3145728 | tf_op jit(solution)/shard_map/all_to_all | solution.py:421
  172.9 0.2 convert_reduce_fusion.1
  173.1 20.9 %all-to-all-done.2 = bf16[64,96,128]{2,1,0:T(8,128)(2,1)S(1)} async-done(((bf16[64,96,128]{2,1,0:T(8,128)(2,1)}), bf16[64,96,128]{2,1,0:T(8,128)(2,1)S(1)}, u32[]{:S(2)}, u32[]{:S(2)}) %all-to-all-start.2) | async-done | bytes 1572896 | tf_op jit(solution)/shard_map/all_to_all | solution.py:421
  193.9 0.2 convert_reduce_fusion
  194.2 0.2 concatenate.14
  194.4 0.9 broadcast_in_dim.10
  195.3 6.5 %all-to-all-start.4 = ((bf16[32,80,128]{2,1,0:T(8,128)(2,1)}), bf16[32,80,128]{2,1,0:T(8,128)(2,1)S(1)}, u32[]{:S(2)}, u32[]{:S(2)}) async-start(bf16[32,80,128]{2,1,0:T(8,128)(2,1)} %broadcast_in_dim.10), calls=%async_computation.4 | async-start | bytes 1310720 | tf_op jit(solution)/shard_map/all_to_all | solution.py:411
  201.9 0.9 collective-permute-start.15
  202.8 1.6 collective-permute-start.16
  204.4 1.3 collective-permute-start.17
  205.7 2.1 collective-permute-done.15.r1_ref
  207.8 0.6 collective-permute-done.16.r2_ref
  208.4 0.3 collective-permute-done.17.r3_ref
  208.7 3.9 %all-to-all-done.4.heads_ref = bf16[32,80,128]{2,1,0:T(8,128)(2,1)S(1)} async-done(((bf16[32,80,128]{2,1,0:T(8,128)(2,1)}), bf16[32,80,128]{2,1,0:T(8,128)(2,1)S(1)}, u32[]{:S(2)}, u32[]{:S(2)}) %all-to-all-start.4) | async-done | bytes 655392 | tf_op jit(solution)/shard_map/all_to_all | solution.py:411
  212.6 0.8 copy-done.2
  213.5 2.3 %shard_map.157 = (f32[48,512]{1,0:T(8,128)}, f32[512,128]{1,0:T(8,128)}, f32[512,128]{1,0:T(8,128)}, f32[512,128]{1,0:T(8,128)}, f32[128,512]{1,0:T(8,128)}, /*index=5*/f32[16,1536]{1,0:T(8,128)}, f32[1,1]{1,0:T(1,128)}) custom-call(s32[2]{0:T(128)} %pad_add_fusion.place_ref, f32[96,128]{1,0:T(8,128)} %copy-done.10, f32[96,128]{1,0:T(8,128)} %copy-done.19, ...), custom_call_target="tpu_custom_call" | custom-call | tf_op jit(solution)/shard_map/pallas_call | solution.py:510
  (59 shorter events, 0.2 us)
Async XLA Ops:
  7.8 44.4 %all-to-all-start = ((bf16[32,16,1664]{2,1,0:T(8,128)(2,1)}), bf16[32,16,1664]{2,1,0:T(8,128)(2,1)S(1)}, u32[]{:S(2)}, u32[]{:S(2)}) async-start(bf16[32,16,1664]{2,1,0:T(8,128)(2,1)} %bitcast.19), calls=%async_computation | async-start | bytes 3407872 | tf_op jit(solution)/shard_map/all_to_all | solution.py:411
  16.5 24.4 %collective-permute-start = (f32[3,1,128,256]{3,2,1,0:T(8,128)S(1)}, f32[3,1,128,256]{3,2,1,0:T(8,128)S(1)}, u32[]{:S(2)}, u32[]{:S(2)}) collective-permute-start(f32[3,1,128,256]{3,2,1,0:T(8,128)S(1)} %get-tuple-element.77), channel_id=1, source_target_pairs={{0,4},{4,8},{8,12},{12,16},{16,20},{20,24},{24,28},{28,32},{32,36}... | collective-permute-start | bytes 1179656 | tf_op jit(solution)/shard_map/ppermute | solution.py:436
  16.7 24.2 %collective-permute-start.1 = (f32[3,1,128,256]{3,2,1,0:T(8,128)S(1)}, f32[3,1,128,256]{3,2,1,0:T(8,128)S(1)}, u32[]{:S(2)}, u32[]{:S(2)}) collective-permute-start(f32[3,1,128,256]{3,2,1,0:T(8,128)S(1)} %get-tuple-element.76), channel_id=1, source_target_pairs={{4,0},{8,4},{12,8},{16,12},{20,16},{24,20},{28,24},{32,28},{36,32}... | collective-permute-start | bytes 1179656 | tf_op jit(solution)/shard_map/ppermute | solution.py:437
  19.4 5.9 %collective-permute-start.2 = (f32[3,8,1,256]{3,2,1,0:T(1,128)S(1)}, f32[3,8,1,256]{3,2,1,0:T(1,128)S(1)}, u32[]{:S(2)}, u32[]{:S(2)}) collective-permute-start(f32[3,8,1,256]{3,2,1,0:T(1,128)S(1)} %get-tuple-element.75), channel_id=1, source_target_pairs={{0,1},{1,2},{2,3},{3,0},{4,5},{5,6},{6,7},{7,4},{8,9},{9,10},{10,1... | collective-permute-start | bytes 73736 | tf_op jit(solution)/shard_map/ppermute | solution.py:439
  21.4 3.9 %collective-permute-start.3 = (f32[3,8,1,256]{3,2,1,0:T(1,128)S(1)}, f32[3,8,1,256]{3,2,1,0:T(1,128)S(1)}, u32[]{:S(2)}, u32[]{:S(2)}) collective-permute-start(f32[3,8,1,256]{3,2,1,0:T(1,128)S(1)} %get-tuple-element.74), channel_id=1, source_target_pairs={{1,0},{2,1},{3,2},{0,3},{5,4},{6,5},{7,6},{4,7},{9,8},{10,9},{11,1... | collective-permute-start | bytes 73736 | tf_op jit(solution)/shard_map/ppermute | solution.py:440
  25.3 15.6 %copy-start.22 = (f32[3,8,1,256]{3,2,1,0:T(1,128)}, f32[3,8,1,256]{3,2,1,0:T(1,128)S(1)}, u32[]{:S(2)}) copy-start(f32[3,8,1,256]{3,2,1,0:T(1,128)S(1)} %collective-permute-done.2.y_prev_ref) | copy-start | bytes 73732
  25.3 15.6 %copy-start.23 = (f32[3,8,1,256]{3,2,1,0:T(1,128)}, f32[3,8,1,256]{3,2,1,0:T(1,128)S(1)}, u32[]{:S(2)}) copy-start(f32[3,8,1,256]{3,2,1,0:T(1,128)S(1)} %collective-permute-done.3.y_next_ref) | copy-start | bytes 73732
  40.9 0.7 copy-start.8
  40.9 0.9 copy-start.9
  52.1 7.3 %copy-start.14 = (bf16[128,512]{1,0:T(8,128)(2,1)S(1)}, bf16[128,512]{1,0:T(8,128)(2,1)}, u32[]{:S(2)}) copy-start(bf16[128,512]{1,0:T(8,128)(2,1)} %param.16) | copy-start | bytes 393220
  52.1 7.3 %copy-start = (bf16[32,16,1664]{2,1,0:T(8,128)(2,1)}, bf16[32,16,1664]{2,1,0:T(8,128)(2,1)S(1)}, u32[]{:S(2)}) copy-start(bf16[32,16,1664]{2,1,0:T(8,128)(2,1)S(1)} %all-to-all-done) | copy-start | bytes 5111812
  52.2 7.4 %copy-start.15 = (bf16[512,128]{1,0:T(8,128)(2,1)S(1)}, bf16[512,128]{1,0:T(8,128)(2,1)}, u32[]{:S(2)}) copy-start(bf16[512,128]{1,0:T(8,128)(2,1)} %param.15) | copy-start | bytes 393220
  52.2 56.5 %all-to-all-start.1 = ((bf16[32,16,1536]{2,1,0:T(8,128)(2,1)}), bf16[32,16,1536]{2,1,0:T(8,128)(2,1)S(1)}, u32[]{:S(2)}, u32[]{:S(2)}) async-start(bf16[32,16,1536]{2,1,0:T(8,128)(2,1)} %bitcast.20), calls=%async_computation.1 | async-start | bytes 3145728 | tf_op jit(solution)/shard_map/all_to_all | solution.py:411
  60.6 28.7 %copy-start.3 = (bf16[4,512,128]{2,1,0:T(8,128)(2,1)}, bf16[4,512,128]{2,1,0:T(8,128)(2,1)S(1)}, u32[]{:S(2)}) copy-start(bf16[4,512,128]{2,1,0:T(8,128)(2,1)S(1)} %pad_maximum_fusion.w0_ref) | copy-start | bytes 1572868
  60.6 16.3 %collective-permute-start.4 = (bf16[4,512,128]{2,1,0:T(8,128)(2,1)S(1)}, bf16[4,512,128]{2,1,0:T(8,128)(2,1)S(1)}, u32[]{:S(2)}, u32[]{:S(2)}) collective-permute-start(bf16[4,512,128]{2,1,0:T(8,128)(2,1)S(1)} %pad_maximum_fusion.w0_ref), channel_id=1, source_target_pairs={{0,1},{1,2},{2,3},{3,0},{4,5},{5,6},{6,7},{7,4},{8,9},{9,10},{10,1... | collective-permute-start | bytes 1572872 | tf_op jit(solution)/shard_map/ppermute | solution.py:406
  62.6 26.7 %collective-permute-start.5 = (bf16[4,512,128]{2,1,0:T(8,128)(2,1)S(1)}, bf16[4,512,128]{2,1,0:T(8,128)(2,1)S(1)}, u32[]{:S(2)}, u32[]{:S(2)}) collective-permute-start(bf16[4,512,128]{2,1,0:T(8,128)(2,1)S(1)} %pad_maximum_fusion.w0_ref), channel_id=1, source_target_pairs={{0,2},{1,3},{2,0},{3,1},{4,6},{5,7},{6,4},{7,5},{8,10},{9,11},{10,... | collective-permute-start | bytes 1572872 | tf_op jit(solution)/shard_map/ppermute | solution.py:406
  66.1 23.2 %collective-permute-start.6 = (bf16[4,512,128]{2,1,0:T(8,128)(2,1)S(1)}, bf16[4,512,128]{2,1,0:T(8,128)(2,1)}, u32[]{:S(2)}, u32[]{:S(2)}) collective-permute-start(bf16[4,512,128]{2,1,0:T(8,128)(2,1)S(1)} %pad_maximum_fusion.w0_ref), channel_id=1, source_target_pairs={{0,3},{1,0},{2,1},{3,2},{4,7},{5,4},{6,5},{7,6},{8,11},{9,8},{10,9... | collective-permute-start | bytes 1572872 | tf_op jit(solution)/shard_map/ppermute | solution.py:406
  76.9 12.4 %copy-start.6 = (bf16[4,512,128]{2,1,0:T(8,128)(2,1)}, bf16[4,512,128]{2,1,0:T(8,128)(2,1)S(1)}, u32[]{:S(2)}) copy-start(bf16[4,512,128]{2,1,0:T(8,128)(2,1)S(1)} %collective-permute-done.4.w1_ref) | copy-start | bytes 1572868
  89.3 0.8 copy-start.7
  99.0 7.2 %collective-permute-start.7 = (f32[264,128]{1,0:T(8,128)}, f32[264,128]{1,0:T(8,128)S(1)}, u32[]{:S(2)}, u32[]{:S(2)}) collective-permute-start(f32[264,128]{1,0:T(8,128)} %get-tuple-element.44.s0_ref), channel_id=1, source_target_pairs={{0,1},{1,2},{2,3},{3,0},{4,5},{5,6},{6,7},{7,4},{8,9},{9,10},{10,1... | collective-permute-start | bytes 405512 | tf_op jit(solution)/shard_map/ppermute | solution.py:406
  99.5 9.0 %collective-permute-start.8 = (f32[264,128]{1,0:T(8,128)}, f32[264,128]{1,0:T(8,128)S(1)}, u32[]{:S(2)}, u32[]{:S(2)}) collective-permute-start(f32[264,128]{1,0:T(8,128)} %get-tuple-element.44.s0_ref), channel_id=1, source_target_pairs={{0,2},{1,3},{2,0},{3,1},{4,6},{5,7},{6,4},{7,5},{8,10},{9,11},{10,... | collective-permute-start | bytes 405512 | tf_op jit(solution)/shard_map/ppermute | solution.py:406
  101.9 6.7 %collective-permute-start.9 = (f32[264,128]{1,0:T(8,128)}, f32[264,128]{1,0:T(8,128)S(1)}, u32[]{:S(2)}, u32[]{:S(2)}) collective-permute-start(f32[264,128]{1,0:T(8,128)} %get-tuple-element.44.s0_ref), channel_id=1, source_target_pairs={{0,3},{1,0},{2,1},{3,2},{4,7},{5,4},{6,5},{7,6},{8,11},{9,8},{10,9... | collective-permute-start | bytes 405512 | tf_op jit(solution)/shard_map/ppermute | solution.py:406
  106.2 2.4 %copy-start.11 = (f32[264,128]{1,0:T(8,128)}, f32[264,128]{1,0:T(8,128)S(1)}, u32[]{:S(2)}) copy-start(f32[264,128]{1,0:T(8,128)S(1)} %collective-permute-done.7.s1_ref) | copy-start | bytes 405508
  108.5 0.7 copy-start.12
  108.6 0.7 copy-start.13
  108.6 1.2 copy-start.1
  118.4 19.1 %collective-permute-start.14 = (bf16[16,4,64,128]{3,2,1,0:T(8,128)(2,1)}, bf16[16,4,64,128]{3,2,1,0:T(8,128)(2,1)S(1)}, u32[]{:S(2)}, u32[]{:S(2)}) collective-permute-start(bf16[16,4,64,128]{3,2,1,0:T(8,128)(2,1)} %get-tuple-element.63), channel_id=1, source_target_pairs={{0,4},{4,0},{8,12},{12,8},{16,20},{20,16},{24,28},{28,24},{32,36},... | collective-permute-start | bytes 3145736 | tf_op jit(solution)/shard_map/ppermute | solution.py:415
  118.5 6.1 %collective-permute-start.10 = (bf16[288,128]{1,0:T(8,128)(2,1)}, bf16[288,128]{1,0:T(8,128)(2,1)S(1)}, u32[]{:S(2)}, u32[]{:S(2)}) collective-permute-start(bf16[288,128]{1,0:T(8,128)(2,1)} %get-tuple-element.49.s0_ref), channel_id=1, source_target_pairs={{0,1},{1,2},{2,3},{3,0},{4,5},{5,6},{6,7},{7,4},{8,9},{9,10},{10,1... | collective-permute-start | bytes 221192 | tf_op jit(solution)/shard_map/ppermute | solution.py:406
  119.2 7.8 %collective-permute-start.11 = (bf16[288,128]{1,0:T(8,128)(2,1)}, bf16[288,128]{1,0:T(8,128)(2,1)S(1)}, u32[]{:S(2)}, u32[]{:S(2)}) collective-permute-start(bf16[288,128]{1,0:T(8,128)(2,1)} %get-tuple-element.49.s0_ref), channel_id=1, source_target_pairs={{0,2},{1,3},{2,0},{3,1},{4,6},{5,7},{6,4},{7,5},{8,10},{9,11},{10,... | collective-permute-start | bytes 221192 | tf_op jit(solution)/shard_map/ppermute | solution.py:406
  122.7 4.6 %collective-permute-start.12 = (bf16[288,128]{1,0:T(8,128)(2,1)}, bf16[288,128]{1,0:T(8,128)(2,1)S(1)}, u32[]{:S(2)}, u32[]{:S(2)}) collective-permute-start(bf16[288,128]{1,0:T(8,128)(2,1)} %get-tuple-element.49.s0_ref), channel_id=1, source_target_pairs={{0,3},{1,0},{2,1},{3,2},{4,7},{5,4},{6,5},{7,6},{8,11},{9,8},{10,9... | collective-permute-start | bytes 221192 | tf_op jit(solution)/shard_map/ppermute | solution.py:406
  124.6 2.7 %copy-start.16 = (bf16[288,128]{1,0:T(8,128)(2,1)}, bf16[288,128]{1,0:T(8,128)(2,1)S(1)}, u32[]{:S(2)}) copy-start(bf16[288,128]{1,0:T(8,128)(2,1)S(1)} %collective-permute-done.10.s1_ref) | copy-start | bytes 221188
  127.0 0.6 copy-start.17
  127.2 0.6 copy-start.18
  127.9 9.7 %copy-start.5 = (bf16[16,4,64,128]{3,2,1,0:T(8,128)(2,1)S(1)}, bf16[16,4,64,128]{3,2,1,0:T(8,128)(2,1)}, u32[]{:S(2)}) copy-start(bf16[16,4,64,128]{3,2,1,0:T(8,128)(2,1)} %get-tuple-element.62) | copy-start | bytes 3145732
  137.4 11.1 %collective-permute-start.13 = (bf16[16,4,96,128]{3,2,1,0:T(8,128)(2,1)}, bf16[16,4,96,128]{3,2,1,0:T(8,128)(2,1)}, u32[]{:S(2)}, u32[]{:S(2)}) collective-permute-start(bf16[16,4,96,128]{3,2,1,0:T(8,128)(2,1)} %get-tuple-element.61), channel_id=1, source_target_pairs={{0,4},{4,0},{8,12},{12,8},{16,20},{20,16},{24,28},{28,24},{32,36},... | collective-permute-start | bytes 4718600 | tf_op jit(solution)/shard_map/ppermute | solution.py:415
  139.0 9.6 %copy-start.4 = (bf16[16,4,96,128]{3,2,1,0:T(8,128)(2,1)S(1)}, bf16[16,4,96,128]{3,2,1,0:T(8,128)(2,1)}, u32[]{:S(2)}) copy-start(bf16[16,4,96,128]{3,2,1,0:T(8,128)(2,1)} %get-tuple-element.60) | copy-start | bytes 4718596
  139.0 26.5 %all-to-all-start.3 = ((bf16[64,64,128]{2,1,0:T(8,128)(2,1)}), bf16[64,64,128]{2,1,0:T(8,128)(2,1)S(1)}, u32[]{:S(2)}, u32[]{:S(2)}) async-start(bf16[64,64,128]{2,1,0:T(8,128)(2,1)} %bitcast.13), calls=%async_computation.3 | async-start | bytes 2097152 | tf_op jit(solution)/shard_map/all_to_all | solution.py:421
  151.5 21.3 %copy-start.24 = (f32[8,128]{1,0:T(8,128)S(1)}, f32[8,128]{1,0:T(8,128)}, u32[]{:S(2)}) copy-start(f32[8,128]{1,0:T(8,128)} %get-tuple-element.64) | copy-start | bytes 12292
  165.5 28.5 %all-to-all-start.2 = ((bf16[64,96,128]{2,1,0:T(8,128)(2,1)}), bf16[64,96,128]{2,1,0:T(8,128)(2,1)S(1)}, u32[]{:S(2)}, u32[]{:S(2)}) async-start(bf16[64,96,128]{2,1,0:T(8,128)(2,1)} %bitcast.12), calls=%async_computation.2 | async-start | bytes 3145728 | tf_op jit(solution)/shard_map/all_to_all | solution.py:421
  195.3 17.3 %all-to-all-start.4 = ((bf16[32,80,128]{2,1,0:T(8,128)(2,1)}), bf16[32,80,128]{2,1,0:T(8,128)(2,1)S(1)}, u32[]{:S(2)}, u32[]{:S(2)}) async-start(bf16[32,80,128]{2,1,0:T(8,128)(2,1)} %broadcast_in_dim.10), calls=%async_computation.4 | async-start | bytes 1310720 | tf_op jit(solution)/shard_map/all_to_all | solution.py:411
  201.9 10.7 %copy-start.10 = (f32[96,128]{1,0:T(8,128)}, f32[96,128]{1,0:T(8,128)S(1)}, u32[]{:S(2)}) copy-start(f32[96,128]{1,0:T(8,128)S(1)} %pad_maximum_fusion.1.r0_ref) | copy-start | bytes 147460
  201.9 5.9 %collective-permute-start.15 = (f32[96,128]{1,0:T(8,128)S(1)}, f32[96,128]{1,0:T(8,128)S(1)}, u32[]{:S(2)}, u32[]{:S(2)}) collective-permute-start(f32[96,128]{1,0:T(8,128)S(1)} %pad_maximum_fusion.1.r0_ref), channel_id=1, source_target_pairs={{0,1},{1,2},{2,3},{3,0},{4,5},{5,6},{6,7},{7,4},{8,9},{9,10},{10,1... | collective-permute-start | bytes 147464 | tf_op jit(solution)/shard_map/ppermute | solution.py:406
  202.8 5.6 %collective-permute-start.16 = (f32[96,128]{1,0:T(8,128)S(1)}, f32[96,128]{1,0:T(8,128)S(1)}, u32[]{:S(2)}, u32[]{:S(2)}) collective-permute-start(f32[96,128]{1,0:T(8,128)S(1)} %pad_maximum_fusion.1.r0_ref), channel_id=1, source_target_pairs={{0,2},{1,3},{2,0},{3,1},{4,6},{5,7},{6,4},{7,5},{8,10},{9,11},{10,... | collective-permute-start | bytes 147464 | tf_op jit(solution)/shard_map/ppermute | solution.py:406
  204.4 4.2 %collective-permute-start.17 = (f32[96,128]{1,0:T(8,128)S(1)}, f32[96,128]{1,0:T(8,128)S(1)}, u32[]{:S(2)}, u32[]{:S(2)}) collective-permute-start(f32[96,128]{1,0:T(8,128)S(1)} %pad_maximum_fusion.1.r0_ref), channel_id=1, source_target_pairs={{0,3},{1,0},{2,1},{3,2},{4,7},{5,4},{6,5},{7,6},{8,11},{9,8},{10,9... | collective-permute-start | bytes 147464 | tf_op jit(solution)/shard_map/ppermute | solution.py:406
  207.8 4.8 %copy-start.19 = (f32[96,128]{1,0:T(8,128)}, f32[96,128]{1,0:T(8,128)S(1)}, u32[]{:S(2)}) copy-start(f32[96,128]{1,0:T(8,128)S(1)} %collective-permute-done.15.r1_ref) | copy-start | bytes 147460
  208.4 4.2 %copy-start.20 = (f32[96,128]{1,0:T(8,128)}, f32[96,128]{1,0:T(8,128)S(1)}, u32[]{:S(2)}) copy-start(f32[96,128]{1,0:T(8,128)S(1)} %collective-permute-done.16.r2_ref) | copy-start | bytes 147460
  208.7 3.9 %copy-start.21 = (f32[96,128]{1,0:T(8,128)}, f32[96,128]{1,0:T(8,128)S(1)}, u32[]{:S(2)}) copy-start(f32[96,128]{1,0:T(8,128)S(1)} %collective-permute-done.17.r3_ref) | copy-start | bytes 147460
  212.6 0.9 copy-start.2
